TPU v7x, 256 devices: a whole 4x4x8 slice. The times are simulated.
256 devices in a mesh: ctx: 32 (over y_hi, z, core), exp: 8 (over y_lo, x).
Axes of the slice: x: 4, y: 4 (y_hi: 2, y_lo: 2; y = y_hi * 2 + y_lo), z: 8, core: 2. Of those that a mesh axis runs over, the one named last changes fastest.
Arguments:
- queries: bfloat16 [4096, 4096], P('ctx', 'exp'), may hold values from -96 to 96
- keys: bfloat16 [4096, 512], P('ctx'), may hold values from -4 to 4
- values: bfloat16 [4096, 512], P('ctx'), may hold values from -5 to 5
- span_order: int32 [64], replicated, may hold values from 0 to 63, each once
- stream_in: bfloat16 [4096, 2048], P(('ctx', 'exp')), may hold values from -12 to 12
- wo: bfloat16 [32, 128, 2048], P('exp', None, 'ctx'), may hold values from -0.09375 to 0.09375
- norm_gain: bfloat16 [2048], replicated, may hold values from 0.5 to 1.5
- expert_ids: int32 [4096, 8], P(('ctx', 'exp')), may hold values from 0 to 127, all different within a row; in each aligned block of 16 rows (0 to 15, 16 to 31, ...) at most 2 rows name the same one
- expert_gates: bfloat16 [4096, 8], P(('ctx', 'exp')), may hold values from 0.019897461 to 0.5
- w_gate: bfloat16 [128, 2048, 768], P('exp', 'ctx'), may hold values from -0.125 to 0.125
- w_up: bfloat16 [128, 2048, 768], P('exp', 'ctx'), may hold values from -0.125 to 0.125
- w_down: bfloat16 [128, 2048, 768], P('exp', 'ctx'), may hold values from -0.21875 to 0.21875
Outputs:
- layer_out: float32 [4096, 2048], P(('ctx', 'exp'))
Inputs may be any that keep to these rules, and one draw needn't show every extreme that they name: `span_order`: each value 0 to 63 appears once. `expert_ids`: each row names 8 different experts. Among the 16 rows of one device (aligned blocks), no expert is named more than 2 times, a bound that some block reaches.
All inputs are finite; a program needn't handle non-finite values.
Results may differ from a plain program's by a relative error of at most 0.005.
Values may be sent and summed in bfloat16 or wider, within the bound.
No kernel may reach another device: no remote copies, remote signals or barrier semaphores. Data moves between devices by JAX's collectives and lax.ppermute only.
A program may use at most 64 MiB of HBM per device.

v0:
```python
import math

import jax
import jax.numpy as jnp
from jax import lax
from jax.sharding import Mesh
from jax.sharding import PartitionSpec as P

D = 2048
QH = 32
KVH = 4
HD = 128
TOPK = 8
EXP_OWN = 16
CTX = ("ctx_0", "ctx_1", "ctx_2")
CTX_EXP = ("ctx_0", "ctx_1", "ctx_2", "exp")


NEG_BIG = -1e30


def sent_together(arrays, axis, dim, along):
    ends, at = ([], 0)
    for a in arrays[:-1]:
        at += a.shape[along]
        ends.append(at)
    both = jnp.concatenate(arrays, axis=along)
    return tuple(jnp.split(lax.all_gather(both, axis, axis=dim, tiled=True), ends, axis=along))


def in_blocks(array, dim, devices):
    shape = array.shape
    tiles = array.reshape(*shape[:dim], devices, shape[dim] // devices, *shape[dim + 1 :])
    return jnp.moveaxis(tiles, dim, 0)


def summed_on_arrival(array, axis, dim):
    tiles = in_blocks(array, dim, lax.axis_size(axis))
    arrived = lax.all_to_all(tiles, axis, split_axis=0, concat_axis=0, tiled=True)
    return arrived.astype(jnp.float32).sum(axis=0)


def side_by_side(arrays, axis, split_dim, concat_dim, along):
    both = jnp.concatenate(arrays, axis=along)
    filled, at, outs = (
        lax.all_to_all(both, axis, split_axis=split_dim, concat_axis=concat_dim, tiled=True),
        0,
        [],
    )
    for a in arrays:
        outs.append(lax.slice_in_dim(filled, at, at + a.shape[along], axis=along))
        at += a.shape[along]
    return tuple(outs)


def laid_out(tiles, dim):
    shape = list(tiles.shape[1:])
    shape[dim] *= tiles.shape[0]
    return jnp.moveaxis(tiles, 0, dim).reshape(shape)


def exchange_in_order(tiles, axes, sequence):
    inside = tiles.shape[1:]
    filled = tiles.reshape(*(lax.axis_size(a) for a in axes), *inside)
    for k in sequence:
        filled = lax.all_to_all(filled, axes[k], k, k, tiled=True)
    return filled.reshape(-1, *inside)


def exchange_by_chip(array, groups, sequence, split_dim, concat_dim):
    devices = lax.axis_size(groups[0]) * lax.axis_size(groups[1])
    tiles = in_blocks(array, split_dim, devices)
    return laid_out(exchange_in_order(tiles, groups, sequence), concat_dim)


def span_place(row_ids, span_order, half):
    table = jnp.arange(span_order.shape[0], dtype=jnp.int32)
    which = row_ids // half
    picked = jnp.sum(jnp.where(which[:, None] == table[None, :], span_order[None, :], 0), axis=1)
    return picked * half + row_ids % half


def expert_apply(tokens, gate_w, up_w, down_w):
    gate_part = jnp.dot(tokens, gate_w, preferred_element_type=jnp.float32)
    up_part = jnp.dot(tokens, up_w, preferred_element_type=jnp.float32)
    active = (jax.nn.silu(gate_part) * up_part).astype(jnp.bfloat16)
    return lax.dot_general(
        active, down_w, (((1,), (1,)), ((), ())), preferred_element_type=jnp.float32
    )


def shards(
    queries,
    keys,
    values,
    span_order,
    stream_in,
    wo,
    norm_gain,
    expert_ids,
    expert_gates,
    w_gate,
    w_up,
    w_down,
):
    ctx_count = lax.axis_size(CTX)
    exp_count = lax.axis_size("exp")
    ctx_index = lax.axis_index(CTX)
    exp_index = lax.axis_index("exp")
    rows = queries.shape[0]
    half = rows // 2
    head_here = queries.shape[1] // HD
    group = QH // KVH
    width_group = min(head_here, group)
    kv_here = head_here // width_group
    kv_first = exp_index * head_here // group
    key_mine = lax.dynamic_slice_in_dim(keys, kv_first * HD, kv_here * HD, 1)
    value_mine = lax.dynamic_slice_in_dim(values, kv_first * HD, kv_here * HD, 1)
    own_rows = ctx_index * rows + jnp.arange(rows, dtype=jnp.int32)
    query_place = span_place(own_rows, span_order, half)
    query_heads = queries.reshape(rows, kv_here, width_group, HD)
    scale = 1.0 / math.sqrt(HD)

    def attend(state, key_block, value_block, key_place):
        top, total, accum = state
        scores = (
            jnp.einsum("tkgd,nkd->kgtn", query_heads, key_block, preferred_element_type=jnp.float32)
            * scale
        )
        visible = key_place[None, None, None, :] <= query_place[None, None, :, None]
        scores = jnp.where(visible, scores, NEG_BIG)
        top_new = jnp.maximum(top, jnp.max(scores, axis=-1))
        probs = jnp.where(visible, jnp.exp(scores - top_new[..., None]), 0.0)
        factor = jnp.exp(top - top_new)
        total = total * factor + jnp.sum(probs, axis=-1)
        accum = accum * factor[..., None] + jnp.einsum(
            "kgtn,nkd->kgtd",
            probs.astype(jnp.bfloat16),
            value_block,
            preferred_element_type=jnp.float32,
        )
        return (top_new, total, accum)

    initial = (
        jnp.full((kv_here, width_group, rows), NEG_BIG, jnp.float32),
        jnp.zeros((kv_here, width_group, rows), jnp.float32),
        jnp.zeros((kv_here, width_group, rows, HD), jnp.float32),
    )
    carry = initial
    key_piece, value_piece = sent_together((key_mine, value_mine), CTX, 0, 1)
    count = key_piece.shape[0]
    blocks = count // half
    key_blocks = key_piece.reshape(blocks, half, kv_here, HD)
    value_blocks = value_piece.reshape(blocks, half, kv_here, HD)
    firsts = half * jnp.arange(blocks, dtype=jnp.int32)

    def visit(state, item):
        key_block, value_block, first = item
        key_place = span_place(first + jnp.arange(half, dtype=jnp.int32), span_order, half)
        state = attend(state, key_block, value_block, key_place)
        return (state, None)

    carry, _ = lax.scan(visit, carry, (key_blocks, value_blocks, firsts))
    top, total, accum = carry
    attended = (
        (accum / total[..., None])
        .transpose(2, 0, 1, 3)
        .reshape(rows, head_here * HD)
        .astype(jnp.bfloat16)
    )
    piece = lax.all_gather(wo, CTX, axis=2, tiled=True)
    partial_value = jnp.dot(
        attended, piece.reshape(head_here * HD, piece.shape[2]), preferred_element_type=jnp.float32
    )
    mixed = summed_on_arrival(partial_value.astype(jnp.bfloat16), "exp", 0)
    resid = stream_in.astype(jnp.float32) + mixed
    normed = (
        resid
        * lax.rsqrt(jnp.mean(resid * resid, axis=-1, keepdims=True) + 1e-06)
        * norm_gain.astype(jnp.float32)
    ).astype(jnp.bfloat16)
    local_rows = stream_in.shape[0]
    expert_count = EXP_OWN * exp_count
    capacity = max(2, 2 * local_rows * TOPK // expert_count)
    flat_ids = expert_ids.reshape(-1)
    hits = (flat_ids[:, None] == jnp.arange(expert_count, dtype=jnp.int32)[None, :]).astype(
        jnp.int32
    )
    rank = jnp.sum((jnp.cumsum(hits, axis=0) - hits) * hits, axis=1)
    slots = (flat_ids * capacity + rank).reshape(local_rows, TOPK)
    slot_ids = jnp.arange(expert_count * capacity, dtype=jnp.int32)
    placing = jnp.any(slots[None, :, :] == slot_ids[:, None, None], axis=2).astype(jnp.bfloat16)
    outgoing = jnp.dot(placing, normed, preferred_element_type=jnp.float32).astype(jnp.bfloat16)
    outgoing = outgoing.reshape(exp_count, EXP_OWN, capacity, D)
    arrived = lax.all_to_all(outgoing, "exp", split_axis=0, concat_axis=0, tiled=True)
    by_expert = arrived.transpose(1, 0, 2, 3).reshape(EXP_OWN, exp_count * capacity, D)
    serving = ctx_count // EXP_OWN
    slot_total = exp_count * capacity
    feat_here = w_gate.shape[1]

    def unit_pieces(weight):
        narrow = weight.shape[2] // serving
        return (
            weight.reshape(EXP_OWN, feat_here, serving, narrow)
            .transpose(0, 2, 1, 3)
            .reshape(ctx_count, feat_here, narrow)
        )

    gate_mine, up_mine, down_mine = side_by_side(
        (unit_pieces(w_gate), unit_pieces(w_up), unit_pieces(w_down)), CTX, 0, 1, 2
    )
    copies = jnp.repeat(by_expert, serving, axis=0)
    mine = exchange_by_chip(copies, (("ctx_0", "ctx_1"), "ctx_2"), (1, 0), 0, 0)
    partial_out = expert_apply(
        mine.reshape(ctx_count * slot_total, D), gate_mine[0], up_mine[0], down_mine[0]
    )
    partial_out = partial_out.reshape(ctx_count, slot_total, D)
    returned = lax.all_to_all(
        partial_out.astype(jnp.bfloat16), CTX, split_axis=0, concat_axis=0, tiled=True
    ).astype(partial_out.dtype)
    results = jnp.sum(returned.reshape(EXP_OWN, serving, slot_total, D), axis=1).astype(
        jnp.bfloat16
    )
    going_home = results.reshape(EXP_OWN, exp_count, capacity, D).transpose(1, 0, 2, 3)
    home = lax.all_to_all(going_home, "exp", split_axis=0, concat_axis=0, tiled=True)
    outputs = home.reshape(expert_count * capacity, D)
    combine = jnp.sum(
        jnp.where(
            slots[:, :, None] == slot_ids[None, None, :],
            expert_gates[:, :, None],
            jnp.zeros((), jnp.bfloat16),
        ),
        axis=1,
    )
    moe = jnp.dot(combine, outputs, preferred_element_type=jnp.float32)
    return resid + moe


def solution(mesh):
    finer = Mesh(
        mesh.devices.reshape(2, 8, 2, mesh.shape["exp"]), ("ctx_0", "ctx_1", "ctx_2", "exp")
    )
    return jax.shard_map(
        shards,
        mesh=finer,
        in_specs=(
            P(CTX, "exp"),
            P(CTX, None),
            P(CTX, None),
            P(),
            P(CTX_EXP, None),
            P("exp", None, CTX),
            P(),
            P(CTX_EXP, None),
            P(CTX_EXP, None),
            P("exp", CTX, None),
            P("exp", CTX, None),
            P("exp", CTX, None),
        ),
        out_specs=P(CTX_EXP, None),
        check_vma=False,
    )
```

profile of v0, /device:TPU:32, one launch (start us, length us, event | category | flops | bytes accessed | tf_op | source)
XLA Modules:
  0.0 585.3 jit_solution(993793440684046741)
XLA Ops:
  8.0 1.6 copy.76
  13.1 2.7 fusion.33
  17.0 74.9 %all-gather.3.cloned.1.call-done = bf16[4096,256]{1,0:T(8,128)(2,1)} async-done(((bf16[128,256]{1,0:T(8,128)(2,1)}), bf16[4096,256]{1,0:T(8,128)(2,1)}) %all-gather.3.cloned.1.call-update) | async-done | bytes 2097168 | tf_op jit(solution)/shard_map/all_gather | solution.py:28
  91.9 1.7 fusion.32
  93.5 176.5 %while.17 = (s32[]{:T(128)}, f32[1,4,128]{2,1,0:T(4,128)S(1)}, f32[1,4,128]{2,1,0:T(4,128)S(1)}, f32[1,4,128,128]{3,2,1,0:T(8,128)S(1)}, s32[64]{0:T(128)S(1)}, ...) while((s32[]{:T(128)}, f32[1,4,128]{2,1,0:T(4,128)S(1)}, ...), condition=%wide.region_5.6_spmd.clone, body=%wide.region_1.5_spmd.clone.sunk | while | flops 17294148 | bytes 1149349 | solution.py:163
  270.3 3.0 copy.77
  274.5 4.3 all-to-all-start
  278.9 2.7 fusion.35
  281.7 7.6 %all-to-all-done = bf16[8,16,2048]{2,1,0:T(8,128)(2,1)S(1)} async-done(((bf16[8,16,2048]{2,1,0:T(8,128)(2,1)}), bf16[8,16,2048]{2,1,0:T(8,128)(2,1)S(1)}, u32[]{:S(2)}, u32[]{:S(2)}) %all-to-all-start) | async-done | bytes 524320 | tf_op jit(solution)/shard_map/all_to_all | solution.py:39
  292.1 3.7 all-to-all-start.1
  297.6 2.5 pad_maximum_fusion
  300.1 11.5 %all-to-all-done.1 = bf16[8,16,2,2048]{3,1,2,0:T(8,128)(2,1)S(1)} async-done(((bf16[8,16,2,2048]{3,1,2,0:T(8,128)(2,1)}), bf16[8,16,2,2048]{3,1,2,0:T(8,128)(2,1)S(1)}, u32[]{:S(2)}, u32[]{:S(2)}) %all-to-all-start.1) | async-done | bytes 1048608 | tf_op jit(solution)/shard_map/all_to_all | solution.py:195
  312.4 5.4 all_to_all.42
  317.8 6.9 %all-to-all-start.4 = ((bf16[32,64,1152]{2,1,0:T(8,128)(2,1)}), bf16[32,64,1152]{2,1,0:T(8,128)(2,1)}, u32[]{:S(2)}, u32[]{:S(2)}) async-start(bf16[32,64,1152]{2,1,0:T(8,128)(2,1)} %pad_maximum_fusion), calls=%async_computation.4 | async-start | bytes 9437184 | tf_op jit(solution)/shard_map/all_to_all | solution.py:46
  324.8 1.5 copy.83
  326.2 104.9 %all-to-all-done.4 = bf16[32,64,1152]{2,1,0:T(8,128)(2,1)} async-done(((bf16[32,64,1152]{2,1,0:T(8,128)(2,1)}), bf16[32,64,1152]{2,1,0:T(8,128)(2,1)}, u32[]{:S(2)}, u32[]{:S(2)}) %all-to-all-start.4) | async-done | bytes 4718624 | tf_op jit(solution)/shard_map/all_to_all | solution.py:46
  431.1 58.1 %all_to_all.43 = bf16[16,2,1,16,2048]{4,3,1,2,0:T(8,128)(2,1)S(1)} all-to-all(bf16[16,2,1,16,2048]{4,3,1,2,0:T(8,128)(2,1)} %copy.83), channel_id=1, replica_groups=mesh['ctx_0'=2,'ctx_1'=8,'ctx_2'=2,'exp'=8] {'ctx_0','ctx_1'}, dimensions={0} | all-to-all | bytes 4194304 | tf_op jit(solution)/shard_map/all_to_all | solution.py:66
  489.3 2.7 fusion.21
  491.9 2.7 fusion.23
  494.6 2.7 convolution_convert_fusion
  497.3 58.3 %all_to_all.44 = bf16[32,16,2048]{2,1,0:T(8,128)(2,1)S(1)} all-to-all(bf16[32,16,2048]{2,1,0:T(8,128)(2,1)S(1)} %convolution_convert_fusion), channel_id=1, replica_groups=mesh['ctx_0'=2,'ctx_1'=8,'ctx_2'=2,'exp'=8] {'ctx_0','ctx_1','ctx_2'}, dimensions={0} | all-to-all | bytes 4194304 | tf_op jit(solution)/shard_map/all_to_all | solution.py:218
  556.1 1.6 copy.84
  557.7 3.6 all-to-all-start.6
  561.5 14.5 %all-to-all-done.6 = bf16[8,16,2,2048]{3,1,2,0:T(8,128)(2,1)S(1)} async-done(((bf16[8,16,2,2048]{3,1,2,0:T(8,128)(2,1)}), bf16[8,16,2,2048]{3,1,2,0:T(8,128)(2,1)S(1)}, u32[]{:S(2)}, u32[]{:S(2)}) %all-to-all-start.6) | async-done | bytes 1048608 | tf_op jit(solution)/shard_map/all_to_all | solution.py:225
  (772 shorter events, 188.8 us)
Async XLA Ops:
  6.5 85.3 %all-gather.3.cloned.1.call-start = ((), (), s32[]{:S(2)}) async-start(), calls=%async_computation.7 | async-start | bytes 2162688 | tf_op jit(solution)/shard_map/all_gather | solution.py:28
  8.0 7.8 %copy-start.5 = (bf16[16,64,768]{2,1,0:T(8,128)(2,1)S(1)}, bf16[16,64,768]{2,1,0:T(8,128)(2,1)}, u32[]{:S(2)}) copy-start(bf16[16,64,768]{2,1,0:T(8,128)(2,1)} %param.24) | copy-start | bytes 4718596
  8.0 262.3 %all-gather.5.cloned.1.call-start = ((), (), s32[]{:S(2)}) async-start(), calls=%async_computation.8 | async-start | bytes 2162688 | tf_op jit(solution)/shard_map/all_gather | solution.py:171
  17.0 76.5 %copy-start.10 = (s32[64]{0:T(128)S(1)}, s32[64]{0:T(128)}, u32[]{:S(2)}) copy-start(s32[64]{0:T(128)} %param.17) | copy-start | bytes 772
  273.2 5.6 copy-start.8
  274.5 14.7 %all-to-all-start = ((bf16[8,16,2048]{2,1,0:T(8,128)(2,1)}), bf16[8,16,2048]{2,1,0:T(8,128)(2,1)S(1)}, u32[]{:S(2)}, u32[]{:S(2)}) async-start(bf16[8,16,2048]{2,1,0:T(8,128)(2,1)} %bitcast.7), calls=%async_computation | async-start | bytes 1048576 | tf_op jit(solution)/shard_map/all_to_all | solution.py:39
  278.8 10.5 %copy-start.6 = (bf16[16,2048]{1,0:T(8,128)(2,1)S(1)}, bf16[16,2048]{1,0:T(8,128)(2,1)}, u32[]{:S(2)}) copy-start(bf16[16,2048]{1,0:T(8,128)(2,1)} %param.18) | copy-start | bytes 196612
  292.1 3.7 copy-start.1
  292.1 3.7 copy-start.2
  292.1 19.5 %all-to-all-start.1 = ((bf16[8,16,2,2048]{3,1,2,0:T(8,128)(2,1)}), bf16[8,16,2,2048]{3,1,2,0:T(8,128)(2,1)S(1)}, u32[]{:S(2)}, u32[]{:S(2)}) async-start(bf16[8,16,2,2048]{3,1,2,0:T(8,128)(2,1)} %copy.81), calls=%async_computation.1 | async-start | bytes 2097152 | tf_op jit(solution)/shard_map/all_to_all | solution.py:195
  295.8 1.1 copy-start
  296.0 1.2 copy-start.3
  296.0 1.4 copy-start.4
  317.8 113.3 %all-to-all-start.4 = ((bf16[32,64,1152]{2,1,0:T(8,128)(2,1)}), bf16[32,64,1152]{2,1,0:T(8,128)(2,1)}, u32[]{:S(2)}, u32[]{:S(2)}) async-start(bf16[32,64,1152]{2,1,0:T(8,128)(2,1)} %pad_maximum_fusion), calls=%async_computation.4 | async-start | bytes 9437184 | tf_op jit(solution)/shard_map/all_to_all | solution.py:46
  556.1 5.1 copy-start.9
  557.7 18.3 %all-to-all-start.6 = ((bf16[8,16,2,2048]{3,1,2,0:T(8,128)(2,1)}), bf16[8,16,2,2048]{3,1,2,0:T(8,128)(2,1)S(1)}, u32[]{:S(2)}, u32[]{:S(2)}) async-start(bf16[8,16,2,2048]{3,1,2,0:T(8,128)(2,1)} %bitcast.22), calls=%async_computation.6 | async-start | bytes 2097152 | tf_op jit(solution)/shard_map/all_to_all | solution.py:225
  561.5 16.1 %copy-start.7 = (bf16[16,2048]{1,0:T(8,128)(2,1)S(1)}, bf16[16,2048]{1,0:T(8,128)(2,1)}, u32[]{:S(2)}) copy-start(bf16[16,2048]{1,0:T(8,128)(2,1)} %param.18) | copy-start | bytes 196612
Sparse Core Ops, SparseCore 0:
  10.1 81.7 all-gather.2
  94.6 76.4 all-gather.4
where the time goes:
time: 587 us; the launch traced here: 585 us
  waiting for transfers between devices  213 us (36%)
  blocking collectives  122 us (21%)
  other arithmetic  111 us (19%)
  local copies, waits for them, and re-layouts  62.5 us (11%)
  matrix products  41 us (7%)
  starting transfers between devices  18.5 us (3%)
  between operations  13.8 us (2%)
    all_to_all x1, waiting for transfers between devices, side_by_side(): lax.all_to_all(both, axis, split_axis=split_dim, concat_axis=concat_dim,...  105 us
    all_gather x1, waiting for transfers between devices, sent_together(): lax.all_gather(both, axis, axis=dim, tiled=True)  74.9 us
    all_to_all x2, blocking collectives, exchange_in_order(): filled = lax.all_to_all(filled, axes[k], k, k, tiled=True)  63.5 us
    all_to_all x1, blocking collectives, shards(): lax.all_to_all(partial_out.astype(jnp.bfloat16), CTX, split_axis=0, conca...  58.3 us
    add x65, other arithmetic, span_place(): return picked * half + row_ids % half  42.6 us
    select_n x65, other arithmetic, span_place(): which = row_ids // half  41.8 us
    dynamic_slice x64, local copies, waits for them, and re-layouts, shards(): carry, _ = lax.scan(visit, carry, (key_blocks, value_blocks, firsts))  37.5 us
    dot_general x64, matrix products, attend(): jnp.einsum('kgtn,nkd->kgtd', probs.astype(jnp.bfloat16), value_block, pre...  18 us
  transfers between devices with their start and end apart: 6, of which 5 were waited for; matrix products, arithmetic and copies ran while one was open for 33% of the time, Pallas kernels for 0%

commit v1 on v0

v1 whole, which is shorter than its diff:
```python
import math

import jax
import jax.numpy as jnp
from jax import lax
from jax.experimental import pallas as pl
from jax.experimental.pallas import tpu as pltpu
from jax.sharding import Mesh
from jax.sharding import PartitionSpec as P

D = 2048
HALF = D // 2
HD = 128
TOPK = 8
SPAN = 64
EXPERTS = 128
OWN = 16
CAP = 2
CHIP = ("yh", "z")
CTX = ("yh", "z", "core")
ALL = ("yh", "z", "core", "exp")
NEG_BIG = -1e30
SWAP = [(0, 1), (1, 0)]


def swapped(x):
    return lax.ppermute(x, "core", SWAP)


def attend_kernel(span_ref, ctx_ref, q_ref, near_ref, far_ref, o_ref, s_ref):
    ctx = ctx_ref[0]
    core = lax.rem(ctx, 2)
    rows = q_ref.shape[0]
    part = near_ref.shape[0]
    q = q_ref[...]
    row = lax.broadcasted_iota(jnp.int32, (rows, 1), 0)
    q_place = jnp.where(
        row < SPAN,
        span_ref[2 * ctx] * SPAN + row,
        span_ref[2 * ctx + 1] * SPAN + row - SPAN,
    )
    lane = lax.broadcasted_iota(jnp.int32, (1, 2 * SPAN), 1)
    dims = (((1,), (1,)), ((), ()))
    top = jnp.full((rows, 128), NEG_BIG, jnp.float32)
    blocks = part // 128
    for side, ref in enumerate((near_ref, far_ref)):
        held = jnp.where(side == 0, core, 1 - core)
        for b in range(blocks):
            k = ref[b * 128 : (b + 1) * 128, 0:HD]
            s = lax.dot_general(q, k, dims, preferred_element_type=jnp.float32)
            at = 2 * (2 * b + held)
            place = jnp.where(
                lane < SPAN,
                span_ref[at] * SPAN + lane,
                span_ref[at + 1] * SPAN + lane - SPAN,
            )
            s = jnp.where(place <= q_place, s, NEG_BIG)
            c0 = (side * blocks + b) * 128
            s_ref[:, c0 : c0 + 128] = s
            top = jnp.maximum(top, s)
    top = jnp.max(top, axis=1, keepdims=True)
    scale = math.log2(math.e) / math.sqrt(HD)
    total = jnp.zeros((rows, 128), jnp.float32)
    acc = jnp.zeros((rows, HD), jnp.float32)
    wide = 512
    for side, ref in enumerate((near_ref, far_ref)):
        for b in range(part // wide):
            c0 = side * part + b * wide
            p = jnp.exp2((s_ref[:, c0 : c0 + wide] - top) * scale)
            for j in range(wide // 128):
                total = total + p[:, j * 128 : (j + 1) * 128]
            v = ref[b * wide : (b + 1) * wide, HD : 2 * HD]
            acc = acc + jnp.dot(p.astype(jnp.bfloat16), v, preferred_element_type=jnp.float32)
    o_ref[...] = (acc / jnp.sum(total, axis=1, keepdims=True)).astype(o_ref.dtype)


def attend(span_order, ctx, queries, near, far):
    rows, width = queries.shape
    keys = near.shape[0] + far.shape[0]
    return pl.pallas_call(
        attend_kernel,
        out_shape=jax.ShapeDtypeStruct((rows, width), jnp.bfloat16),
        grid_spec=pltpu.PrefetchScalarGridSpec(
            num_scalar_prefetch=2,
            grid=(width // HD,),
            in_specs=[
                pl.BlockSpec((rows, HD), lambda h, *_: (0, h)),
                pl.BlockSpec(near.shape, lambda h, *_: (0, 0)),
                pl.BlockSpec(far.shape, lambda h, *_: (0, 0)),
            ],
            out_specs=pl.BlockSpec((rows, HD), lambda h, *_: (0, h)),
            scratch_shapes=[pltpu.VMEM((rows, keys), jnp.float32)],
        ),
        cost_estimate=pl.CostEstimate(
            flops=4 * rows * width * keys,
            bytes_accessed=4 * keys * HD * 2 + 4 * rows * width,
            transcendentals=rows * keys * width // HD,
        ),
    )(span_order, ctx, queries, near, far)


def copies(x, axes):
    count = lax.axis_size(axes)
    return jnp.broadcast_to(x[None], (count, *x.shape))


def gathered(x):
    near = lax.all_to_all(copies(x, CHIP), CHIP, 0, 0, tiled=True)
    near = near.reshape(-1, x.shape[-1])
    return near, swapped(near)


def by_plane(x):
    rows = x.shape[0]
    return x.reshape(rows, D // 128, 2, 64).transpose(0, 2, 1, 3).reshape(rows, D)


def from_planes(x):
    rows = x.shape[0]
    return x.reshape(rows, 2, D // 128, 64).transpose(0, 2, 1, 3).reshape(rows, D)


def shards(
    queries,
    keys,
    values,
    span_order,
    stream_in,
    wo,
    norm_gain,
    expert_ids,
    expert_gates,
    w_gate,
    w_up,
    w_down,
):
    core = lax.axis_index("core")
    ctx = lax.axis_index(CTX)
    exp = lax.axis_index("exp")

    gate_w = lax.all_to_all(w_gate, CHIP, 0, 0, tiled=True)
    up_w = lax.all_to_all(w_up, CHIP, 0, 0, tiled=True)
    down_w = lax.all_to_all(w_down, CHIP, 0, 0, tiled=True)

    head = exp // 2 * HD
    mine = jnp.concatenate(
        [
            lax.dynamic_slice_in_dim(keys, head, HD, 1),
            lax.dynamic_slice_in_dim(values, head, HD, 1),
        ],
        axis=1,
    )
    near, far = gathered(mine)
    wo_near, wo_far = gathered(wo.transpose(2, 0, 1).reshape(wo.shape[2], -1))

    attended = attend(span_order, ctx[None].astype(jnp.int32), queries, near, far)
    dims = (((1,), (1,)), ((), ()))
    a = lax.dot_general(attended, wo_near, dims, preferred_element_type=jnp.float32)
    b = lax.dot_general(attended, wo_far, dims, preferred_element_type=jnp.float32)
    mixed = jnp.concatenate(
        [jnp.where(core == 0, a, b), jnp.where(core == 0, b, a)], axis=1
    ).astype(jnp.bfloat16)
    mixed = lax.all_to_all(
        mixed.reshape(8, -1, D), "exp", 0, 0, tiled=True
    )
    resid = by_plane(stream_in.astype(jnp.float32)) + mixed.astype(jnp.float32).sum(axis=0)
    gain = by_plane(norm_gain.astype(jnp.float32)[None])
    normed = (
        resid
        * lax.rsqrt(jnp.mean(resid * resid, axis=-1, keepdims=True) + 1e-06)
        * gain
    ).astype(jnp.bfloat16)

    rows = stream_in.shape[0]
    flat = expert_ids.reshape(-1)
    hits = (flat[:, None] == jnp.arange(EXPERTS, dtype=jnp.int32)[None, :]).astype(jnp.float32)
    before = (
        jnp.arange(rows * TOPK)[:, None] > jnp.arange(rows * TOPK)[None, :]
    ).astype(jnp.float32)
    ahead = jnp.dot(before, hits, preferred_element_type=jnp.float32)
    rank = jnp.sum(ahead * hits, axis=1).astype(jnp.int32)
    slots = (((flat % OWN) * 8 + flat // OWN) * CAP + rank).reshape(rows, TOPK)
    slot_ids = jnp.arange(EXPERTS * CAP, dtype=jnp.int32)
    placing = jnp.any(slots[None, :, :] == slot_ids[:, None, None], axis=2).astype(jnp.bfloat16)
    combine = jnp.sum(
        jnp.where(
            slots[:, :, None] == slot_ids[None, None, :],
            expert_gates[:, :, None],
            jnp.zeros((), jnp.bfloat16),
        ),
        axis=1,
    )

    outgoing = jnp.dot(placing, normed, preferred_element_type=jnp.float32).astype(jnp.bfloat16)
    outgoing = (
        outgoing.reshape(OWN, 8, CAP, 2, HALF)
        .transpose(0, 3, 1, 2, 4)
        .reshape(256, CAP, HALF)
    )
    tokens = lax.all_to_all(outgoing, ALL, 0, 0, tiled=True).reshape(512, HALF)

    gate_w = gate_w.reshape(HALF, -1)
    up_w = up_w.reshape(HALF, -1)
    down_w = down_w.reshape(HALF, -1)
    g = jnp.dot(tokens, gate_w, preferred_element_type=jnp.float32)
    u = jnp.dot(tokens, up_w, preferred_element_type=jnp.float32)
    gu = jnp.concatenate([g, u], axis=1).reshape(2, 256, -1)
    keep = jnp.where(core == 0, gu[0], gu[1])
    send = jnp.where(core == 0, gu[1], gu[0])
    both = keep + swapped(send)
    width = both.shape[1] // 2
    act = (jax.nn.silu(both[:, :width]) * both[:, width:]).astype(jnp.bfloat16)
    act_other = swapped(act)
    act = jnp.concatenate(
        [jnp.where(core == 0, act, act_other), jnp.where(core == 0, act_other, act)],
        axis=0,
    )
    out = lax.dot_general(
        act, down_w, (((1,), (1,)), ((), ())), preferred_element_type=jnp.float32
    ).astype(jnp.bfloat16)
    home = lax.all_to_all(out.reshape(256, CAP, HALF), ALL, 0, 0, tiled=True)
    home = home.reshape(OWN, 2, 8, CAP, HALF).transpose(0, 2, 3, 1, 4).reshape(EXPERTS * CAP, D)
    moe = jnp.dot(combine, home, preferred_element_type=jnp.float32)
    return from_planes(resid + moe)


def solution(mesh):
    finer = Mesh(mesh.devices.reshape(2, 8, 2, 8), ALL)
    return jax.shard_map(
        shards,
        mesh=finer,
        in_specs=(
            P(CTX, "exp"),
            P(CTX, None),
            P(CTX, None),
            P(),
            P(ALL, None),
            P("exp", None, CTX),
            P(),
            P(ALL, None),
            P(ALL, None),
            P("exp", CTX, None),
            P("exp", CTX, None),
            P("exp", CTX, None),
        ),
        out_specs=P(ALL, None),
        check_vma=False,
    )
```

time: 587 us -> 327 us (0.56)
  other arithmetic: 111 us -> 4.25 us
  blocking collectives: 122 us -> 51.8 us
  local copies, waits for them, and re-layouts: 62.5 us -> 12.6 us
  matrix products: 41 us -> 11.5 us
  starting transfers between devices: 18.5 us -> 43 us
  waiting for transfers between devices: 213 us -> 193 us
  between operations: 13.8 us -> 0.26 us
  Pallas kernels: 0 us -> 9.48 us
    all_gather x2 -> x0, waiting for transfers between devices: 74.9 us -> none  [the longest x1 74.9 us: sent_together(): lax.all_gather(both, axis, axis=dim, tiled=True)]
    all_to_all x3 -> x2, blocking collectives: 122 us -> 51.8 us  [the longest x1 36.8 us: shards(): tokens = lax.all_to_all(outgoing, ALL, 0, 0, tiled=True).reshape(512, HALF)]
    all_to_all x4 -> x6, waiting for transfers between devices: 138 us -> 191 us  [the longest x2 55.4 us: gathered(): near = lax.all_to_all(copies(x, CHIP), CHIP, 0, 0, tiled=True)]
    add x130 -> x3, other arithmetic: 43.6 us -> 1.71 us  [the longest x1 1.68 us: shards(): both = keep + swapped(send)]
    select_n x65 -> x2, other arithmetic: 41.8 us -> 1.7 us  [the longest x1 1.35 us: shards(): send = jnp.where(core == 0, gu[1], gu[0])]
    dynamic_slice x65 -> x1, local copies, waits for them, and re-layouts: 38.3 us -> 0.81 us  [shards(): lax.dynamic_slice_in_dim(values, head, HD, 1)]
    dot_general x133 -> x7, matrix products: 40.5 us -> 11 us  [the longest x1 2.7 us: shards(): g = jnp.dot(tokens, gate_w, preferred_element_type=jnp.float32)]
    all_to_all x4 -> x6, starting transfers between devices: 18.5 us -> 42.8 us  [the longest x2 16.5 us: gathered(): near = lax.all_to_all(copies(x, CHIP), CHIP, 0, 0, tiled=True)]
  transfers between devices with their start and end apart: 6 -> 10, of which waited for: 5 -> 7; matrix products, arithmetic and copies ran while one was open for 33% -> 3% of each run, Pallas kernels for 0% -> 3%
where the time goes in v1:
time: 327 us; the launch traced here: 325 us
  waiting for transfers between devices  193 us (59%)
  blocking collectives  51.8 us (16%)
  starting transfers between devices  43 us (13%)
  local copies, waits for them, and re-layouts  12.6 us (4%)
  matrix products  11.5 us (4%)
  Pallas kernels  9.48 us (3%)
  other arithmetic  4.25 us (1%)
    all_to_all x2, waiting for transfers between devices, gathered(): near = lax.all_to_all(copies(x, CHIP), CHIP, 0, 0, tiled=True)  55.4 us
    all_to_all x1, blocking collectives, shards(): tokens = lax.all_to_all(outgoing, ALL, 0, 0, tiled=True).reshape(512, HALF)  36.8 us
    all_to_all x1, waiting for transfers between devices, shards(): up_w = lax.all_to_all(w_up, CHIP, 0, 0, tiled=True)  35.2 us
    all_to_all x1, waiting for transfers between devices, shards(): down_w = lax.all_to_all(w_down, CHIP, 0, 0, tiled=True)  34.9 us
    all_to_all x1, waiting for transfers between devices, shards(): gate_w = lax.all_to_all(w_gate, CHIP, 0, 0, tiled=True)  34.8 us
    all_to_all x1, waiting for transfers between devices, shards(): home = lax.all_to_all(out.reshape(256, CAP, HALF), ALL, 0, 0, tiled=True)  30.6 us
    all_to_all x2, starting transfers between devices, gathered(): near = lax.all_to_all(copies(x, CHIP), CHIP, 0, 0, tiled=True)  16.5 us
    all_to_all x1, blocking collectives, shards(): mixed = lax.all_to_all(mixed.reshape(8, -1, D), 'exp', 0, 0, tiled=True)  15 us
  transfers between devices with their start and end apart: 10, of which 7 were waited for; matrix products, arithmetic and copies ran while one was open for 3% of the time, Pallas kernels for 3%

profile of v1, /device:TPU:32, one launch (start us, length us, event | category | flops | bytes accessed | tf_op | source)
XLA Modules:
  0.0 325.4 jit_solution(12122645594343353317)
XLA Ops:
  1.9 11.2 %all-to-all-start = ((bf16[16,128,256]{2,1,0:T(8,128)(2,1)}), bf16[16,128,256]{2,1,0:T(8,128)(2,1)S(1)}, u32[]{:S(2)}, u32[]{:S(2)}) async-start(bf16[16,128,256]{2,1,0:T(8,128)(2,1)} %broadcast_in_dim.17), calls=%async_computation | async-start | bytes 2097152 | tf_op jit(solution)/shard_map/all_to_all | solution.py:108
  13.1 27.7 %all-to-all-done = bf16[16,128,256]{2,1,0:T(8,128)(2,1)S(1)} async-done(((bf16[16,128,256]{2,1,0:T(8,128)(2,1)}), bf16[16,128,256]{2,1,0:T(8,128)(2,1)S(1)}, u32[]{:S(2)}, u32[]{:S(2)}) %all-to-all-start) | async-done | bytes 1048608 | tf_op jit(solution)/shard_map/all_to_all | solution.py:108
  40.8 1.2 broadcast_in_dim.38
  42.0 5.3 %all-to-all-start.1 = ((bf16[16,64,512]{2,1,0:T(8,128)(2,1)}), bf16[16,64,512]{2,1,0:T(8,128)(2,1)S(1)}, u32[]{:S(2)}, u32[]{:S(2)}) async-start(bf16[16,64,512]{2,1,0:T(8,128)(2,1)} %broadcast_in_dim.38), calls=%async_computation.1 | async-start | bytes 2097152 | tf_op jit(solution)/shard_map/all_to_all | solution.py:108
  47.4 27.7 %all-to-all-done.1 = bf16[16,64,512]{2,1,0:T(8,128)(2,1)S(1)} async-done(((bf16[16,64,512]{2,1,0:T(8,128)(2,1)}), bf16[16,64,512]{2,1,0:T(8,128)(2,1)S(1)}, u32[]{:S(2)}, u32[]{:S(2)}) %all-to-all-start.1) | async-done | bytes 1048608 | tf_op jit(solution)/shard_map/all_to_all | solution.py:108
  75.2 9.5 %shard_map.118 = bf16[128,512]{1,0:T(8,128)(2,1)} custom-call(s32[64]{0:T(128)} %span_ref.1, s32[1]{0:T(128)} %bitcast.1.ctx_ref, bf16[128,512]{1,0:T(8,128)(2,1)} %q_ref.1, bf16[2048,256]{1,0:T(8,128)(2,1)} %bitcast.54, bf16[2048,256]{1,0:T(8,128)(2,1)} %collective-permute-done.far_ref), custom_call_target="tpu_custom_call" | custom-call | flops 1073741824 | bytes 4456448 | tf_op jit(solution)/shard_map/pallas_call | solution.py:80
  84.6 1.4 fusion.21
  86.0 1.4 select_convert_fusion.1
  87.4 15.0 %all_to_all.40 = bf16[8,16,2048]{2,1,0:T(8,128)(2,1)S(1)} all-to-all(bf16[8,16,2048]{2,1,0:T(8,128)(2,1)S(1)} %pad_maximum_fusion.1), channel_id=1, replica_groups=mesh['yh'=2,'z'=8,'core'=2,'exp'=8] {'exp'}, dimensions={0} | all-to-all | bytes 1048576 | tf_op jit(solution)/shard_map/all_to_all | solution.py:163
  102.4 6.1 %all-to-all-start.4 = ((bf16[16,64,768]{2,1,0:T(8,128)(2,1)}), bf16[16,64,768]{2,1,0:T(8,128)(2,1)}, u32[]{:S(2)}, u32[]{:S(2)}) async-start(bf16[16,64,768]{2,1,0:T(8,128)(2,1)} %param.21), calls=%async_computation.4 | async-start | bytes 3145728 | tf_op jit(solution)/shard_map/all_to_all | solution.py:141
  112.8 34.8 %all-to-all-done.4 = bf16[16,64,768]{2,1,0:T(8,128)(2,1)} async-done(((bf16[16,64,768]{2,1,0:T(8,128)(2,1)}), bf16[16,64,768]{2,1,0:T(8,128)(2,1)}, u32[]{:S(2)}, u32[]{:S(2)}) %all-to-all-start.4) | async-done | bytes 1572896 | tf_op jit(solution)/shard_map/all_to_all | solution.py:141
  147.6 36.8 %all_to_all.41 = bf16[256,2,1024]{2,1,0:T(2,128)(2,1)S(1)} all-to-all(bf16[256,2,1024]{2,1,0:T(2,128)(2,1)S(1)} %copy.69), channel_id=1, replica_groups=mesh['yh'=2,'z'=8,'core'=2,'exp'=8] {'yh','z','core','exp'}, dimensions={0} | all-to-all | bytes 2097152 | tf_op jit(solution)/shard_map/all_to_all | solution.py:200
  184.5 5.4 %all-to-all-start.5 = ((bf16[16,64,768]{2,1,0:T(8,128)(2,1)}), bf16[16,64,768]{2,1,0:T(8,128)(2,1)S(1)}, u32[]{:S(2)}, u32[]{:S(2)}) async-start(bf16[16,64,768]{2,1,0:T(8,128)(2,1)} %param.22), calls=%async_computation.5 | async-start | bytes 3145728 | tf_op jit(solution)/shard_map/all_to_all | solution.py:142
  191.1 2.7 fusion.22
  193.8 35.2 %all-to-all-done.5 = bf16[16,64,768]{2,1,0:T(8,128)(2,1)S(1)} async-done(((bf16[16,64,768]{2,1,0:T(8,128)(2,1)}), bf16[16,64,768]{2,1,0:T(8,128)(2,1)S(1)}, u32[]{:S(2)}, u32[]{:S(2)}) %all-to-all-start.5) | async-done | bytes 1572896 | tf_op jit(solution)/shard_map/all_to_all | solution.py:142
  230.2 2.7 fusion.23
  232.9 1.3 broadcast_select_fusion
  234.2 5.5 %all-to-all-start.6 = ((bf16[16,64,768]{2,1,0:T(8,128)(2,1)}), bf16[16,64,768]{2,1,0:T(8,128)(2,1)}, u32[]{:S(2)}, u32[]{:S(2)}) async-start(bf16[16,64,768]{2,1,0:T(8,128)(2,1)} %param.23), calls=%async_computation.6 | async-start | bytes 3145728 | tf_op jit(solution)/shard_map/all_to_all | solution.py:143
  239.7 1.7 select_add_fusion
  241.7 1.7 collective-permute-done.3
  243.8 34.9 %all-to-all-done.6 = bf16[16,64,768]{2,1,0:T(8,128)(2,1)} async-done(((bf16[16,64,768]{2,1,0:T(8,128)(2,1)}), bf16[16,64,768]{2,1,0:T(8,128)(2,1)}, u32[]{:S(2)}, u32[]{:S(2)}) %all-to-all-start.6) | async-done | bytes 1572896 | tf_op jit(solution)/shard_map/all_to_all | solution.py:143
  278.7 2.4 convolution_convert_fusion.1
  282.3 9.2 %all-to-all-start.7 = ((bf16[256,2,1024]{2,1,0:T(2,128)(2,1)}), bf16[256,2,1024]{2,1,0:T(2,128)(2,1)S(1)}, u32[]{:S(2)}, u32[]{:S(2)}) async-start(bf16[256,2,1024]{2,1,0:T(2,128)(2,1)} %reshape.153), calls=%async_computation.7 | async-start | bytes 2097152 | tf_op jit(solution)/shard_map/all_to_all | solution.py:221
  291.8 30.6 %all-to-all-done.7 = bf16[256,2,1024]{2,1,0:T(2,128)(2,1)S(1)} async-done(((bf16[256,2,1024]{2,1,0:T(2,128)(2,1)}), bf16[256,2,1024]{2,1,0:T(2,128)(2,1)S(1)}, u32[]{:S(2)}, u32[]{:S(2)}) %all-to-all-start.7) | async-done | bytes 1048608 | tf_op jit(solution)/shard_map/all_to_all | solution.py:221
  (61 shorter events, 13.8 us)
Async XLA Ops:
  0.0 13.1 %copy-start = (bf16[4,128,64]{1,2,0:T(8,128)(2,1)S(1)}, bf16[4,128,64]{1,2,0:T(8,128)(2,1)}, u32[]{:S(2)}) copy-start(bf16[4,128,64]{1,2,0:T(8,128)(2,1)} %param.17) | copy-start | bytes 196612
  1.9 38.9 %all-to-all-start = ((bf16[16,128,256]{2,1,0:T(8,128)(2,1)}), bf16[16,128,256]{2,1,0:T(8,128)(2,1)S(1)}, u32[]{:S(2)}, u32[]{:S(2)}) async-start(bf16[16,128,256]{2,1,0:T(8,128)(2,1)} %broadcast_in_dim.17), calls=%async_computation | async-start | bytes 2097152 | tf_op jit(solution)/shard_map/all_to_all | solution.py:108
  40.8 6.5 %copy-start.2 = (bf16[16,128,256]{2,1,0:T(8,128)(2,1)}, bf16[16,128,256]{2,1,0:T(8,128)(2,1)S(1)}, u32[]{:S(2)}) copy-start(bf16[16,128,256]{2,1,0:T(8,128)(2,1)S(1)} %all-to-all-done) | copy-start | bytes 3145732
  42.0 33.1 %all-to-all-start.1 = ((bf16[16,64,512]{2,1,0:T(8,128)(2,1)}), bf16[16,64,512]{2,1,0:T(8,128)(2,1)S(1)}, u32[]{:S(2)}, u32[]{:S(2)}) async-start(bf16[16,64,512]{2,1,0:T(8,128)(2,1)} %broadcast_in_dim.38), calls=%async_computation.1 | async-start | bytes 2097152 | tf_op jit(solution)/shard_map/all_to_all | solution.py:108
  47.3 27.8 %collective-permute-start = (bf16[2048,256]{1,0:T(8,128)(2,1)S(1)}, bf16[2048,256]{1,0:T(8,128)(2,1)}, u32[]{:S(2)}, u32[]{:S(2)}) collective-permute-start(bf16[2048,256]{1,0:T(8,128)(2,1)S(1)} %bitcast.53), channel_id=1, source_target_pairs={{0,8},{8,0},{1,9},{9,1},{2,10},{10,2},{3,11},{11,3},{4,12},{12,4},... | collective-permute-start | bytes 3145736 | tf_op jit(solution)/shard_map/ppermute | solution.py:27
  75.2 9.5 %collective-permute-start.1 = (bf16[1024,512]{1,0:T(8,128)(2,1)S(1)}, bf16[1024,512]{1,0:T(8,128)(2,1)S(1)}, u32[]{:S(2)}, u32[]{:S(2)}) collective-permute-start(bf16[1024,512]{1,0:T(8,128)(2,1)S(1)} %bitcast.47), channel_id=1, source_target_pairs={{0,8},{8,0},{1,9},{9,1},{2,10},{10,2},{3,11},{11,3},{4,12},{12,4},... | collective-permute-start | bytes 3145736 | tf_op jit(solution)/shard_map/ppermute | solution.py:27
  102.4 6.1 %copy-start.3 = (bf16[16,2048]{1,0:T(8,128)(2,1)S(1)}, bf16[16,2048]{1,0:T(8,128)(2,1)}, u32[]{:S(2)}) copy-start(bf16[16,2048]{1,0:T(8,128)(2,1)} %param.16) | copy-start | bytes 196612
  102.4 6.5 %copy-start.4 = (s32[16,8]{0,1:T(8,128)S(1)}, s32[16,8]{0,1:T(8,128)}, u32[]{:S(2)}) copy-start(s32[16,8]{0,1:T(8,128)} %param.19) | copy-start | bytes 1540
  102.4 6.9 %copy-start.5 = (bf16[2048]{0:T(1024)(128)(2,1)S(1)}, bf16[2048]{0:T(1024)(128)(2,1)}, u32[]{:S(2)}) copy-start(bf16[2048]{0:T(1024)(128)(2,1)} %param.18) | copy-start | bytes 12292
  102.4 45.2 %all-to-all-start.4 = ((bf16[16,64,768]{2,1,0:T(8,128)(2,1)}), bf16[16,64,768]{2,1,0:T(8,128)(2,1)}, u32[]{:S(2)}, u32[]{:S(2)}) async-start(bf16[16,64,768]{2,1,0:T(8,128)(2,1)} %param.21), calls=%async_computation.4 | async-start | bytes 3145728 | tf_op jit(solution)/shard_map/all_to_all | solution.py:141
  184.5 44.6 %all-to-all-start.5 = ((bf16[16,64,768]{2,1,0:T(8,128)(2,1)}), bf16[16,64,768]{2,1,0:T(8,128)(2,1)S(1)}, u32[]{:S(2)}, u32[]{:S(2)}) async-start(bf16[16,64,768]{2,1,0:T(8,128)(2,1)} %param.22), calls=%async_computation.5 | async-start | bytes 3145728 | tf_op jit(solution)/shard_map/all_to_all | solution.py:142
  229.0 1.2 copy-start.1
  234.2 5.5 %collective-permute-start.2 = (f32[256,1536]{1,0:T(8,128)}, f32[256,1536]{1,0:T(8,128)}, u32[]{:S(2)}, u32[]{:S(2)}) collective-permute-start(f32[256,1536]{1,0:T(8,128)} %broadcast_select_fusion), channel_id=1, source_target_pairs={{0,8},{8,0},{1,9},{9,1},{2,10},{10,2},{3,11},{11,3},{4,12},{12,4},... | collective-permute-start | bytes 4718600 | tf_op jit(solution)/shard_map/ppermute | solution.py:27
  234.2 44.5 %all-to-all-start.6 = ((bf16[16,64,768]{2,1,0:T(8,128)(2,1)}), bf16[16,64,768]{2,1,0:T(8,128)(2,1)}, u32[]{:S(2)}, u32[]{:S(2)}) async-start(bf16[16,64,768]{2,1,0:T(8,128)(2,1)} %param.23), calls=%async_computation.6 | async-start | bytes 3145728 | tf_op jit(solution)/shard_map/all_to_all | solution.py:143
  241.6 1.8 collective-permute-start.3
  282.3 9.3 %copy-start.6 = (bf16[16,8]{0,1:T(8,128)(2,1)S(1)}, bf16[16,8]{0,1:T(8,128)(2,1)}, u32[]{:S(2)}) copy-start(bf16[16,8]{0,1:T(8,128)(2,1)} %param.20) | copy-start | bytes 772
  282.3 40.0 %all-to-all-start.7 = ((bf16[256,2,1024]{2,1,0:T(2,128)(2,1)}), bf16[256,2,1024]{2,1,0:T(2,128)(2,1)S(1)}, u32[]{:S(2)}, u32[]{:S(2)}) async-start(bf16[256,2,1024]{2,1,0:T(2,128)(2,1)} %reshape.153), calls=%async_computation.7 | async-start | bytes 2097152 | tf_op jit(solution)/shard_map/all_to_all | solution.py:221

commit v2 on v1

--- a/solution.py
+++ b/solution.py
@@ -7,6 +7,7 @@
 from jax.experimental.pallas import tpu as pltpu
 from jax.sharding import Mesh
 from jax.sharding import PartitionSpec as P
+
 
 D = 2048
 HALF = D // 2
@@ -27,11 +28,12 @@
     return lax.ppermute(x, "core", SWAP)
 
 
-def attend_kernel(span_ref, ctx_ref, q_ref, near_ref, far_ref, o_ref, s_ref):
-    ctx = ctx_ref[0]
+def attend_pieces(span_ref, ctx, q_ref, keys, values, o_ref, s_ref):
+    rows = q_ref.shape[0]
+    part = keys[0].shape[0]
+    blocks = part // 128
+    yh = ctx // 16
     core = lax.rem(ctx, 2)
-    rows = q_ref.shape[0]
-    part = near_ref.shape[0]
     q = q_ref[...]
     row = lax.broadcasted_iota(jnp.int32, (rows, 1), 0)
     q_place = jnp.where(
@@ -42,13 +44,12 @@
     lane = lax.broadcasted_iota(jnp.int32, (1, 2 * SPAN), 1)
     dims = (((1,), (1,)), ((), ()))
     top = jnp.full((rows, 128), NEG_BIG, jnp.float32)
-    blocks = part // 128
-    for side, ref in enumerate((near_ref, far_ref)):
-        held = jnp.where(side == 0, core, 1 - core)
+    for side in range(4):
+        first = (yh if side % 2 == 0 else 1 - yh) * 16 + (core if side < 2 else 1 - core)
         for b in range(blocks):
-            k = ref[b * 128 : (b + 1) * 128, 0:HD]
+            k = keys[side][b * 128 : (b + 1) * 128, :]
             s = lax.dot_general(q, k, dims, preferred_element_type=jnp.float32)
-            at = 2 * (2 * b + held)
+            at = 2 * (first + 2 * b)
             place = jnp.where(
                 lane < SPAN,
                 span_ref[at] * SPAN + lane,
@@ -63,51 +64,68 @@
     total = jnp.zeros((rows, 128), jnp.float32)
     acc = jnp.zeros((rows, HD), jnp.float32)
     wide = 512
-    for side, ref in enumerate((near_ref, far_ref)):
+    for side in range(4):
         for b in range(part // wide):
             c0 = side * part + b * wide
             p = jnp.exp2((s_ref[:, c0 : c0 + wide] - top) * scale)
             for j in range(wide // 128):
                 total = total + p[:, j * 128 : (j + 1) * 128]
-            v = ref[b * wide : (b + 1) * wide, HD : 2 * HD]
+            v = values[side][b * wide : (b + 1) * wide, :]
             acc = acc + jnp.dot(p.astype(jnp.bfloat16), v, preferred_element_type=jnp.float32)
     o_ref[...] = (acc / jnp.sum(total, axis=1, keepdims=True)).astype(o_ref.dtype)
 
 
-def attend(span_order, ctx, queries, near, far):
+def attend_kernel(span_ref, where_ref, q_ref, *refs):
+    own, cross = refs[0:4], refs[4:8]
+    o_ref, s_ref = refs[8:]
+    ctx = where_ref[0]
+
+    @pl.when(where_ref[1] == 0)
+    def _():
+        attend_pieces(span_ref, ctx, q_ref, own, cross, o_ref, s_ref)
+
+    @pl.when(where_ref[1] != 0)
+    def _():
+        attend_pieces(span_ref, ctx, q_ref, cross, own, o_ref, s_ref)
+
+
+def attend(span_order, where, queries, own, cross):
     rows, width = queries.shape
-    keys = near.shape[0] + far.shape[0]
+    keys = 4 * own[0].shape[0]
     return pl.pallas_call(
         attend_kernel,
         out_shape=jax.ShapeDtypeStruct((rows, width), jnp.bfloat16),
         grid_spec=pltpu.PrefetchScalarGridSpec(
             num_scalar_prefetch=2,
             grid=(width // HD,),
-            in_specs=[
-                pl.BlockSpec((rows, HD), lambda h, *_: (0, h)),
-                pl.BlockSpec(near.shape, lambda h, *_: (0, 0)),
-                pl.BlockSpec(far.shape, lambda h, *_: (0, 0)),
-            ],
+            in_specs=[pl.BlockSpec((rows, HD), lambda h, *_: (0, h))]
+            + [pl.BlockSpec(own[0].shape, lambda h, *_: (0, 0))] * 8,
             out_specs=pl.BlockSpec((rows, HD), lambda h, *_: (0, h)),
             scratch_shapes=[pltpu.VMEM((rows, keys), jnp.float32)],
         ),
         cost_estimate=pl.CostEstimate(
             flops=4 * rows * width * keys,
-            bytes_accessed=4 * keys * HD * 2 + 4 * rows * width,
+            bytes_accessed=4 * keys * HD + 4 * rows * width,
             transcendentals=rows * keys * width // HD,
         ),
-    )(span_order, ctx, queries, near, far)
+    )(span_order, where, queries, *own, *cross)
 
 
 def copies(x, axes):
-    count = lax.axis_size(axes)
-    return jnp.broadcast_to(x[None], (count, *x.shape))
-
-
-def gathered(x):
-    near = lax.all_to_all(copies(x, CHIP), CHIP, 0, 0, tiled=True)
-    near = near.reshape(-1, x.shape[-1])
-    return near, swapped(near)
+    return jnp.broadcast_to(x[None], (lax.axis_size(axes), *x.shape))
+
+
+def across_y(x):
+    return lax.ppermute(x, "yh", SWAP)
+
+
+def across_x(x):
+    return lax.ppermute(x, "exp", [(e, e ^ 1) for e in range(8)])
+
+
+def across_xy(x):
+    pairs = [(y * 8 + e, (1 - y) * 8 + (e ^ 1)) for y in range(2) for e in range(8)]
+    return lax.ppermute(x, ("yh", "exp"), pairs)
 
 
 def by_plane(x):
@@ -137,33 +155,59 @@
     core = lax.axis_index("core")
     ctx = lax.axis_index(CTX)
     exp = lax.axis_index("exp")
-
-    gate_w = lax.all_to_all(w_gate, CHIP, 0, 0, tiled=True)
-    up_w = lax.all_to_all(w_up, CHIP, 0, 0, tiled=True)
-    down_w = lax.all_to_all(w_down, CHIP, 0, 0, tiled=True)
+    yh = lax.axis_index("yh")
 
     head = exp // 2 * HD
-    mine = jnp.concatenate(
-        [
-            lax.dynamic_slice_in_dim(keys, head, HD, 1),
-            lax.dynamic_slice_in_dim(values, head, HD, 1),
-        ],
-        axis=1,
-    )
-    near, far = gathered(mine)
-    wo_near, wo_far = gathered(wo.transpose(2, 0, 1).reshape(wo.shape[2], -1))
-
-    attended = attend(span_order, ctx[None].astype(jnp.int32), queries, near, far)
-    dims = (((1,), (1,)), ((), ()))
-    a = lax.dot_general(attended, wo_near, dims, preferred_element_type=jnp.float32)
-    b = lax.dot_general(attended, wo_far, dims, preferred_element_type=jnp.float32)
+    mine = jnp.where(
+        exp % 2 == 0,
+        lax.dynamic_slice_in_dim(keys, head, HD, 1),
+        lax.dynamic_slice_in_dim(values, head, HD, 1),
+    )
+    packed = jnp.concatenate([mine, wo.transpose(0, 2, 1).reshape(-1, HD)], axis=0)
+    packed = lax.all_to_all(copies(packed, "z"), "z", 0, 0, tiled=True)
+    gate_up_w = lax.all_to_all(
+        jnp.concatenate([w_gate, w_up], axis=2), CHIP, 0, 0, tiled=True
+    ).reshape(HALF, -1)
+    down_w = lax.all_to_all(w_down, CHIP, 0, 0, tiled=True).reshape(HALF, -1)
+
+    piece = packed[:, : keys.shape[0]].reshape(-1, HD)
+    near = [piece, across_y(piece), across_x(piece), across_xy(piece)]
+    far = [swapped(p) for p in near]
+    wo_near = packed[:, keys.shape[0] :]
+    wo_far = swapped(wo_near)
+
+    attended = attend(
+        span_order,
+        jnp.stack([ctx, exp % 2]).astype(jnp.int32),
+        queries,
+        near[0:2] + far[0:2],
+        near[2:4] + far[2:4],
+    )
+    partner = across_y(attended)
+    rows = jnp.stack(
+        [attended.reshape(8, -1, 4 * HD), partner.reshape(8, -1, 4 * HD)], axis=1
+    ).reshape(-1, 4, HD)
+
+    def projected(w):
+        w = w.reshape(8, 4, 64, HD)
+        out = jnp.einsum("rhd,zhfd->rzf", rows, w, preferred_element_type=jnp.float32)
+        return out.reshape(-1, HALF // 2)
+
+    a, b = projected(wo_near), projected(wo_far)
     mixed = jnp.concatenate(
         [jnp.where(core == 0, a, b), jnp.where(core == 0, b, a)], axis=1
     ).astype(jnp.bfloat16)
-    mixed = lax.all_to_all(
-        mixed.reshape(8, -1, D), "exp", 0, 0, tiled=True
-    )
-    resid = by_plane(stream_in.astype(jnp.float32)) + mixed.astype(jnp.float32).sum(axis=0)
+    mixed = mixed.reshape(8, 32, HALF)
+    summed = lax.dynamic_index_in_dim(mixed, exp, 0, False).astype(jnp.float32)
+    for d in range(1, 8):
+        sent = lax.dynamic_index_in_dim(mixed, exp ^ d, 0, False)
+        got = lax.ppermute(sent, "exp", [(e, e ^ d) for e in range(8)])
+        summed = summed + got.astype(jnp.float32)
+    got = across_y(summed[16:])
+    low = jnp.where(yh == 0, summed[:16], got).reshape(16, 2, 1, -1)
+    high = jnp.where(yh == 0, got, summed[:16]).reshape(16, 2, 1, -1)
+    summed = jnp.concatenate([low, high], axis=2).reshape(16, D)
+    resid = by_plane(stream_in.astype(jnp.float32)) + summed
     gain = by_plane(norm_gain.astype(jnp.float32)[None])
     normed = (
         resid
@@ -199,12 +243,8 @@
     )
     tokens = lax.all_to_all(outgoing, ALL, 0, 0, tiled=True).reshape(512, HALF)
 
-    gate_w = gate_w.reshape(HALF, -1)
-    up_w = up_w.reshape(HALF, -1)
-    down_w = down_w.reshape(HALF, -1)
-    g = jnp.dot(tokens, gate_w, preferred_element_type=jnp.float32)
-    u = jnp.dot(tokens, up_w, preferred_element_type=jnp.float32)
-    gu = jnp.concatenate([g, u], axis=1).reshape(2, 256, -1)
+    gu = jnp.dot(tokens, gate_up_w, preferred_element_type=jnp.float32)
+    gu = gu.reshape(2, 256, -1)
     keep = jnp.where(core == 0, gu[0], gu[1])
     send = jnp.where(core == 0, gu[1], gu[0])
     both = keep + swapped(send)

time: 327 us -> 313 us (0.957)
  blocking collectives: 51.8 us -> 30 us
  starting transfers between devices: 43 us -> 54.8 us
  other arithmetic: 4.25 us -> 10.1 us
  waiting for transfers between devices: 193 us -> 189 us
  matrix products: 11.5 us -> 8 us
    all_to_all x5 -> x3, waiting for transfers between devices: 160 us -> 134 us  [the longest x1 71.8 us: shards(): lax.all_to_all(jnp.concatenate([w_gate, w_up], axis=2), CHIP, 0, 0, tiled...]
    all_to_all x2 -> x1, blocking collectives: 51.8 us -> 30 us  [shards(): packed = lax.all_to_all(copies(packed, 'z'), 'z', 0, 0, tiled=True)]
    ppermute x0 -> x12, waiting for transfers between devices: none -> 21.5 us  [the longest x3 11.7 us: across_y(): return lax.ppermute(x, 'yh', SWAP)]
    ppermute x0 -> x12, starting transfers between devices: none -> 21.2 us  [the longest x7 10.8 us: shards(): got = lax.ppermute(sent, 'exp', [(e, e ^ d) for e in range(8)])]
    all_to_all x5 -> x3, starting transfers between devices: 33.5 us -> 20.9 us  [the longest x1 8.65 us: shards(): tokens = lax.all_to_all(outgoing, ALL, 0, 0, tiled=True).reshape(512, HALF)]
    concatenate x2 -> x3, other arithmetic: 0.05 us -> 4.28 us  [the longest x1 3.31 us: shards(): jnp.concatenate([w_gate, w_up], axis=2)]
    dot_general x4 -> x3, matrix products: 8.15 us -> 4.67 us  [the longest x1 4 us: shards(): gu = jnp.dot(tokens, gate_up_w, preferred_element_type=jnp.float32)]
  transfers between devices with their start and end apart: 10 -> 23, of which waited for: 7 -> 14; matrix products, arithmetic and copies ran while one was open for 3% -> 3% of each run, Pallas kernels for 3% -> 3%
where the time goes in v2:
time: 313 us; the launch traced here: 312 us
  waiting for transfers between devices  189 us (60%)
  starting transfers between devices  54.8 us (18%)
  blocking collectives  30 us (10%)
  local copies, waits for them, and re-layouts  10.8 us (3%)
  other arithmetic  10.1 us (3%)
  Pallas kernels  9.14 us (3%)
  matrix products  8 us (3%)
    all_to_all x1, waiting for transfers between devices, shards(): lax.all_to_all(jnp.concatenate([w_gate, w_up], axis=2), CHIP, 0, 0, tiled...  71.8 us
    all_to_all x1, waiting for transfers between devices, shards(): down_w = lax.all_to_all(w_down, CHIP, 0, 0, tiled=True).reshape(HALF, -1)  34.8 us
    all_to_all x1, waiting for transfers between devices, shards(): home = lax.all_to_all(out.reshape(256, CAP, HALF), ALL, 0, 0, tiled=True)  30.6 us
    all_to_all x1, blocking collectives, shards(): packed = lax.all_to_all(copies(packed, 'z'), 'z', 0, 0, tiled=True)  30 us
    all_to_all x1, waiting for transfers between devices, shards(): tokens = lax.all_to_all(outgoing, ALL, 0, 0, tiled=True).reshape(512, HALF)  27.5 us
    all_to_all x1, starting transfers between devices, shards(): home = lax.all_to_all(out.reshape(256, CAP, HALF), ALL, 0, 0, tiled=True)  12 us
    ppermute x3, waiting for transfers between devices, across_y(): return lax.ppermute(x, 'yh', SWAP)  11.7 us
    ppermute x7, starting transfers between devices, shards(): got = lax.ppermute(sent, 'exp', [(e, e ^ d) for e in range(8)])  10.8 us
  transfers between devices with their start and end apart: 23, of which 14 were waited for; matrix products, arithmetic and copies ran while one was open for 3% of the time, Pallas kernels for 3%

profile of v2, /device:TPU:32, one launch (start us, length us, event | category | flops | bytes accessed | tf_op | source)
XLA Modules:
  0.0 312.0 jit_solution(13198742434031186678)
XLA Ops:
  1.7 30.0 %all_to_all.25 = bf16[8,384,128]{2,1,0:T(8,128)(2,1)S(1)} all-to-all(bf16[8,384,128]{2,1,0:T(8,128)(2,1)S(1)} %broadcast_in_dim.10), channel_id=1, replica_groups=mesh['yh'=2,'z'=8,'core'=2,'exp'=8] {'z'}, dimensions={0} | all-to-all | bytes 1572864 | tf_op jit(solution)/shard_map/all_to_all | solution.py:167
  31.8 3.3 %collective-permute-start = (bf16[1024,128]{1,0:T(8,128)(2,1)S(1)}, bf16[1024,128]{1,0:T(8,128)(2,1)S(1)}, u32[]{:S(2)}, u32[]{:S(2)}) collective-permute-start(bf16[1024,128]{1,0:T(8,128)(2,1)S(1)} %bitcast.91), channel_id=1, source_target_pairs={{0,128},{128,0},{1,129},{129,1},{2,130},{130,2},{3,131},{131,3},{4... | collective-permute-start | bytes 786440 | tf_op jit(solution)/shard_map/ppermute | solution.py:119
  37.5 4.3 %collective-permute-done.refs_1_ = bf16[1024,128]{1,0:T(8,128)(2,1)S(1)} collective-permute-done((bf16[1024,128]{1,0:T(8,128)(2,1)S(1)}, bf16[1024,128]{1,0:T(8,128)(2,1)S(1)}, u32[]{:S(2)}, u32[]{:S(2)}) %collective-permute-start) | collective-permute-done | bytes 262176 | tf_op jit(solution)/shard_map/ppermute | solution.py:119
  43.3 3.5 %collective-permute-done.4.refs_5_ = bf16[1024,128]{1,0:T(8,128)(2,1)S(1)} collective-permute-done((bf16[1024,128]{1,0:T(8,128)(2,1)S(1)}, bf16[1024,128]{1,0:T(8,128)(2,1)S(1)}, u32[]{:S(2)}, u32[]{:S(2)}) %collective-permute-start.4) | collective-permute-done | bytes 262176 | tf_op jit(solution)/shard_map/ppermute | solution.py:128
  49.1 9.1 %shard_map.118 = bf16[128,512]{1,0:T(8,128)(2,1)} custom-call(s32[64]{0:T(128)} %span_ref.1, s32[2]{0:T(128)} %pad_add_fusion.where_ref, bf16[128,512]{1,0:T(8,128)(2,1)} %q_ref.1, bf16[1024,128]{1,0:T(8,128)(2,1)} %bitcast.95, bf16[1024,128]{1,0:T(8,128)(2,1)} %copy-done.7, bf16[1024,128]{1,0:T(8,128)(2,1)} %copy-done.10, bf16[1024,128]{1,0:T(8,128)(2,1)} %copy-done.11, ...), custom_call_target="tpu_custom_call" | custom-call | flops 1073741824 | bytes 2359296 | tf_op jit(solution)/shard_map/pallas_call | solution.py:95
  58.3 2.3 collective-permute-start.7
  61.1 4.7 %collective-permute-done.7 = bf16[128,512]{1,0:T(8,128)(2,1)S(1)} collective-permute-done((bf16[128,512]{1,0:T(8,128)(2,1)}, bf16[128,512]{1,0:T(8,128)(2,1)S(1)}, u32[]{:S(2)}, u32[]{:S(2)}) %collective-permute-start.7) | collective-permute-done | bytes 131104 | tf_op jit(solution)/shard_map/ppermute | solution.py:119
  66.7 2.9 collective-permute-start.10
  71.7 4.3 %collective-permute-start.14 = (bf16[32,1024]{1,0:T(8,128)(2,1)S(1)}, bf16[32,1024]{1,0:T(8,128)(2,1)S(1)}, u32[]{:S(2)}, u32[]{:S(2)}) collective-permute-start(bf16[32,1024]{1,0:T(8,128)(2,1)S(1)} %get-tuple-element.12), channel_id=1, source_target_pairs={{0,6},{1,7},{2,4},{3,5},{4,2},{5,3},{6,0},{7,1},{8,14},{9,15},{10,... | collective-permute-start | bytes 196616 | tf_op jit(solution)/shard_map/ppermute | solution.py:204
  80.4 2.4 collective-permute-done.15
  82.9 3.0 collective-permute-start.16
  86.0 2.8 collective-permute-done.16
  91.2 2.0 copy.101
  93.3 8.7 %all-to-all-start.1 = ((bf16[256,2,1024]{2,1,0:T(2,128)(2,1)}), bf16[256,2,1024]{2,1,0:T(2,128)(2,1)S(1)}, u32[]{:S(2)}, u32[]{:S(2)}) async-start(bf16[256,2,1024]{2,1,0:T(2,128)(2,1)} %copy.101), calls=%async_computation.1 | async-start | bytes 2097152 | tf_op jit(solution)/shard_map/all_to_all | solution.py:244
  102.0 3.3 %pad_maximum_fusion = bf16[16,64,1536]{2,1,0:T(8,128)(2,1)} fusion(bf16[16,64,768]{2,1,0:T(8,128)(2,1)S(1)} %copy-done, bf16[16,64,768]{2,1,0:T(8,128)(2,1)} %param.21), kind=kLoop, calls=%fused_computation | loop fusion | flops 6291456 | bytes 6291456 | tf_op jit(solution)/shard_map/concatenate | solution.py:169
  105.3 27.5 %all-to-all-done.1 = bf16[256,2,1024]{2,1,0:T(2,128)(2,1)S(1)} async-done(((bf16[256,2,1024]{2,1,0:T(2,128)(2,1)}), bf16[256,2,1024]{2,1,0:T(2,128)(2,1)S(1)}, u32[]{:S(2)}, u32[]{:S(2)}) %all-to-all-start.1) | async-done | bytes 1048608 | tf_op jit(solution)/shard_map/all_to_all | solution.py:244
  132.7 5.4 %all-to-all-start.2 = ((bf16[16,64,1536]{2,1,0:T(8,128)(2,1)}), bf16[16,64,1536]{2,1,0:T(8,128)(2,1)}, u32[]{:S(2)}, u32[]{:S(2)}) async-start(bf16[16,64,1536]{2,1,0:T(8,128)(2,1)} %pad_maximum_fusion), calls=%async_computation.2 | async-start | bytes 6291456 | tf_op jit(solution)/shard_map/all_to_all | solution.py:168
  139.4 71.8 %all-to-all-done.2 = bf16[16,64,1536]{2,1,0:T(8,128)(2,1)} async-done(((bf16[16,64,1536]{2,1,0:T(8,128)(2,1)}), bf16[16,64,1536]{2,1,0:T(8,128)(2,1)}, u32[]{:S(2)}, u32[]{:S(2)}) %all-to-all-start.2) | async-done | bytes 3145760 | tf_op jit(solution)/shard_map/all_to_all | solution.py:168
  211.2 4.0 %fusion.43 = f32[512,1536]{1,0:T(8,128)S(1)} fusion(bf16[512,1024]{1,0:T(8,128)(2,1)} %reshape.178, bf16[1024,1536]{1,0:T(8,128)(2,1)} %bitcast.31), kind=kOutput, calls=%fused_computation.95 | convolution fusion | flops 1610612736 | bytes 7340032 | tf_op jit(solution)/shard_map/dot_general | solution.py:246
  216.6 6.8 %all-to-all-start.3 = ((bf16[16,64,768]{2,1,0:T(8,128)(2,1)}), bf16[16,64,768]{2,1,0:T(8,128)(2,1)}, u32[]{:S(2)}, u32[]{:S(2)}) async-start(bf16[16,64,768]{2,1,0:T(8,128)(2,1)} %param.23), calls=%async_computation.3 | async-start | bytes 3145728 | tf_op jit(solution)/shard_map/all_to_all | solution.py:171
  227.7 34.8 %all-to-all-done.3 = bf16[16,64,768]{2,1,0:T(8,128)(2,1)} async-done(((bf16[16,64,768]{2,1,0:T(8,128)(2,1)}), bf16[16,64,768]{2,1,0:T(8,128)(2,1)}, u32[]{:S(2)}, u32[]{:S(2)}) %all-to-all-start.3) | async-done | bytes 1572896 | tf_op jit(solution)/shard_map/all_to_all | solution.py:171
  262.4 2.4 convolution_convert_fusion.1
  266.1 12.0 %all-to-all-start.4 = ((bf16[256,2,1024]{2,1,0:T(2,128)(2,1)}), bf16[256,2,1024]{2,1,0:T(2,128)(2,1)S(1)}, u32[]{:S(2)}, u32[]{:S(2)}) async-start(bf16[256,2,1024]{2,1,0:T(2,128)(2,1)} %reshape.181), calls=%async_computation.4 | async-start | bytes 2097152 | tf_op jit(solution)/shard_map/all_to_all | solution.py:261
  278.3 30.6 %all-to-all-done.4 = bf16[256,2,1024]{2,1,0:T(2,128)(2,1)S(1)} async-done(((bf16[256,2,1024]{2,1,0:T(2,128)(2,1)}), bf16[256,2,1024]{2,1,0:T(2,128)(2,1)S(1)}, u32[]{:S(2)}, u32[]{:S(2)}) %all-to-all-start.4) | async-done | bytes 1048608 | tf_op jit(solution)/shard_map/all_to_all | solution.py:261
  (112 shorter events, 29.6 us)
Async XLA Ops:
  31.8 16.6 %copy-start.1 = (bf16[8,128,128]{2,1,0:T(8,128)(2,1)}, bf16[8,128,128]{2,1,0:T(8,128)(2,1)S(1)}, u32[]{:S(2)}) copy-start(bf16[8,128,128]{2,1,0:T(8,128)(2,1)S(1)} %slice.37) | copy-start | bytes 786436
  31.8 10.0 %collective-permute-start = (bf16[1024,128]{1,0:T(8,128)(2,1)S(1)}, bf16[1024,128]{1,0:T(8,128)(2,1)S(1)}, u32[]{:S(2)}, u32[]{:S(2)}) collective-permute-start(bf16[1024,128]{1,0:T(8,128)(2,1)S(1)} %bitcast.91), channel_id=1, source_target_pairs={{0,128},{128,0},{1,129},{129,1},{2,130},{130,2},{3,131},{131,3},{4... | collective-permute-start | bytes 786440 | tf_op jit(solution)/shard_map/ppermute | solution.py:119
  35.1 8.3 %collective-permute-start.3 = (bf16[1024,128]{1,0:T(8,128)(2,1)S(1)}, bf16[1024,128]{1,0:T(8,128)(2,1)S(1)}, u32[]{:S(2)}, u32[]{:S(2)}) collective-permute-start(bf16[1024,128]{1,0:T(8,128)(2,1)S(1)} %bitcast.92), channel_id=1, source_target_pairs={{0,1},{1,0},{2,3},{3,2},{4,5},{5,4},{6,7},{7,6},{8,9},{9,8},{10,11... | collective-permute-start | bytes 786440 | tf_op jit(solution)/shard_map/ppermute | solution.py:123
  36.6 10.3 %collective-permute-start.4 = (bf16[1024,128]{1,0:T(8,128)(2,1)S(1)}, bf16[1024,128]{1,0:T(8,128)(2,1)S(1)}, u32[]{:S(2)}, u32[]{:S(2)}) collective-permute-start(bf16[1024,128]{1,0:T(8,128)(2,1)S(1)} %bitcast.93), channel_id=1, source_target_pairs={{0,129},{1,128},{2,131},{3,130},{4,133},{5,132},{6,135},{7,134},{1... | collective-permute-start | bytes 786440 | tf_op jit(solution)/shard_map/ppermute | solution.py:128
  36.9 24.1 %collective-permute-start.8 = (bf16[8,256,128]{2,1,0:T(8,128)(2,1)S(1)}, bf16[8,256,128]{2,1,0:T(8,128)(2,1)S(1)}, u32[]{:S(2)}, u32[]{:S(2)}) collective-permute-start(bf16[8,256,128]{2,1,0:T(8,128)(2,1)S(1)} %slice.38), channel_id=1, source_target_pairs={{0,8},{8,0},{1,9},{9,1},{2,10},{10,2},{3,11},{11,3},{4,12},{12,4},... | collective-permute-start | bytes 1572872 | tf_op jit(solution)/shard_map/ppermute | solution.py:28
  37.0 10.4 %collective-permute-start.1 = (bf16[1024,128]{1,0:T(8,128)(2,1)S(1)}, bf16[1024,128]{1,0:T(8,128)(2,1)S(1)}, u32[]{:S(2)}, u32[]{:S(2)}) collective-permute-start(bf16[1024,128]{1,0:T(8,128)(2,1)S(1)} %bitcast.94), channel_id=1, source_target_pairs={{0,8},{8,0},{1,9},{9,1},{2,10},{10,2},{3,11},{11,3},{4,12},{12,4},... | collective-permute-start | bytes 786440 | tf_op jit(solution)/shard_map/ppermute | solution.py:28
  41.8 5.6 %collective-permute-start.2 = (bf16[1024,128]{1,0:T(8,128)(2,1)S(1)}, bf16[1024,128]{1,0:T(8,128)(2,1)S(1)}, u32[]{:S(2)}, u32[]{:S(2)}) collective-permute-start(bf16[1024,128]{1,0:T(8,128)(2,1)S(1)} %collective-permute-done.refs_1_), channel_id=1, source_target_pairs={{0,8},{8,0},{1,9},{9,1},{2,10},{10,2},{3,11},{11,3},{4,12},{12,4},... | collective-permute-start | bytes 786440 | tf_op jit(solution)/shard_map/ppermute | solution.py:28
  43.3 4.1 %collective-permute-start.5 = (bf16[1024,128]{1,0:T(8,128)(2,1)S(1)}, bf16[1024,128]{1,0:T(8,128)(2,1)S(1)}, u32[]{:S(2)}, u32[]{:S(2)}) collective-permute-start(bf16[1024,128]{1,0:T(8,128)(2,1)S(1)} %collective-permute-done.3.refs_4_), channel_id=1, source_target_pairs={{0,8},{8,0},{1,9},{9,1},{2,10},{10,2},{3,11},{11,3},{4,12},{12,4},... | collective-permute-start | bytes 786440 | tf_op jit(solution)/shard_map/ppermute | solution.py:28
  46.8 1.5 collective-permute-start.6
  58.3 7.5 %collective-permute-start.7 = (bf16[128,512]{1,0:T(8,128)(2,1)}, bf16[128,512]{1,0:T(8,128)(2,1)S(1)}, u32[]{:S(2)}, u32[]{:S(2)}) collective-permute-start(bf16[128,512]{1,0:T(8,128)(2,1)} %shard_map.118), channel_id=1, source_target_pairs={{0,128},{128,0},{1,129},{129,1},{2,130},{130,2},{3,131},{131,3},{4... | collective-permute-start | bytes 393224 | tf_op jit(solution)/shard_map/ppermute | solution.py:119
  66.7 9.4 %collective-permute-start.10 = (bf16[32,1024]{1,0:T(8,128)(2,1)S(1)}, bf16[32,1024]{1,0:T(8,128)(2,1)S(1)}, u32[]{:S(2)}, u32[]{:S(2)}) collective-permute-start(bf16[32,1024]{1,0:T(8,128)(2,1)S(1)} %get-tuple-element.8), channel_id=1, source_target_pairs={{0,2},{1,3},{2,0},{3,1},{4,6},{5,7},{6,4},{7,5},{8,10},{9,11},{10,... | collective-permute-start | bytes 196616 | tf_op jit(solution)/shard_map/ppermute | solution.py:204
  69.6 6.6 %collective-permute-start.11 = (bf16[32,1024]{1,0:T(8,128)(2,1)S(1)}, bf16[32,1024]{1,0:T(8,128)(2,1)S(1)}, u32[]{:S(2)}, u32[]{:S(2)}) collective-permute-start(bf16[32,1024]{1,0:T(8,128)(2,1)S(1)} %get-tuple-element.9), channel_id=1, source_target_pairs={{0,3},{1,2},{2,1},{3,0},{4,7},{5,6},{6,5},{7,4},{8,11},{9,10},{10,... | collective-permute-start | bytes 196616 | tf_op jit(solution)/shard_map/ppermute | solution.py:204
  70.1 8.0 %collective-permute-start.12 = (bf16[32,1024]{1,0:T(8,128)(2,1)S(1)}, bf16[32,1024]{1,0:T(8,128)(2,1)S(1)}, u32[]{:S(2)}, u32[]{:S(2)}) collective-permute-start(bf16[32,1024]{1,0:T(8,128)(2,1)S(1)} %get-tuple-element.10), channel_id=1, source_target_pairs={{0,4},{1,5},{2,6},{3,7},{4,0},{5,1},{6,2},{7,3},{8,12},{9,13},{10,... | collective-permute-start | bytes 196616 | tf_op jit(solution)/shard_map/ppermute | solution.py:204
  71.6 6.5 %collective-permute-start.13 = (bf16[32,1024]{1,0:T(8,128)(2,1)S(1)}, bf16[32,1024]{1,0:T(8,128)(2,1)S(1)}, u32[]{:S(2)}, u32[]{:S(2)}) collective-permute-start(bf16[32,1024]{1,0:T(8,128)(2,1)S(1)} %get-tuple-element.11), channel_id=1, source_target_pairs={{0,5},{1,4},{2,7},{3,6},{4,1},{5,0},{6,3},{7,2},{8,13},{9,12},{10,... | collective-permute-start | bytes 196616 | tf_op jit(solution)/shard_map/ppermute | solution.py:204
  71.7 7.8 %collective-permute-start.14 = (bf16[32,1024]{1,0:T(8,128)(2,1)S(1)}, bf16[32,1024]{1,0:T(8,128)(2,1)S(1)}, u32[]{:S(2)}, u32[]{:S(2)}) collective-permute-start(bf16[32,1024]{1,0:T(8,128)(2,1)S(1)} %get-tuple-element.12), channel_id=1, source_target_pairs={{0,6},{1,7},{2,4},{3,5},{4,2},{5,3},{6,0},{7,1},{8,14},{9,15},{10,... | collective-permute-start | bytes 196616 | tf_op jit(solution)/shard_map/ppermute | solution.py:204
  76.1 4.4 %collective-permute-start.9 = (bf16[32,1024]{1,0:T(8,128)(2,1)S(1)}, bf16[32,1024]{1,0:T(8,128)(2,1)S(1)}, u32[]{:S(2)}, u32[]{:S(2)}) collective-permute-start(bf16[32,1024]{1,0:T(8,128)(2,1)S(1)} %get-tuple-element.7), channel_id=1, source_target_pairs={{0,1},{1,0},{2,3},{3,2},{4,5},{5,4},{6,7},{7,6},{8,9},{9,8},{10,11... | collective-permute-start | bytes 196616 | tf_op jit(solution)/shard_map/ppermute | solution.py:204
  76.2 6.6 %collective-permute-start.15 = (bf16[32,1024]{1,0:T(8,128)(2,1)S(1)}, bf16[32,1024]{1,0:T(8,128)(2,1)S(1)}, u32[]{:S(2)}, u32[]{:S(2)}) collective-permute-start(bf16[32,1024]{1,0:T(8,128)(2,1)S(1)} %fusion.32), channel_id=1, source_target_pairs={{0,7},{1,6},{2,5},{3,4},{4,3},{5,2},{6,1},{7,0},{8,15},{9,14},{10,... | collective-permute-start | bytes 196616 | tf_op jit(solution)/shard_map/ppermute | solution.py:204
  82.9 5.9 %collective-permute-start.16 = (f32[16,1024]{1,0:T(8,128)S(1)}, f32[16,1024]{1,0:T(8,128)S(1)}, u32[]{:S(2)}, u32[]{:S(2)}) collective-permute-start(f32[16,1024]{1,0:T(8,128)S(1)} %slice.40), channel_id=1, source_target_pairs={{0,128},{128,0},{1,129},{129,1},{2,130},{130,2},{3,131},{131,3},{4... | collective-permute-start | bytes 196616 | tf_op jit(solution)/shard_map/ppermute | solution.py:119
  93.3 39.5 %all-to-all-start.1 = ((bf16[256,2,1024]{2,1,0:T(2,128)(2,1)}), bf16[256,2,1024]{2,1,0:T(2,128)(2,1)S(1)}, u32[]{:S(2)}, u32[]{:S(2)}) async-start(bf16[256,2,1024]{2,1,0:T(2,128)(2,1)} %copy.101), calls=%async_computation.1 | async-start | bytes 2097152 | tf_op jit(solution)/shard_map/all_to_all | solution.py:244
  132.7 78.5 %all-to-all-start.2 = ((bf16[16,64,1536]{2,1,0:T(8,128)(2,1)}), bf16[16,64,1536]{2,1,0:T(8,128)(2,1)}, u32[]{:S(2)}, u32[]{:S(2)}) async-start(bf16[16,64,1536]{2,1,0:T(8,128)(2,1)} %pad_maximum_fusion), calls=%async_computation.2 | async-start | bytes 6291456 | tf_op jit(solution)/shard_map/all_to_all | solution.py:168
  216.6 6.8 %collective-permute-start.17 = (f32[256,1536]{1,0:T(8,128)}, f32[256,1536]{1,0:T(8,128)}, u32[]{:S(2)}, u32[]{:S(2)}) collective-permute-start(f32[256,1536]{1,0:T(8,128)} %slice_select_fusion), channel_id=1, source_target_pairs={{0,8},{8,0},{1,9},{9,1},{2,10},{10,2},{3,11},{11,3},{4,12},{12,4},... | collective-permute-start | bytes 4718600 | tf_op jit(solution)/shard_map/ppermute | solution.py:28
  216.6 45.8 %all-to-all-start.3 = ((bf16[16,64,768]{2,1,0:T(8,128)(2,1)}), bf16[16,64,768]{2,1,0:T(8,128)(2,1)}, u32[]{:S(2)}, u32[]{:S(2)}) async-start(bf16[16,64,768]{2,1,0:T(8,128)(2,1)} %param.23), calls=%async_computation.3 | async-start | bytes 3145728 | tf_op jit(solution)/shard_map/all_to_all | solution.py:171
  225.5 1.8 collective-permute-start.18
  266.1 42.8 %all-to-all-start.4 = ((bf16[256,2,1024]{2,1,0:T(2,128)(2,1)}), bf16[256,2,1024]{2,1,0:T(2,128)(2,1)S(1)}, u32[]{:S(2)}, u32[]{:S(2)}) async-start(bf16[256,2,1024]{2,1,0:T(2,128)(2,1)} %reshape.181), calls=%async_computation.4 | async-start | bytes 2097152 | tf_op jit(solution)/shard_map/all_to_all | solution.py:261
  (13 other events, 80.7 us)

commit v3 on v2

--- a/solution.py
+++ b/solution.py
@@ -16,6 +16,7 @@
 SPAN = 64
 EXPERTS = 128
 OWN = 16
+FF = 768
 CAP = 2
 CHIP = ("yh", "z")
 CTX = ("yh", "z", "core")
@@ -111,8 +112,35 @@
     )(span_order, where, queries, *own, *cross)
 
 
-def copies(x, axes):
-    return jnp.broadcast_to(x[None], (lax.axis_size(axes), *x.shape))
+def assemble_kernel(z_ref, *refs):
+    parts, (piece_ref, wo_ref) = refs[:8], refs[8:]
+    for r, part in enumerate(parts):
+        at = lax.rem(z_ref[0] + r, 8)
+        piece_ref[pl.ds(pl.multiple_of(at * HD, HD), HD), :] = part[0:HD, :]
+        for h in range(4):
+            wo_ref[pl.ds(pl.multiple_of(at * 64, 64), 64), h * HD : (h + 1) * HD] = part[
+                HD + h * 64 : HD + (h + 1) * 64, :
+            ]
+
+
+def assembled(z, parts):
+    return pl.pallas_call(
+        assemble_kernel,
+        out_shape=(
+            jax.ShapeDtypeStruct((8 * HD, HD), jnp.bfloat16),
+            jax.ShapeDtypeStruct((8 * 64, 4 * HD), jnp.bfloat16),
+        ),
+        grid_spec=pltpu.PrefetchScalarGridSpec(
+            num_scalar_prefetch=1,
+            grid=(1,),
+            in_specs=[pl.BlockSpec(parts[0].shape, lambda i, *_: (0, 0))] * 8,
+            out_specs=(
+                pl.BlockSpec((8 * HD, HD), lambda i, *_: (0, 0)),
+                pl.BlockSpec((8 * 64, 4 * HD), lambda i, *_: (0, 0)),
+            ),
+        ),
+        cost_estimate=pl.CostEstimate(flops=0, bytes_accessed=1572864, transcendentals=0),
+    )(z[None].astype(jnp.int32), *parts)
 
 
 def across_y(x):
@@ -164,16 +192,18 @@
         lax.dynamic_slice_in_dim(values, head, HD, 1),
     )
     packed = jnp.concatenate([mine, wo.transpose(0, 2, 1).reshape(-1, HD)], axis=0)
-    packed = lax.all_to_all(copies(packed, "z"), "z", 0, 0, tiled=True)
-    gate_up_w = lax.all_to_all(
-        jnp.concatenate([w_gate, w_up], axis=2), CHIP, 0, 0, tiled=True
+    parts = [packed] + [
+        lax.ppermute(packed, "z", [((i + r) % 8, i) for i in range(8)])
+        for r in range(1, 8)
+    ]
+    weights = lax.all_to_all(
+        jnp.concatenate([w_gate, w_up, w_down], axis=2), CHIP, 0, 0, tiled=True
     ).reshape(HALF, -1)
-    down_w = lax.all_to_all(w_down, CHIP, 0, 0, tiled=True).reshape(HALF, -1)
-
-    piece = packed[:, : keys.shape[0]].reshape(-1, HD)
+    gate_up_w, down_w = weights[:, : 2 * FF], weights[:, 2 * FF :]
+
+    piece, wo_near = assembled(lax.axis_index("z"), parts)
     near = [piece, across_y(piece), across_x(piece), across_xy(piece)]
     far = [swapped(p) for p in near]
-    wo_near = packed[:, keys.shape[0] :]
     wo_far = swapped(wo_near)
 
     attended = attend(
@@ -186,12 +216,12 @@
     partner = across_y(attended)
     rows = jnp.stack(
         [attended.reshape(8, -1, 4 * HD), partner.reshape(8, -1, 4 * HD)], axis=1
-    ).reshape(-1, 4, HD)
+    ).reshape(-1, 4 * HD)
 
     def projected(w):
-        w = w.reshape(8, 4, 64, HD)
-        out = jnp.einsum("rhd,zhfd->rzf", rows, w, preferred_element_type=jnp.float32)
-        return out.reshape(-1, HALF // 2)
+        return lax.dot_general(
+            rows, w, (((1,), (1,)), ((), ())), preferred_element_type=jnp.float32
+        )
 
     a, b = projected(wo_near), projected(wo_far)
     mixed = jnp.concatenate(

time: 313 us -> 313 us (level)
  blocking collectives: 30 us -> 0 us
  waiting for transfers between devices: 189 us -> 204 us
  starting transfers between devices: 54.8 us -> 68.7 us
    all_to_all x1 -> x0, blocking collectives: 30 us -> none  [shards(): packed = lax.all_to_all(copies(packed, 'z'), 'z', 0, 0, tiled=True)]
    ppermute x0 -> x7, starting transfers between devices: none -> 17.6 us  [shards(): lax.ppermute(packed, 'z', [((i + r) % 8, i) for i in range(8)])]
    ppermute x0 -> x7, waiting for transfers between devices: none -> 12.3 us  [shards(): lax.ppermute(packed, 'z', [((i + r) % 8, i) for i in range(8)])]
    all_to_all x2 -> x1, starting transfers between devices: 12.3 us -> 5.44 us  [shards(): lax.all_to_all(jnp.concatenate([w_gate, w_up, w_down], axis=2), CHIP, 0,...]
    ppermute x3, waiting for transfers between devices: 11.7 us -> 7.73 us  [across_y(): return lax.ppermute(x, 'yh', SWAP)]
    ppermute x1, starting transfers between devices: 0.31 us -> 4.12 us  [across_xy(): return lax.ppermute(x, ('yh', 'exp'), pairs)]
    ppermute x1, waiting for transfers between devices: 1.52 us -> 4.93 us  [across_x(): return lax.ppermute(x, 'exp', [(e, e ^ 1) for e in range(8)])]
    ppermute x1, waiting for transfers between devices: 3.5 us -> 6.79 us  [across_xy(): return lax.ppermute(x, ('yh', 'exp'), pairs)]
  transfers between devices with their start and end apart: 23 -> 29, of which waited for: 14 -> 17; matrix products, arithmetic and copies ran while one was open for 3% -> 2% of each run, Pallas kernels for 3% -> 3%
where the time goes in v3:
time: 313 us; the launch traced here: 312 us
  waiting for transfers between devices  204 us (65%)
  starting transfers between devices  68.7 us (22%)
  Pallas kernels  11.3 us (4%)
  local copies, waits for them, and re-layouts  10.8 us (3%)
  other arithmetic  8.86 us (3%)
  matrix products  7.67 us (2%)
    all_to_all x1, waiting for transfers between devices, shards(): lax.all_to_all(jnp.concatenate([w_gate, w_up, w_down], axis=2), CHIP, 0,...  106 us
    all_to_all x1, waiting for transfers between devices, shards(): home = lax.all_to_all(out.reshape(256, CAP, HALF), ALL, 0, 0, tiled=True)  30.6 us
    all_to_all x1, waiting for transfers between devices, shards(): tokens = lax.all_to_all(outgoing, ALL, 0, 0, tiled=True).reshape(512, HALF)  27.1 us
    ppermute x7, starting transfers between devices, shards(): lax.ppermute(packed, 'z', [((i + r) % 8, i) for i in range(8)])  17.6 us
    all_to_all x1, starting transfers between devices, shards(): home = lax.all_to_all(out.reshape(256, CAP, HALF), ALL, 0, 0, tiled=True)  13.7 us
    ppermute x7, waiting for transfers between devices, shards(): lax.ppermute(packed, 'z', [((i + r) % 8, i) for i in range(8)])  12.3 us
    ppermute x7, starting transfers between devices, shards(): got = lax.ppermute(sent, 'exp', [(e, e ^ d) for e in range(8)])  12.1 us
    pallas_call x1, Pallas kernels, attend(): pl.pallas_call(attend_kernel, out_shape=jax.ShapeDtypeStruct((rows, width...  9.14 us
  transfers between devices with their start and end apart: 29, of which 17 were waited for; matrix products, arithmetic and copies ran while one was open for 2% of the time, Pallas kernels for 3%

profile of v3, /device:TPU:32, one launch (start us, length us, event | category | flops | bytes accessed | tf_op | source)
XLA Modules:
  0.0 311.8 jit_solution(12924104522325499875)
XLA Ops:
  3.6 4.5 %collective-permute-start.5 = (bf16[384,128]{1,0:T(8,128)(2,1)S(1)}, bf16[384,128]{1,0:T(8,128)(2,1)S(1)}, u32[]{:S(2)}, u32[]{:S(2)}) collective-permute-start(bf16[384,128]{1,0:T(8,128)(2,1)S(1)} %pad_maximum_fusion.3.refs_0_), channel_id=1, source_target_pairs={{96,0},{112,16},{0,32},{16,48},{32,64},{48,80},{64,96},{80,112},{9... | collective-permute-start | bytes 294920 | tf_op jit(solution)/shard_map/ppermute | solution.py:196
  11.5 3.1 %collective-permute-start.2 = (bf16[384,128]{1,0:T(8,128)(2,1)S(1)}, bf16[384,128]{1,0:T(8,128)(2,1)S(1)}, u32[]{:S(2)}, u32[]{:S(2)}) collective-permute-start(bf16[384,128]{1,0:T(8,128)(2,1)S(1)} %pad_maximum_fusion.3.refs_0_), channel_id=1, source_target_pairs={{48,0},{64,16},{80,32},{96,48},{112,64},{0,80},{16,96},{32,112},{4... | collective-permute-start | bytes 294920 | tf_op jit(solution)/shard_map/ppermute | solution.py:196
  19.2 5.6 %collective-permute-done.4.refs_5_ = bf16[384,128]{1,0:T(8,128)(2,1)S(1)} collective-permute-done((bf16[384,128]{1,0:T(8,128)(2,1)S(1)}, bf16[384,128]{1,0:T(8,128)(2,1)S(1)}, u32[]{:S(2)}, u32[]{:S(2)}) %collective-permute-start.4) | collective-permute-done | bytes 98336 | tf_op jit(solution)/shard_map/ppermute | solution.py:196
  25.4 5.0 %collective-permute-done.1.refs_2_ = bf16[384,128]{1,0:T(8,128)(2,1)S(1)} collective-permute-done((bf16[384,128]{1,0:T(8,128)(2,1)S(1)}, bf16[384,128]{1,0:T(8,128)(2,1)S(1)}, u32[]{:S(2)}, u32[]{:S(2)}) %collective-permute-start.1) | collective-permute-done | bytes 98336 | tf_op jit(solution)/shard_map/ppermute | solution.py:196
  34.4 4.1 %collective-permute-start.11 = (bf16[1024,128]{1,0:T(8,128)(2,1)}, bf16[1024,128]{1,0:T(8,128)(2,1)S(1)}, u32[]{:S(2)}, u32[]{:S(2)}) collective-permute-start(bf16[1024,128]{1,0:T(8,128)(2,1)} %get-tuple-element.7.refs_0_), channel_id=1, source_target_pairs={{0,129},{1,128},{2,131},{3,130},{4,133},{5,132},{6,135},{7,134},{1... | collective-permute-start | bytes 786440 | tf_op jit(solution)/shard_map/ppermute | solution.py:156
  39.3 6.8 %collective-permute-done.11.refs_5_ = bf16[1024,128]{1,0:T(8,128)(2,1)S(1)} collective-permute-done((bf16[1024,128]{1,0:T(8,128)(2,1)}, bf16[1024,128]{1,0:T(8,128)(2,1)S(1)}, u32[]{:S(2)}, u32[]{:S(2)}) %collective-permute-start.11) | collective-permute-done | bytes 262176 | tf_op jit(solution)/shard_map/ppermute | solution.py:156
  46.1 4.9 %collective-permute-done.10.refs_4_ = bf16[1024,128]{1,0:T(8,128)(2,1)S(1)} collective-permute-done((bf16[1024,128]{1,0:T(8,128)(2,1)}, bf16[1024,128]{1,0:T(8,128)(2,1)S(1)}, u32[]{:S(2)}, u32[]{:S(2)}) %collective-permute-start.10) | collective-permute-done | bytes 262176 | tf_op jit(solution)/shard_map/ppermute | solution.py:151
  54.1 9.1 %shard_map.119 = bf16[128,512]{1,0:T(8,128)(2,1)} custom-call(s32[64]{0:T(128)} %span_ref.1, s32[2]{0:T(128)} %pad_add_fusion.where_ref, bf16[128,512]{1,0:T(8,128)(2,1)} %q_ref.1, bf16[1024,128]{1,0:T(8,128)(2,1)} %get-tuple-element.7.refs_0_, bf16[1024,128]{1,0:T(8,128)(2,1)} %copy-done.16, bf16[1024,128]{1,0:T(8,128)(2,1)} %copy-done.17, ...), custom_call_target="tpu_custom_call" | custom-call | flops 1073741824 | bytes 2359296 | tf_op jit(solution)/shard_map/pallas_call | solution.py:96
  63.3 2.6 collective-permute-start.14
  66.1 4.5 %collective-permute-done.14 = bf16[128,512]{1,0:T(8,128)(2,1)S(1)} collective-permute-done((bf16[128,512]{1,0:T(8,128)(2,1)}, bf16[128,512]{1,0:T(8,128)(2,1)S(1)}, u32[]{:S(2)}, u32[]{:S(2)}) %collective-permute-start.14) | collective-permute-done | bytes 131104 | tf_op jit(solution)/shard_map/ppermute | solution.py:147
  72.3 3.1 collective-permute-start.22
  77.8 2.8 collective-permute-start.18
  81.8 2.9 collective-permute-start.21
  88.6 2.5 collective-permute-start.23
  91.3 3.2 %collective-permute-done.23 = f32[16,1024]{1,0:T(8,128)S(1)} collective-permute-done((f32[16,1024]{1,0:T(8,128)S(1)}, f32[16,1024]{1,0:T(8,128)S(1)}, u32[]{:S(2)}, u32[]{:S(2)}) %collective-permute-start.23) | collective-permute-done | bytes 65568 | tf_op jit(solution)/shard_map/ppermute | solution.py:147
  99.1 8.6 %all-to-all-start = ((bf16[256,2,1024]{2,1,0:T(2,128)(2,1)}), bf16[256,2,1024]{2,1,0:T(2,128)(2,1)S(1)}, u32[]{:S(2)}, u32[]{:S(2)}) async-start(bf16[256,2,1024]{2,1,0:T(2,128)(2,1)} %copy.83), calls=%async_computation | async-start | bytes 2097152 | tf_op jit(solution)/shard_map/all_to_all | solution.py:274
  107.7 3.7 %pad_maximum_fusion = bf16[16,64,2304]{2,1,0:T(8,128)(2,1)} fusion(bf16[16,64,768]{2,1,0:T(8,128)(2,1)S(1)} %copy-done, bf16[16,64,768]{2,1,0:T(8,128)(2,1)} %param.22, bf16[16,64,768]{2,1,0:T(8,128)(2,1)} %param.21), kind=kLoop, calls=%fused_computation | loop fusion | flops 14155776 | bytes 9437184 | tf_op jit(solution)/shard_map/concatenate | solution.py:200
  111.4 27.1 %all-to-all-done = bf16[256,2,1024]{2,1,0:T(2,128)(2,1)S(1)} async-done(((bf16[256,2,1024]{2,1,0:T(2,128)(2,1)}), bf16[256,2,1024]{2,1,0:T(2,128)(2,1)S(1)}, u32[]{:S(2)}, u32[]{:S(2)}) %all-to-all-start) | async-done | bytes 1048608 | tf_op jit(solution)/shard_map/all_to_all | solution.py:274
  138.5 5.4 %all-to-all-start.1 = ((bf16[16,64,2304]{2,1,0:T(8,128)(2,1)}), bf16[16,64,2304]{2,1,0:T(8,128)(2,1)}, u32[]{:S(2)}, u32[]{:S(2)}) async-start(bf16[16,64,2304]{2,1,0:T(8,128)(2,1)} %pad_maximum_fusion), calls=%async_computation.1 | async-start | bytes 9437184 | tf_op jit(solution)/shard_map/all_to_all | solution.py:199
  144.4 105.9 %all-to-all-done.1 = bf16[16,64,2304]{2,1,0:T(8,128)(2,1)} async-done(((bf16[16,64,2304]{2,1,0:T(8,128)(2,1)}), bf16[16,64,2304]{2,1,0:T(8,128)(2,1)}, u32[]{:S(2)}, u32[]{:S(2)}) %all-to-all-start.1) | async-done | bytes 4718624 | tf_op jit(solution)/shard_map/all_to_all | solution.py:199
  250.3 3.7 %fusion = f32[512,1536]{1,0:T(8,128)S(1)} fusion(bf16[512,1024]{1,0:T(8,128)(2,1)S(1)} %reshape.158, bf16[1024,2304]{1,0:T(8,128)(2,1)} %bitcast.24), kind=kOutput, calls=%fused_computation.1 | convolution fusion | flops 1610612736 | bytes 7340032 | tf_op jit(solution)/shard_map/dot_general | solution.py:276
  254.3 3.4 %collective-permute-done.24 = f32[256,1536]{1,0:T(8,128)S(1)} collective-permute-done((f32[256,1536]{1,0:T(8,128)S(1)}, f32[256,1536]{1,0:T(8,128)S(1)}, u32[]{:S(2)}, u32[]{:S(2)}) %collective-permute-start.24) | collective-permute-done | bytes 1572896 | tf_op jit(solution)/shard_map/ppermute | solution.py:29
  264.2 13.7 %all-to-all-start.2 = ((bf16[256,2,1024]{2,1,0:T(2,128)(2,1)}), bf16[256,2,1024]{2,1,0:T(2,128)(2,1)S(1)}, u32[]{:S(2)}, u32[]{:S(2)}) async-start(bf16[256,2,1024]{2,1,0:T(2,128)(2,1)} %reshape.160), calls=%async_computation.2 | async-start | bytes 2097152 | tf_op jit(solution)/shard_map/all_to_all | solution.py:291
  278.2 30.6 %all-to-all-done.2 = bf16[256,2,1024]{2,1,0:T(2,128)(2,1)S(1)} async-done(((bf16[256,2,1024]{2,1,0:T(2,128)(2,1)}), bf16[256,2,1024]{2,1,0:T(2,128)(2,1)S(1)}, u32[]{:S(2)}, u32[]{:S(2)}) %all-to-all-start.2) | async-done | bytes 1048608 | tf_op jit(solution)/shard_map/all_to_all | solution.py:291
  (132 shorter events, 44.4 us)
Async XLA Ops:
  1.6 13.0 %collective-permute-start.6 = (bf16[384,128]{1,0:T(8,128)(2,1)S(1)}, bf16[384,128]{1,0:T(8,128)(2,1)S(1)}, u32[]{:S(2)}, u32[]{:S(2)}) collective-permute-start(bf16[384,128]{1,0:T(8,128)(2,1)S(1)} %pad_maximum_fusion.3.refs_0_), channel_id=1, source_target_pairs={{112,0},{0,16},{16,32},{32,48},{48,64},{64,80},{80,96},{96,112},{1... | collective-permute-start | bytes 294920 | tf_op jit(solution)/shard_map/ppermute | solution.py:196
  3.6 13.4 %collective-permute-start.5 = (bf16[384,128]{1,0:T(8,128)(2,1)S(1)}, bf16[384,128]{1,0:T(8,128)(2,1)S(1)}, u32[]{:S(2)}, u32[]{:S(2)}) collective-permute-start(bf16[384,128]{1,0:T(8,128)(2,1)S(1)} %pad_maximum_fusion.3.refs_0_), channel_id=1, source_target_pairs={{96,0},{112,16},{0,32},{16,48},{32,64},{48,80},{64,96},{80,112},{9... | collective-permute-start | bytes 294920 | tf_op jit(solution)/shard_map/ppermute | solution.py:196
  8.1 16.7 %collective-permute-start.4 = (bf16[384,128]{1,0:T(8,128)(2,1)S(1)}, bf16[384,128]{1,0:T(8,128)(2,1)S(1)}, u32[]{:S(2)}, u32[]{:S(2)}) collective-permute-start(bf16[384,128]{1,0:T(8,128)(2,1)S(1)} %pad_maximum_fusion.3.refs_0_), channel_id=1, source_target_pairs={{80,0},{96,16},{112,32},{0,48},{16,64},{32,80},{48,96},{64,112},{8... | collective-permute-start | bytes 294920 | tf_op jit(solution)/shard_map/ppermute | solution.py:196
  10.1 14.7 %collective-permute-start.3 = (bf16[384,128]{1,0:T(8,128)(2,1)S(1)}, bf16[384,128]{1,0:T(8,128)(2,1)S(1)}, u32[]{:S(2)}, u32[]{:S(2)}) collective-permute-start(bf16[384,128]{1,0:T(8,128)(2,1)S(1)} %pad_maximum_fusion.3.refs_0_), channel_id=1, source_target_pairs={{64,0},{80,16},{96,32},{112,48},{0,64},{16,80},{32,96},{48,112},{6... | collective-permute-start | bytes 294920 | tf_op jit(solution)/shard_map/ppermute | solution.py:196
  11.5 13.9 %collective-permute-start.2 = (bf16[384,128]{1,0:T(8,128)(2,1)S(1)}, bf16[384,128]{1,0:T(8,128)(2,1)S(1)}, u32[]{:S(2)}, u32[]{:S(2)}) collective-permute-start(bf16[384,128]{1,0:T(8,128)(2,1)S(1)} %pad_maximum_fusion.3.refs_0_), channel_id=1, source_target_pairs={{48,0},{64,16},{80,32},{96,48},{112,64},{0,80},{16,96},{32,112},{4... | collective-permute-start | bytes 294920 | tf_op jit(solution)/shard_map/ppermute | solution.py:196
  14.6 15.8 %collective-permute-start.1 = (bf16[384,128]{1,0:T(8,128)(2,1)S(1)}, bf16[384,128]{1,0:T(8,128)(2,1)S(1)}, u32[]{:S(2)}, u32[]{:S(2)}) collective-permute-start(bf16[384,128]{1,0:T(8,128)(2,1)S(1)} %pad_maximum_fusion.3.refs_0_), channel_id=1, source_target_pairs={{32,0},{48,16},{64,32},{80,48},{96,64},{112,80},{0,96},{16,112},{3... | collective-permute-start | bytes 294920 | tf_op jit(solution)/shard_map/ppermute | solution.py:196
  17.0 14.5 %collective-permute-start = (bf16[384,128]{1,0:T(8,128)(2,1)S(1)}, bf16[384,128]{1,0:T(8,128)(2,1)S(1)}, u32[]{:S(2)}, u32[]{:S(2)}) collective-permute-start(bf16[384,128]{1,0:T(8,128)(2,1)S(1)} %pad_maximum_fusion.3.refs_0_), channel_id=1, source_target_pairs={{16,0},{32,16},{48,32},{64,48},{80,64},{96,80},{112,96},{0,112},{1... | collective-permute-start | bytes 294920 | tf_op jit(solution)/shard_map/ppermute | solution.py:196
  34.4 11.8 %collective-permute-start.11 = (bf16[1024,128]{1,0:T(8,128)(2,1)}, bf16[1024,128]{1,0:T(8,128)(2,1)S(1)}, u32[]{:S(2)}, u32[]{:S(2)}) collective-permute-start(bf16[1024,128]{1,0:T(8,128)(2,1)} %get-tuple-element.7.refs_0_), channel_id=1, source_target_pairs={{0,129},{1,128},{2,131},{3,130},{4,133},{5,132},{6,135},{7,134},{1... | collective-permute-start | bytes 786440 | tf_op jit(solution)/shard_map/ppermute | solution.py:156
  38.5 12.6 %collective-permute-start.10 = (bf16[1024,128]{1,0:T(8,128)(2,1)}, bf16[1024,128]{1,0:T(8,128)(2,1)S(1)}, u32[]{:S(2)}, u32[]{:S(2)}) collective-permute-start(bf16[1024,128]{1,0:T(8,128)(2,1)} %get-tuple-element.7.refs_0_), channel_id=1, source_target_pairs={{0,1},{1,0},{2,3},{3,2},{4,5},{5,4},{6,7},{7,6},{8,9},{9,8},{10,11... | collective-permute-start | bytes 786440 | tf_op jit(solution)/shard_map/ppermute | solution.py:151
  39.0 12.1 %collective-permute-start.7 = (bf16[1024,128]{1,0:T(8,128)(2,1)}, bf16[1024,128]{1,0:T(8,128)(2,1)S(1)}, u32[]{:S(2)}, u32[]{:S(2)}) collective-permute-start(bf16[1024,128]{1,0:T(8,128)(2,1)} %get-tuple-element.7.refs_0_), channel_id=1, source_target_pairs={{0,128},{128,0},{1,129},{129,1},{2,130},{130,2},{3,131},{131,3},{4... | collective-permute-start | bytes 786440 | tf_op jit(solution)/shard_map/ppermute | solution.py:147
  39.3 13.2 %collective-permute-start.8 = (bf16[1024,128]{1,0:T(8,128)(2,1)}, bf16[1024,128]{1,0:T(8,128)(2,1)S(1)}, u32[]{:S(2)}, u32[]{:S(2)}) collective-permute-start(bf16[1024,128]{1,0:T(8,128)(2,1)} %get-tuple-element.7.refs_0_), channel_id=1, source_target_pairs={{0,8},{8,0},{1,9},{9,1},{2,10},{10,2},{3,11},{11,3},{4,12},{12,4},... | collective-permute-start | bytes 786440 | tf_op jit(solution)/shard_map/ppermute | solution.py:29
  46.1 6.4 %collective-permute-start.13 = (bf16[1024,128]{1,0:T(8,128)(2,1)S(1)}, bf16[1024,128]{1,0:T(8,128)(2,1)S(1)}, u32[]{:S(2)}, u32[]{:S(2)}) collective-permute-start(bf16[1024,128]{1,0:T(8,128)(2,1)S(1)} %collective-permute-done.11.refs_5_), channel_id=1, source_target_pairs={{0,8},{8,0},{1,9},{9,1},{2,10},{10,2},{3,11},{11,3},{4,12},{12,4},... | collective-permute-start | bytes 786440 | tf_op jit(solution)/shard_map/ppermute | solution.py:29
  51.6 20.0 %collective-permute-start.15 = (bf16[512,512]{1,0:T(8,128)(2,1)}, bf16[512,512]{1,0:T(8,128)(2,1)S(1)}, u32[]{:S(2)}, u32[]{:S(2)}) collective-permute-start(bf16[512,512]{1,0:T(8,128)(2,1)} %get-tuple-element.8), channel_id=1, source_target_pairs={{0,8},{8,0},{1,9},{9,1},{2,10},{10,2},{3,11},{11,3},{4,12},{12,4},... | collective-permute-start | bytes 1572872 | tf_op jit(solution)/shard_map/ppermute | solution.py:29
  63.3 7.4 %collective-permute-start.14 = (bf16[128,512]{1,0:T(8,128)(2,1)}, bf16[128,512]{1,0:T(8,128)(2,1)S(1)}, u32[]{:S(2)}, u32[]{:S(2)}) collective-permute-start(bf16[128,512]{1,0:T(8,128)(2,1)} %shard_map.119), channel_id=1, source_target_pairs={{0,128},{128,0},{1,129},{129,1},{2,130},{130,2},{3,131},{131,3},{4... | collective-permute-start | bytes 393224 | tf_op jit(solution)/shard_map/ppermute | solution.py:147
  72.3 9.5 %collective-permute-start.22 = (bf16[32,1024]{1,0:T(8,128)(2,1)S(1)}, bf16[32,1024]{1,0:T(8,128)(2,1)S(1)}, u32[]{:S(2)}, u32[]{:S(2)}) collective-permute-start(bf16[32,1024]{1,0:T(8,128)(2,1)S(1)} %fusion.37), channel_id=1, source_target_pairs={{0,7},{1,6},{2,5},{3,4},{4,3},{5,2},{6,1},{7,0},{8,15},{9,14},{10,... | collective-permute-start | bytes 196616 | tf_op jit(solution)/shard_map/ppermute | solution.py:234
  75.4 6.4 %collective-permute-start.16 = (bf16[32,1024]{1,0:T(8,128)(2,1)S(1)}, bf16[32,1024]{1,0:T(8,128)(2,1)S(1)}, u32[]{:S(2)}, u32[]{:S(2)}) collective-permute-start(bf16[32,1024]{1,0:T(8,128)(2,1)S(1)} %get-tuple-element.11), channel_id=1, source_target_pairs={{0,1},{1,0},{2,3},{3,2},{4,5},{5,4},{6,7},{7,6},{8,9},{9,8},{10,11... | collective-permute-start | bytes 196616 | tf_op jit(solution)/shard_map/ppermute | solution.py:234
  76.0 9.3 %collective-permute-start.17 = (bf16[32,1024]{1,0:T(8,128)(2,1)S(1)}, bf16[32,1024]{1,0:T(8,128)(2,1)S(1)}, u32[]{:S(2)}, u32[]{:S(2)}) collective-permute-start(bf16[32,1024]{1,0:T(8,128)(2,1)S(1)} %get-tuple-element.12), channel_id=1, source_target_pairs={{0,2},{1,3},{2,0},{3,1},{4,6},{5,7},{6,4},{7,5},{8,10},{9,11},{10,... | collective-permute-start | bytes 196616 | tf_op jit(solution)/shard_map/ppermute | solution.py:234
  77.8 7.5 %collective-permute-start.18 = (bf16[32,1024]{1,0:T(8,128)(2,1)S(1)}, bf16[32,1024]{1,0:T(8,128)(2,1)S(1)}, u32[]{:S(2)}, u32[]{:S(2)}) collective-permute-start(bf16[32,1024]{1,0:T(8,128)(2,1)S(1)} %get-tuple-element.13), channel_id=1, source_target_pairs={{0,3},{1,2},{2,1},{3,0},{4,7},{5,6},{6,5},{7,4},{8,11},{9,10},{10,... | collective-permute-start | bytes 196616 | tf_op jit(solution)/shard_map/ppermute | solution.py:234
  81.8 5.2 %collective-permute-start.20 = (bf16[32,1024]{1,0:T(8,128)(2,1)S(1)}, bf16[32,1024]{1,0:T(8,128)(2,1)S(1)}, u32[]{:S(2)}, u32[]{:S(2)}) collective-permute-start(bf16[32,1024]{1,0:T(8,128)(2,1)S(1)} %get-tuple-element.15), channel_id=1, source_target_pairs={{0,5},{1,4},{2,7},{3,6},{4,1},{5,0},{6,3},{7,2},{8,13},{9,12},{10,... | collective-permute-start | bytes 196616 | tf_op jit(solution)/shard_map/ppermute | solution.py:234
  81.8 6.8 %collective-permute-start.21 = (bf16[32,1024]{1,0:T(8,128)(2,1)S(1)}, bf16[32,1024]{1,0:T(8,128)(2,1)S(1)}, u32[]{:S(2)}, u32[]{:S(2)}) collective-permute-start(bf16[32,1024]{1,0:T(8,128)(2,1)S(1)} %get-tuple-element.16), channel_id=1, source_target_pairs={{0,6},{1,7},{2,4},{3,5},{4,2},{5,3},{6,0},{7,1},{8,14},{9,15},{10,... | collective-permute-start | bytes 196616 | tf_op jit(solution)/shard_map/ppermute | solution.py:234
  88.6 5.9 %collective-permute-start.23 = (f32[16,1024]{1,0:T(8,128)S(1)}, f32[16,1024]{1,0:T(8,128)S(1)}, u32[]{:S(2)}, u32[]{:S(2)}) collective-permute-start(f32[16,1024]{1,0:T(8,128)S(1)} %slice.38), channel_id=1, source_target_pairs={{0,128},{128,0},{1,129},{129,1},{2,130},{130,2},{3,131},{131,3},{4... | collective-permute-start | bytes 196616 | tf_op jit(solution)/shard_map/ppermute | solution.py:147
  99.1 39.4 %all-to-all-start = ((bf16[256,2,1024]{2,1,0:T(2,128)(2,1)}), bf16[256,2,1024]{2,1,0:T(2,128)(2,1)S(1)}, u32[]{:S(2)}, u32[]{:S(2)}) async-start(bf16[256,2,1024]{2,1,0:T(2,128)(2,1)} %copy.83), calls=%async_computation | async-start | bytes 2097152 | tf_op jit(solution)/shard_map/all_to_all | solution.py:274
  138.5 111.8 %all-to-all-start.1 = ((bf16[16,64,2304]{2,1,0:T(8,128)(2,1)}), bf16[16,64,2304]{2,1,0:T(8,128)(2,1)}, u32[]{:S(2)}, u32[]{:S(2)}) async-start(bf16[16,64,2304]{2,1,0:T(8,128)(2,1)} %pad_maximum_fusion), calls=%async_computation.1 | async-start | bytes 9437184 | tf_op jit(solution)/shard_map/all_to_all | solution.py:199
  264.2 44.5 %all-to-all-start.2 = ((bf16[256,2,1024]{2,1,0:T(2,128)(2,1)}), bf16[256,2,1024]{2,1,0:T(2,128)(2,1)S(1)}, u32[]{:S(2)}, u32[]{:S(2)}) async-start(bf16[256,2,1024]{2,1,0:T(2,128)(2,1)} %reshape.160), calls=%async_computation.2 | async-start | bytes 2097152 | tf_op jit(solution)/shard_map/all_to_all | solution.py:291
  (26 other events, 179.9 us)

commit v4 on v3

--- a/solution.py
+++ b/solution.py
@@ -143,6 +143,36 @@
     )(z[None].astype(jnp.int32), *parts)
 
 
+def project_kernel(ctx_ref, x_ref, *refs):
+    weights, o_ref = refs[:4], refs[4]
+    yh, core = ctx_ref[0] // 16, lax.rem(ctx_ref[0], 2)
+    x = x_ref[...]
+    for side, w in enumerate(weights):
+        half = yh if side % 2 == 0 else 1 - yh
+        plane = core if side < 2 else 1 - core
+        out = lax.dot_general(
+            x, w[...], (((1,), (1,)), ((), ())), preferred_element_type=jnp.float32
+        )
+        at = pl.multiple_of((2 * plane + half) * 512, 512)
+        o_ref[:, pl.ds(at, 512)] = out.astype(o_ref.dtype)
+
+
+def project(ctx, x, weights):
+    return pl.pallas_call(
+        project_kernel,
+        out_shape=jax.ShapeDtypeStruct((x.shape[0], D), jnp.bfloat16),
+        grid_spec=pltpu.PrefetchScalarGridSpec(
+            num_scalar_prefetch=1,
+            grid=(1,),
+            in_specs=[pl.BlockSpec(a.shape, lambda i, *_: (0, 0)) for a in [x, *weights]],
+            out_specs=pl.BlockSpec((x.shape[0], D), lambda i, *_: (0, 0)),
+        ),
+        cost_estimate=pl.CostEstimate(
+            flops=2 * x.shape[0] * x.shape[1] * D, bytes_accessed=2752512, transcendentals=0
+        ),
+    )(ctx[None].astype(jnp.int32), x, *weights)
+
+
 def across_y(x):
     return lax.ppermute(x, "yh", SWAP)
 
@@ -183,7 +213,6 @@
     core = lax.axis_index("core")
     ctx = lax.axis_index(CTX)
     exp = lax.axis_index("exp")
-    yh = lax.axis_index("yh")
 
     head = exp // 2 * HD
     mine = jnp.where(
@@ -199,12 +228,12 @@
     weights = lax.all_to_all(
         jnp.concatenate([w_gate, w_up, w_down], axis=2), CHIP, 0, 0, tiled=True
     ).reshape(HALF, -1)
-    gate_up_w, down_w = weights[:, : 2 * FF], weights[:, 2 * FF :]
 
     piece, wo_near = assembled(lax.axis_index("z"), parts)
     near = [piece, across_y(piece), across_x(piece), across_xy(piece)]
+    wo_near = [wo_near, across_y(wo_near)]
     far = [swapped(p) for p in near]
-    wo_far = swapped(wo_near)
+    wo_far = [swapped(w) for w in wo_near]
 
     attended = attend(
         span_order,
@@ -213,30 +242,12 @@
         near[0:2] + far[0:2],
         near[2:4] + far[2:4],
     )
-    partner = across_y(attended)
-    rows = jnp.stack(
-        [attended.reshape(8, -1, 4 * HD), partner.reshape(8, -1, 4 * HD)], axis=1
-    ).reshape(-1, 4 * HD)
-
-    def projected(w):
-        return lax.dot_general(
-            rows, w, (((1,), (1,)), ((), ())), preferred_element_type=jnp.float32
-        )
-
-    a, b = projected(wo_near), projected(wo_far)
-    mixed = jnp.concatenate(
-        [jnp.where(core == 0, a, b), jnp.where(core == 0, b, a)], axis=1
-    ).astype(jnp.bfloat16)
-    mixed = mixed.reshape(8, 32, HALF)
+    mixed = project(ctx, attended, wo_near + wo_far).reshape(8, 16, D)
     summed = lax.dynamic_index_in_dim(mixed, exp, 0, False).astype(jnp.float32)
     for d in range(1, 8):
         sent = lax.dynamic_index_in_dim(mixed, exp ^ d, 0, False)
         got = lax.ppermute(sent, "exp", [(e, e ^ d) for e in range(8)])
         summed = summed + got.astype(jnp.float32)
-    got = across_y(summed[16:])
-    low = jnp.where(yh == 0, summed[:16], got).reshape(16, 2, 1, -1)
-    high = jnp.where(yh == 0, got, summed[:16]).reshape(16, 2, 1, -1)
-    summed = jnp.concatenate([low, high], axis=2).reshape(16, D)
     resid = by_plane(stream_in.astype(jnp.float32)) + summed
     gain = by_plane(norm_gain.astype(jnp.float32)[None])
     normed = (
@@ -273,21 +284,29 @@
     )
     tokens = lax.all_to_all(outgoing, ALL, 0, 0, tiled=True).reshape(512, HALF)
 
-    gu = jnp.dot(tokens, gate_up_w, preferred_element_type=jnp.float32)
-    gu = gu.reshape(2, 256, -1)
-    keep = jnp.where(core == 0, gu[0], gu[1])
-    send = jnp.where(core == 0, gu[1], gu[0])
-    both = keep + swapped(send)
-    width = both.shape[1] // 2
-    act = (jax.nn.silu(both[:, :width]) * both[:, width:]).astype(jnp.bfloat16)
+    half = FF // 2
+
+    def columns(first, at):
+        return lax.dynamic_slice_in_dim(weights, first + at * half, half, 1)
+
+    def gate_up(at):
+        return jnp.concatenate([columns(0, at), columns(FF, at)], axis=1)
+
+    own_w = gate_up(core)
+    other_w = swapped(gate_up(1 - core))
+    own_down = columns(2 * FF, core)
+    other_down = columns(2 * FF, 1 - core)
+    tokens_other = swapped(tokens)
+    hidden = jnp.dot(tokens, own_w, preferred_element_type=jnp.float32)
+    hidden, tokens_other = lax.optimization_barrier((hidden, tokens_other))
+    hidden = hidden + jnp.dot(tokens_other, other_w, preferred_element_type=jnp.float32)
+    act = (jax.nn.silu(hidden[:, :half]) * hidden[:, half:]).astype(jnp.bfloat16)
+    dims = (((1,), (1,)), ((), ()))
     act_other = swapped(act)
-    act = jnp.concatenate(
-        [jnp.where(core == 0, act, act_other), jnp.where(core == 0, act_other, act)],
-        axis=0,
-    )
-    out = lax.dot_general(
-        act, down_w, (((1,), (1,)), ((), ())), preferred_element_type=jnp.float32
-    ).astype(jnp.bfloat16)
+    out = lax.dot_general(act, own_down, dims, preferred_element_type=jnp.float32)
+    out, act_other = lax.optimization_barrier((out, act_other))
+    out = out + lax.dot_general(act_other, other_down, dims, preferred_element_type=jnp.float32)
+    out = out.astype(jnp.bfloat16)
     home = lax.all_to_all(out.reshape(256, CAP, HALF), ALL, 0, 0, tiled=True)
     home = home.reshape(OWN, 2, 8, CAP, HALF).transpose(0, 2, 3, 1, 4).reshape(EXPERTS * CAP, D)
     moe = jnp.dot(combine, home, preferred_element_type=jnp.float32)

time: 313 us -> 306 us (0.978)
  starting transfers between devices: 68.7 us -> 57.7 us
  local copies, waits for them, and re-layouts: 10.8 us -> 16.8 us
  waiting for transfers between devices: 204 us -> 198 us
  Pallas kernels: 11.3 us -> 14.5 us
    all_to_all x1, waiting for transfers between devices: 106 us -> 0.01 us  [shards(): lax.all_to_all(jnp.concatenate([w_gate, w_up, w_down], axis=2), CHIP, 0,...]
    ppermute x7, waiting for transfers between devices: 12.3 us -> 114 us  [shards(): lax.ppermute(packed, 'z', [((i + r) % 8, i) for i in range(8)])]
    ppermute x3 -> x2, waiting for transfers between devices: 7.73 us -> 19.6 us  [across_y(): return lax.ppermute(x, 'yh', SWAP)]
    all_to_all x1, starting transfers between devices: 13.7 us -> 6.41 us  [shards(): home = lax.all_to_all(out.reshape(256, CAP, HALF), ALL, 0, 0, tiled=True)]
    ppermute x1, waiting for transfers between devices: 6.79 us -> 0.01 us  [across_xy(): return lax.ppermute(x, ('yh', 'exp'), pairs)]
    all_to_all x1, starting transfers between devices: 5.44 us -> 11.3 us  [shards(): lax.all_to_all(jnp.concatenate([w_gate, w_up, w_down], axis=2), CHIP, 0,...]
    ppermute x1, waiting for transfers between devices: 4.93 us -> 0.01 us  [across_x(): return lax.ppermute(x, 'exp', [(e, e ^ 1) for e in range(8)])]
    ppermute x7, starting transfers between devices: 17.6 us -> 13.2 us  [shards(): lax.ppermute(packed, 'z', [((i + r) % 8, i) for i in range(8)])]
  transfers between devices with their start and end apart: 29 -> 30, of which waited for: 17 -> 12; matrix products, arithmetic and copies ran while one was open for 2% -> 6% of each run, Pallas kernels for 3% -> 5%
where the time goes in v4:
time: 306 us; the launch traced here: 304 us
  waiting for transfers between devices  198 us (65%)
  starting transfers between devices  57.7 us (19%)
  local copies, waits for them, and re-layouts  16.8 us (5%)
  Pallas kernels  14.5 us (5%)
  matrix products  9.47 us (3%)
  other arithmetic  7.75 us (3%)
    ppermute x7, waiting for transfers between devices, shards(): lax.ppermute(packed, 'z', [((i + r) % 8, i) for i in range(8)])  114 us
    all_to_all x1, waiting for transfers between devices, shards(): home = lax.all_to_all(out.reshape(256, CAP, HALF), ALL, 0, 0, tiled=True)  30.6 us
    all_to_all x1, waiting for transfers between devices, shards(): tokens = lax.all_to_all(outgoing, ALL, 0, 0, tiled=True).reshape(512, HALF)  27.1 us
    ppermute x2, waiting for transfers between devices, across_y(): return lax.ppermute(x, 'yh', SWAP)  19.6 us
    ppermute x7, starting transfers between devices, shards(): lax.ppermute(packed, 'z', [((i + r) % 8, i) for i in range(8)])  13.2 us
    all_to_all x1, starting transfers between devices, shards(): lax.all_to_all(jnp.concatenate([w_gate, w_up, w_down], axis=2), CHIP, 0,...  11.3 us
    ppermute x7, starting transfers between devices, shards(): got = lax.ppermute(sent, 'exp', [(e, e ^ d) for e in range(8)])  11 us
    pallas_call x1, Pallas kernels, attend(): pl.pallas_call(attend_kernel, out_shape=jax.ShapeDtypeStruct((rows, width...  9.14 us
  transfers between devices with their start and end apart: 30, of which 12 were waited for; matrix products, arithmetic and copies ran while one was open for 6% of the time, Pallas kernels for 5%

profile of v4, /device:TPU:32, one launch (start us, length us, event | category | flops | bytes accessed | tf_op | source)
XLA Modules:
  0.0 304.3 jit_solution(10096378143647902911)
XLA Ops:
  0.0 3.9 %pad_maximum_fusion = bf16[16,64,2304]{2,1,0:T(8,128)(2,1)} fusion(bf16[16,64,768]{2,1,0:T(8,128)(2,1)} %param.23, bf16[16,64,768]{2,1,0:T(8,128)(2,1)} %param.22, bf16[16,64,768]{2,1,0:T(8,128)(2,1)} %param.21), kind=kLoop, calls=%fused_computation | loop fusion | flops 14155776 | bytes 9437184 | tf_op jit(solution)/shard_map/concatenate | solution.py:229
  3.9 11.3 %all-to-all-start.1 = ((bf16[16,64,2304]{2,1,0:T(8,128)(2,1)}), bf16[16,64,2304]{2,1,0:T(8,128)(2,1)}, u32[]{:S(2)}, u32[]{:S(2)}) async-start(bf16[16,64,2304]{2,1,0:T(8,128)(2,1)} %pad_maximum_fusion), calls=%async_computation.1 | async-start | bytes 9437184 | tf_op jit(solution)/shard_map/all_to_all | solution.py:228
  16.4 4.0 %collective-permute-start.1 = (bf16[384,128]{1,0:T(8,128)(2,1)S(1)}, bf16[384,128]{1,0:T(8,128)(2,1)S(1)}, u32[]{:S(2)}, u32[]{:S(2)}) collective-permute-start(bf16[384,128]{1,0:T(8,128)(2,1)S(1)} %pad_maximum_fusion.2.refs_0_), channel_id=1, source_target_pairs={{32,0},{48,16},{64,32},{80,48},{96,64},{112,80},{0,96},{16,112},{3... | collective-permute-start | bytes 294920 | tf_op jit(solution)/shard_map/ppermute | solution.py:225
  20.3 2.4 collective-permute-start.2
  22.7 2.7 collective-permute-start.3
  25.4 2.4 collective-permute-start.4
  27.7 105.3 %collective-permute-done.refs_1_ = bf16[384,128]{1,0:T(8,128)(2,1)S(1)} collective-permute-done((bf16[384,128]{1,0:T(8,128)(2,1)S(1)}, bf16[384,128]{1,0:T(8,128)(2,1)S(1)}, u32[]{:S(2)}, u32[]{:S(2)}) %collective-permute-start) | collective-permute-done | bytes 98336 | tf_op jit(solution)/shard_map/ppermute | solution.py:225
  134.7 9.1 %collective-permute-done.3.refs_4_ = bf16[384,128]{1,0:T(8,128)(2,1)S(1)} collective-permute-done((bf16[384,128]{1,0:T(8,128)(2,1)S(1)}, bf16[384,128]{1,0:T(8,128)(2,1)S(1)}, u32[]{:S(2)}, u32[]{:S(2)}) %collective-permute-start.3) | collective-permute-done | bytes 98336 | tf_op jit(solution)/shard_map/ppermute | solution.py:225
  144.5 2.2 shard_map.118
  146.7 1.9 collective-permute-start.14
  153.7 19.6 %collective-permute-done.7.refs_1_ = bf16[1024,128]{1,0:T(8,128)(2,1)S(1)} collective-permute-done((bf16[1024,128]{1,0:T(8,128)(2,1)}, bf16[1024,128]{1,0:T(8,128)(2,1)S(1)}, u32[]{:S(2)}, u32[]{:S(2)}) %collective-permute-start.7) | collective-permute-done | bytes 262176 | tf_op jit(solution)/shard_map/ppermute | solution.py:177
  178.3 9.1 %shard_map.119.x_ref = bf16[128,512]{1,0:T(8,128)(2,1)} custom-call(s32[64]{0:T(128)} %span_ref.1, s32[2]{0:T(128)} %pad_add_fusion.where_ref, bf16[128,512]{1,0:T(8,128)(2,1)} %q_ref.1, bf16[1024,128]{1,0:T(8,128)(2,1)} %get-tuple-element.11.refs_0_, bf16[1024,128]{1,0:T(8,128)(2,1)} %copy-done.16, bf16[1024,128]{1,0:T(8,128)(2,1)} %copy-done.17, ...), custom_call_target="tpu_custom_call" | custom-call | flops 1073741824 | bytes 2359296 | tf_op jit(solution)/shard_map/pallas_call | solution.py:96
  189.1 3.2 %shard_map.120 = bf16[128,2048]{1,0:T(8,128)(2,1)} custom-call(s32[1]{0:T(128)} %bitcast.1.ctx_ref, bf16[128,512]{1,0:T(8,128)(2,1)} %shard_map.119.x_ref, bf16[512,512]{1,0:T(8,128)(2,1)} %get-tuple-element.12.refs_0_, bf16[512,512]{1,0:T(8,128)(2,1)} %copy-done, bf16[512,512]{1,0:T(8,128)(2,1)} %copy-done.1, bf16[512,512]{1,0:T(8,128)(2,1)} %copy-done.2), custom_call_target="tpu_custom_call" | custom-call | flops 268435456 | bytes 2752512 | tf_op jit(solution)/shard_map/pallas_call | solution.py:161
  193.3 3.0 collective-permute-start.23
  200.5 2.8 collective-permute-start.19
  205.9 3.1 %collective-permute-done.18 = bf16[16,2048]{1,0:T(8,128)(2,1)S(1)} collective-permute-done((bf16[16,2048]{1,0:T(8,128)(2,1)S(1)}, bf16[16,2048]{1,0:T(8,128)(2,1)S(1)}, u32[]{:S(2)}, u32[]{:S(2)}) %collective-permute-start.18) | collective-permute-done | bytes 65568 | tf_op jit(solution)/shard_map/ppermute | solution.py:249
  211.7 2.0 copy.65
  213.7 6.9 %all-to-all-start = ((bf16[256,2,1024]{2,1,0:T(2,128)(2,1)}), bf16[256,2,1024]{2,1,0:T(2,128)(2,1)S(1)}, u32[]{:S(2)}, u32[]{:S(2)}) async-start(bf16[256,2,1024]{2,1,0:T(2,128)(2,1)} %copy.65), calls=%async_computation | async-start | bytes 2097152 | tf_op jit(solution)/shard_map/all_to_all | solution.py:285
  220.6 3.1 %constant_dynamic-slice_fusion.1 = (bf16[1024,384]{1,0:T(8,128)(2,1)S(1)}, bf16[1024,384]{1,0:T(8,128)(2,1)S(1)}, bf16[1024,384]{1,0:T(8,128)(2,1)S(1)}, bf16[1024,384]{1,0:T(8,128)(2,1)}) fusion(bf16[1024,2304]{1,0:T(8,128)(2,1)} %bitcast.18, s32[]{:T(128)S(6)} %select_n.109, s32[]{:T(128)S(6)} %select_n.110, s32[]{:T(128)S(6)} %select_n.108, s32[]{:T(128)S(6)} %select_n.107), kind=kLoop, calls=%fused_computation.64 | loop fusion | bytes 6291472 | tf_op jit(solution)/shard_map/dynamic_slice | solution.py:290
  224.3 27.1 %all-to-all-done = bf16[256,2,1024]{2,1,0:T(2,128)(2,1)S(1)} async-done(((bf16[256,2,1024]{2,1,0:T(2,128)(2,1)}), bf16[256,2,1024]{2,1,0:T(2,128)(2,1)S(1)}, u32[]{:S(2)}, u32[]{:S(2)}) %all-to-all-start) | async-done | bytes 1048608 | tf_op jit(solution)/shard_map/all_to_all | solution.py:285
  252.6 2.4 fusion
  255.5 2.4 fusion.35
  264.1 6.4 %all-to-all-start.2 = ((bf16[256,2,1024]{2,1,0:T(2,128)(2,1)}), bf16[256,2,1024]{2,1,0:T(2,128)(2,1)S(1)}, u32[]{:S(2)}, u32[]{:S(2)}) async-start(bf16[256,2,1024]{2,1,0:T(2,128)(2,1)} %reshape.138), calls=%async_computation.2 | async-start | bytes 2097152 | tf_op jit(solution)/shard_map/all_to_all | solution.py:310
  270.7 30.6 %all-to-all-done.2 = bf16[256,2,1024]{2,1,0:T(2,128)(2,1)S(1)} async-done(((bf16[256,2,1024]{2,1,0:T(2,128)(2,1)}), bf16[256,2,1024]{2,1,0:T(2,128)(2,1)S(1)}, u32[]{:S(2)}, u32[]{:S(2)}) %all-to-all-start.2) | async-done | bytes 1048608 | tf_op jit(solution)/shard_map/all_to_all | solution.py:310
  (129 shorter events, 37.2 us)
Async XLA Ops:
  3.9 209.8 %all-to-all-start.1 = ((bf16[16,64,2304]{2,1,0:T(8,128)(2,1)}), bf16[16,64,2304]{2,1,0:T(8,128)(2,1)}, u32[]{:S(2)}, u32[]{:S(2)}) async-start(bf16[16,64,2304]{2,1,0:T(8,128)(2,1)} %pad_maximum_fusion), calls=%async_computation.1 | async-start | bytes 9437184 | tf_op jit(solution)/shard_map/all_to_all | solution.py:228
  16.1 116.9 %collective-permute-start = (bf16[384,128]{1,0:T(8,128)(2,1)S(1)}, bf16[384,128]{1,0:T(8,128)(2,1)S(1)}, u32[]{:S(2)}, u32[]{:S(2)}) collective-permute-start(bf16[384,128]{1,0:T(8,128)(2,1)S(1)} %pad_maximum_fusion.2.refs_0_), channel_id=1, source_target_pairs={{16,0},{32,16},{48,32},{64,48},{80,64},{96,80},{112,96},{0,112},{1... | collective-permute-start | bytes 294920 | tf_op jit(solution)/shard_map/ppermute | solution.py:225
  16.4 116.6 %collective-permute-start.1 = (bf16[384,128]{1,0:T(8,128)(2,1)S(1)}, bf16[384,128]{1,0:T(8,128)(2,1)S(1)}, u32[]{:S(2)}, u32[]{:S(2)}) collective-permute-start(bf16[384,128]{1,0:T(8,128)(2,1)S(1)} %pad_maximum_fusion.2.refs_0_), channel_id=1, source_target_pairs={{32,0},{48,16},{64,32},{80,48},{96,64},{112,80},{0,96},{16,112},{3... | collective-permute-start | bytes 294920 | tf_op jit(solution)/shard_map/ppermute | solution.py:225
  20.3 114.3 %collective-permute-start.2 = (bf16[384,128]{1,0:T(8,128)(2,1)S(1)}, bf16[384,128]{1,0:T(8,128)(2,1)S(1)}, u32[]{:S(2)}, u32[]{:S(2)}) collective-permute-start(bf16[384,128]{1,0:T(8,128)(2,1)S(1)} %pad_maximum_fusion.2.refs_0_), channel_id=1, source_target_pairs={{48,0},{64,16},{80,32},{96,48},{112,64},{0,80},{16,96},{32,112},{4... | collective-permute-start | bytes 294920 | tf_op jit(solution)/shard_map/ppermute | solution.py:225
  22.7 121.0 %collective-permute-start.3 = (bf16[384,128]{1,0:T(8,128)(2,1)S(1)}, bf16[384,128]{1,0:T(8,128)(2,1)S(1)}, u32[]{:S(2)}, u32[]{:S(2)}) collective-permute-start(bf16[384,128]{1,0:T(8,128)(2,1)S(1)} %pad_maximum_fusion.2.refs_0_), channel_id=1, source_target_pairs={{64,0},{80,16},{96,32},{112,48},{0,64},{16,80},{32,96},{48,112},{6... | collective-permute-start | bytes 294920 | tf_op jit(solution)/shard_map/ppermute | solution.py:225
  25.4 118.4 %collective-permute-start.4 = (bf16[384,128]{1,0:T(8,128)(2,1)S(1)}, bf16[384,128]{1,0:T(8,128)(2,1)S(1)}, u32[]{:S(2)}, u32[]{:S(2)}) collective-permute-start(bf16[384,128]{1,0:T(8,128)(2,1)S(1)} %pad_maximum_fusion.2.refs_0_), channel_id=1, source_target_pairs={{80,0},{96,16},{112,32},{0,48},{16,64},{32,80},{48,96},{64,112},{8... | collective-permute-start | bytes 294920 | tf_op jit(solution)/shard_map/ppermute | solution.py:225
  133.0 10.7 %collective-permute-start.5 = (bf16[384,128]{1,0:T(8,128)(2,1)S(1)}, bf16[384,128]{1,0:T(8,128)(2,1)S(1)}, u32[]{:S(2)}, u32[]{:S(2)}) collective-permute-start(bf16[384,128]{1,0:T(8,128)(2,1)S(1)} %pad_maximum_fusion.2.refs_0_), channel_id=1, source_target_pairs={{96,0},{112,16},{0,32},{16,48},{32,64},{48,80},{64,96},{80,112},{9... | collective-permute-start | bytes 294920 | tf_op jit(solution)/shard_map/ppermute | solution.py:225
  133.0 10.7 %collective-permute-start.6 = (bf16[384,128]{1,0:T(8,128)(2,1)S(1)}, bf16[384,128]{1,0:T(8,128)(2,1)S(1)}, u32[]{:S(2)}, u32[]{:S(2)}) collective-permute-start(bf16[384,128]{1,0:T(8,128)(2,1)S(1)} %pad_maximum_fusion.2.refs_0_), channel_id=1, source_target_pairs={{112,0},{0,16},{16,32},{32,48},{48,64},{64,80},{80,96},{96,112},{1... | collective-permute-start | bytes 294920 | tf_op jit(solution)/shard_map/ppermute | solution.py:225
  146.7 26.6 %collective-permute-start.14 = (bf16[512,512]{1,0:T(8,128)(2,1)}, bf16[512,512]{1,0:T(8,128)(2,1)S(1)}, u32[]{:S(2)}, u32[]{:S(2)}) collective-permute-start(bf16[512,512]{1,0:T(8,128)(2,1)} %get-tuple-element.12.refs_0_), channel_id=1, source_target_pairs={{0,128},{128,0},{1,129},{129,1},{2,130},{130,2},{3,131},{131,3},{4... | collective-permute-start | bytes 1572872 | tf_op jit(solution)/shard_map/ppermute | solution.py:177
  148.7 24.6 %collective-permute-start.7 = (bf16[1024,128]{1,0:T(8,128)(2,1)}, bf16[1024,128]{1,0:T(8,128)(2,1)S(1)}, u32[]{:S(2)}, u32[]{:S(2)}) collective-permute-start(bf16[1024,128]{1,0:T(8,128)(2,1)} %get-tuple-element.11.refs_0_), channel_id=1, source_target_pairs={{0,128},{128,0},{1,129},{129,1},{2,130},{130,2},{3,131},{131,3},{4... | collective-permute-start | bytes 786440 | tf_op jit(solution)/shard_map/ppermute | solution.py:177
  150.3 23.5 %collective-permute-start.8 = (bf16[1024,128]{1,0:T(8,128)(2,1)}, bf16[1024,128]{1,0:T(8,128)(2,1)S(1)}, u32[]{:S(2)}, u32[]{:S(2)}) collective-permute-start(bf16[1024,128]{1,0:T(8,128)(2,1)} %get-tuple-element.11.refs_0_), channel_id=1, source_target_pairs={{0,8},{8,0},{1,9},{9,1},{2,10},{10,2},{3,11},{11,3},{4,12},{12,4},... | collective-permute-start | bytes 786440 | tf_op jit(solution)/shard_map/ppermute | solution.py:29
  150.3 23.6 %collective-permute-start.10 = (bf16[1024,128]{1,0:T(8,128)(2,1)}, bf16[1024,128]{1,0:T(8,128)(2,1)S(1)}, u32[]{:S(2)}, u32[]{:S(2)}) collective-permute-start(bf16[1024,128]{1,0:T(8,128)(2,1)} %get-tuple-element.11.refs_0_), channel_id=1, source_target_pairs={{0,1},{1,0},{2,3},{3,2},{4,5},{5,4},{6,7},{7,6},{8,9},{9,8},{10,11... | collective-permute-start | bytes 786440 | tf_op jit(solution)/shard_map/ppermute | solution.py:181
  151.8 22.6 %collective-permute-start.11 = (bf16[1024,128]{1,0:T(8,128)(2,1)}, bf16[1024,128]{1,0:T(8,128)(2,1)S(1)}, u32[]{:S(2)}, u32[]{:S(2)}) collective-permute-start(bf16[1024,128]{1,0:T(8,128)(2,1)} %get-tuple-element.11.refs_0_), channel_id=1, source_target_pairs={{0,129},{1,128},{2,131},{3,130},{4,133},{5,132},{6,135},{7,134},{1... | collective-permute-start | bytes 786440 | tf_op jit(solution)/shard_map/ppermute | solution.py:186
  173.3 14.2 %collective-permute-start.15 = (bf16[512,512]{1,0:T(8,128)(2,1)}, bf16[512,512]{1,0:T(8,128)(2,1)S(1)}, u32[]{:S(2)}, u32[]{:S(2)}) collective-permute-start(bf16[512,512]{1,0:T(8,128)(2,1)} %get-tuple-element.12.refs_0_), channel_id=1, source_target_pairs={{0,8},{8,0},{1,9},{9,1},{2,10},{10,2},{3,11},{11,3},{4,12},{12,4},... | collective-permute-start | bytes 1572872 | tf_op jit(solution)/shard_map/ppermute | solution.py:29
  173.3 14.2 %collective-permute-start.16 = (bf16[512,512]{1,0:T(8,128)(2,1)S(1)}, bf16[512,512]{1,0:T(8,128)(2,1)S(1)}, u32[]{:S(2)}, u32[]{:S(2)}) collective-permute-start(bf16[512,512]{1,0:T(8,128)(2,1)S(1)} %collective-permute-done.14.refs_1_), channel_id=1, source_target_pairs={{0,8},{8,0},{1,9},{9,1},{2,10},{10,2},{3,11},{11,3},{4,12},{12,4},... | collective-permute-start | bytes 1572872 | tf_op jit(solution)/shard_map/ppermute | solution.py:29
  193.3 9.9 %collective-permute-start.23 = (bf16[16,2048]{1,0:T(8,128)(2,1)S(1)}, bf16[16,2048]{1,0:T(8,128)(2,1)S(1)}, u32[]{:S(2)}, u32[]{:S(2)}) collective-permute-start(bf16[16,2048]{1,0:T(8,128)(2,1)S(1)} %get-tuple-element.24), channel_id=1, source_target_pairs={{0,7},{1,6},{2,5},{3,4},{4,3},{5,2},{6,1},{7,0},{8,15},{9,14},{10,... | collective-permute-start | bytes 196616 | tf_op jit(solution)/shard_map/ppermute | solution.py:249
  196.3 7.7 %collective-permute-start.22 = (bf16[16,2048]{1,0:T(8,128)(2,1)S(1)}, bf16[16,2048]{1,0:T(8,128)(2,1)S(1)}, u32[]{:S(2)}, u32[]{:S(2)}) collective-permute-start(bf16[16,2048]{1,0:T(8,128)(2,1)S(1)} %get-tuple-element.25), channel_id=1, source_target_pairs={{0,6},{1,7},{2,4},{3,5},{4,2},{5,3},{6,0},{7,1},{8,14},{9,15},{10,... | collective-permute-start | bytes 196616 | tf_op jit(solution)/shard_map/ppermute | solution.py:249
  198.4 6.6 %collective-permute-start.21 = (bf16[16,2048]{1,0:T(8,128)(2,1)S(1)}, bf16[16,2048]{1,0:T(8,128)(2,1)S(1)}, u32[]{:S(2)}, u32[]{:S(2)}) collective-permute-start(bf16[16,2048]{1,0:T(8,128)(2,1)S(1)} %get-tuple-element.26), channel_id=1, source_target_pairs={{0,5},{1,4},{2,7},{3,6},{4,1},{5,0},{6,3},{7,2},{8,13},{9,12},{10,... | collective-permute-start | bytes 196616 | tf_op jit(solution)/shard_map/ppermute | solution.py:249
  199.1 6.1 %collective-permute-start.20 = (bf16[16,2048]{1,0:T(8,128)(2,1)S(1)}, bf16[16,2048]{1,0:T(8,128)(2,1)S(1)}, u32[]{:S(2)}, u32[]{:S(2)}) collective-permute-start(bf16[16,2048]{1,0:T(8,128)(2,1)S(1)} %get-tuple-element.27), channel_id=1, source_target_pairs={{0,4},{1,5},{2,6},{3,7},{4,0},{5,1},{6,2},{7,3},{8,12},{9,13},{10,... | collective-permute-start | bytes 196616 | tf_op jit(solution)/shard_map/ppermute | solution.py:249
  200.5 5.5 %collective-permute-start.19 = (bf16[16,2048]{1,0:T(8,128)(2,1)S(1)}, bf16[16,2048]{1,0:T(8,128)(2,1)S(1)}, u32[]{:S(2)}, u32[]{:S(2)}) collective-permute-start(bf16[16,2048]{1,0:T(8,128)(2,1)S(1)} %get-tuple-element.28), channel_id=1, source_target_pairs={{0,3},{1,2},{2,1},{3,0},{4,7},{5,6},{6,5},{7,4},{8,11},{9,10},{10,... | collective-permute-start | bytes 196616 | tf_op jit(solution)/shard_map/ppermute | solution.py:249
  203.2 5.8 %collective-permute-start.18 = (bf16[16,2048]{1,0:T(8,128)(2,1)S(1)}, bf16[16,2048]{1,0:T(8,128)(2,1)S(1)}, u32[]{:S(2)}, u32[]{:S(2)}) collective-permute-start(bf16[16,2048]{1,0:T(8,128)(2,1)S(1)} %get-tuple-element.29), channel_id=1, source_target_pairs={{0,2},{1,3},{2,0},{3,1},{4,6},{5,7},{6,4},{7,5},{8,10},{9,11},{10,... | collective-permute-start | bytes 196616 | tf_op jit(solution)/shard_map/ppermute | solution.py:249
  213.7 37.7 %all-to-all-start = ((bf16[256,2,1024]{2,1,0:T(2,128)(2,1)}), bf16[256,2,1024]{2,1,0:T(2,128)(2,1)S(1)}, u32[]{:S(2)}, u32[]{:S(2)}) async-start(bf16[256,2,1024]{2,1,0:T(2,128)(2,1)} %copy.65), calls=%async_computation | async-start | bytes 2097152 | tf_op jit(solution)/shard_map/all_to_all | solution.py:285
  223.9 31.6 %collective-permute-start.25 = (bf16[1024,768]{1,0:T(8,128)(2,1)S(1)}, bf16[1024,768]{1,0:T(8,128)(2,1)}, u32[]{:S(2)}, u32[]{:S(2)}) collective-permute-start(bf16[1024,768]{1,0:T(8,128)(2,1)S(1)} %pad_maximum_fusion.1), channel_id=1, source_target_pairs={{0,8},{8,0},{1,9},{9,1},{2,10},{10,2},{3,11},{11,3},{4,12},{12,4},... | collective-permute-start | bytes 4718600 | tf_op jit(solution)/shard_map/ppermute | solution.py:29
  264.1 37.2 %all-to-all-start.2 = ((bf16[256,2,1024]{2,1,0:T(2,128)(2,1)}), bf16[256,2,1024]{2,1,0:T(2,128)(2,1)S(1)}, u32[]{:S(2)}, u32[]{:S(2)}) async-start(bf16[256,2,1024]{2,1,0:T(2,128)(2,1)} %reshape.138), calls=%async_computation.2 | async-start | bytes 2097152 | tf_op jit(solution)/shard_map/all_to_all | solution.py:310
  (29 other events, 423.4 us)

commit v5 on v4

--- a/solution.py
+++ b/solution.py
@@ -33,8 +33,6 @@
     rows = q_ref.shape[0]
     part = keys[0].shape[0]
     blocks = part // 128
-    yh = ctx // 16
-    core = lax.rem(ctx, 2)
     q = q_ref[...]
     row = lax.broadcasted_iota(jnp.int32, (rows, 1), 0)
     q_place = jnp.where(
@@ -46,11 +44,11 @@
     dims = (((1,), (1,)), ((), ()))
     top = jnp.full((rows, 128), NEG_BIG, jnp.float32)
     for side in range(4):
-        first = (yh if side % 2 == 0 else 1 - yh) * 16 + (core if side < 2 else 1 - core)
         for b in range(blocks):
             k = keys[side][b * 128 : (b + 1) * 128, :]
             s = lax.dot_general(q, k, dims, preferred_element_type=jnp.float32)
-            at = 2 * (first + 2 * b)
+            plane, half, z = block_of(ctx, side, b)
+            at = 2 * (half * 16 + z * 2 + plane)
             place = jnp.where(
                 lane < SPAN,
                 span_ref[at] * SPAN + lane,
@@ -112,49 +110,52 @@
     )(span_order, where, queries, *own, *cross)
 
 
-def assemble_kernel(z_ref, *refs):
-    parts, (piece_ref, wo_ref) = refs[:8], refs[8:]
-    for r, part in enumerate(parts):
-        at = lax.rem(z_ref[0] + r, 8)
-        piece_ref[pl.ds(pl.multiple_of(at * HD, HD), HD), :] = part[0:HD, :]
-        for h in range(4):
-            wo_ref[pl.ds(pl.multiple_of(at * 64, 64), 64), h * HD : (h + 1) * HD] = part[
-                HD + h * 64 : HD + (h + 1) * 64, :
-            ]
-
-
-def assembled(z, parts):
+def assemble_kernel(*refs):
+    parts, (piece_ref, wo_ref) = refs[:5], refs[5:]
+    rows = 3 * HD
+    at = 0
+    for part in parts:
+        for first in range(0, part.shape[0], rows):
+            piece_ref[at * HD : (at + 1) * HD, :] = part[first : first + HD, :]
+            for h in range(4):
+                f = first + HD + h * 64
+                wo_ref[at * 64 : (at + 1) * 64, h * HD : (h + 1) * HD] = part[f : f + 64, :]
+            at += 1
+
+
+def assembled(parts):
     return pl.pallas_call(
         assemble_kernel,
         out_shape=(
             jax.ShapeDtypeStruct((8 * HD, HD), jnp.bfloat16),
             jax.ShapeDtypeStruct((8 * 64, 4 * HD), jnp.bfloat16),
         ),
-        grid_spec=pltpu.PrefetchScalarGridSpec(
-            num_scalar_prefetch=1,
-            grid=(1,),
-            in_specs=[pl.BlockSpec(parts[0].shape, lambda i, *_: (0, 0))] * 8,
-            out_specs=(
-                pl.BlockSpec((8 * HD, HD), lambda i, *_: (0, 0)),
-                pl.BlockSpec((8 * 64, 4 * HD), lambda i, *_: (0, 0)),
-            ),
-        ),
+        in_specs=[pl.BlockSpec(memory_space=pltpu.VMEM)] * 5,
+        out_specs=(pl.BlockSpec(memory_space=pltpu.VMEM),) * 2,
         cost_estimate=pl.CostEstimate(flops=0, bytes_accessed=1572864, transcendentals=0),
-    )(z[None].astype(jnp.int32), *parts)
+    )(*parts)
+
+
+def block_of(ctx, side, b):
+    yh, z, core = ctx // 16, lax.rem(ctx, 16) // 2, lax.rem(ctx, 2)
+    half = yh if side % 2 == 0 else 1 - yh
+    holder = core if side < 2 else 1 - core
+    plane = holder if b in (0, 7) else (b - 1) % 2
+    away = (0, 1, 1, 2, 2, 3, 3, 4)[b]
+    return plane, half, lax.rem(z + 8 + away * (1 - 2 * holder), 8)
 
 
 def project_kernel(ctx_ref, x_ref, *refs):
-    weights, o_ref = refs[:4], refs[4]
-    yh, core = ctx_ref[0] // 16, lax.rem(ctx_ref[0], 2)
-    x = x_ref[...]
+    weights, (o_ref, w_ref) = refs[:4], refs[4:]
     for side, w in enumerate(weights):
-        half = yh if side % 2 == 0 else 1 - yh
-        plane = core if side < 2 else 1 - core
-        out = lax.dot_general(
-            x, w[...], (((1,), (1,)), ((), ())), preferred_element_type=jnp.float32
-        )
-        at = pl.multiple_of((2 * plane + half) * 512, 512)
-        o_ref[:, pl.ds(at, 512)] = out.astype(o_ref.dtype)
+        for b in range(8):
+            plane, half, z = block_of(ctx_ref[0], side, b)
+            at = pl.multiple_of(plane * HALF + half * (HALF // 2) + z * 64, 64)
+            w_ref[pl.ds(at, 64), :] = w[b * 64 : (b + 1) * 64, :]
+    out = lax.dot_general(
+        x_ref[...], w_ref[...], (((1,), (1,)), ((), ())), preferred_element_type=jnp.float32
+    )
+    o_ref[...] = out.astype(o_ref.dtype)
 
 
 def project(ctx, x, weights):
@@ -166,6 +167,7 @@
             grid=(1,),
             in_specs=[pl.BlockSpec(a.shape, lambda i, *_: (0, 0)) for a in [x, *weights]],
             out_specs=pl.BlockSpec((x.shape[0], D), lambda i, *_: (0, 0)),
+            scratch_shapes=[pltpu.VMEM((D, x.shape[1]), jnp.bfloat16)],
         ),
         cost_estimate=pl.CostEstimate(
             flops=2 * x.shape[0] * x.shape[1] * D, bytes_accessed=2752512, transcendentals=0
@@ -221,15 +223,24 @@
         lax.dynamic_slice_in_dim(values, head, HD, 1),
     )
     packed = jnp.concatenate([mine, wo.transpose(0, 2, 1).reshape(-1, HD)], axis=0)
-    parts = [packed] + [
-        lax.ppermute(packed, "z", [((i + r) % 8, i) for i in range(8)])
-        for r in range(1, 8)
-    ]
+    other = swapped(packed)
+    both = jnp.concatenate(
+        [jnp.where(core == 0, packed, other), jnp.where(core == 0, other, packed)], axis=0
+    )
+    parts = [packed]
+    for j in range(1, 4):
+        pairs = [
+            ((i + (j if c == 0 else 8 - j)) % 8 * 2 + c, i * 2 + c)
+            for i in range(8)
+            for c in range(2)
+        ]
+        parts.append(lax.ppermute(both, ("z", "core"), pairs))
+    parts.append(lax.ppermute(packed, "z", [((i + 4) % 8, i) for i in range(8)]))
     weights = lax.all_to_all(
         jnp.concatenate([w_gate, w_up, w_down], axis=2), CHIP, 0, 0, tiled=True
     ).reshape(HALF, -1)
 
-    piece, wo_near = assembled(lax.axis_index("z"), parts)
+    piece, wo_near = assembled(parts)
     near = [piece, across_y(piece), across_x(piece), across_xy(piece)]
     wo_near = [wo_near, across_y(wo_near)]
     far = [swapped(p) for p in near]

time: 306 us -> 305 us (level)
  waiting for transfers between devices: 198 us -> 192 us
  starting transfers between devices: 57.7 us -> 61.8 us
    ppermute x2, waiting for transfers between devices: 19.6 us -> 7.08 us  [across_y(): return lax.ppermute(x, 'yh', SWAP)]
    all_to_all x1, starting transfers between devices: 6.86 us -> 14.8 us  [shards(): tokens = lax.all_to_all(outgoing, ALL, 0, 0, tiled=True).reshape(512, HALF)]
    ppermute x1, waiting for transfers between devices: 0.01 us -> 4.4 us  [across_xy(): return lax.ppermute(x, ('yh', 'exp'), pairs)]
    ppermute x7 -> x4, starting transfers between devices: 13.2 us -> 9.25 us  [the longest x3 6.57 us: shards(): parts.append(lax.ppermute(both, ('z', 'core'), pairs))]
    ppermute x7 -> x4, waiting for transfers between devices: 114 us -> 117 us  [the longest x1 117 us: shards(): lax.ppermute(packed, 'z', [((i + 4) % 8, i) for i in range(8)])]
  transfers between devices with their start and end apart: 30 -> 28, of which waited for: 12 -> 11; matrix products, arithmetic and copies ran while one was open for 6% -> 6% of each run, Pallas kernels for 5% -> 5%
where the time goes in v5:
time: 305 us; the launch traced here: 304 us
  waiting for transfers between devices  192 us (63%)
  starting transfers between devices  61.8 us (20%)
  local copies, waits for them, and re-layouts  17.6 us (6%)
  Pallas kernels  14.7 us (5%)
  matrix products  9.49 us (3%)
  other arithmetic  7.8 us (3%)
    ppermute x1, waiting for transfers between devices, shards(): lax.ppermute(packed, 'z', [((i + 4) % 8, i) for i in range(8)])  117 us
    all_to_all x1, waiting for transfers between devices, shards(): home = lax.all_to_all(out.reshape(256, CAP, HALF), ALL, 0, 0, tiled=True)  30.6 us
    all_to_all x1, waiting for transfers between devices, shards(): tokens = lax.all_to_all(outgoing, ALL, 0, 0, tiled=True).reshape(512, HALF)  27 us
    all_to_all x1, starting transfers between devices, shards(): tokens = lax.all_to_all(outgoing, ALL, 0, 0, tiled=True).reshape(512, HALF)  14.8 us
    ppermute x7, starting transfers between devices, shards(): got = lax.ppermute(sent, 'exp', [(e, e ^ d) for e in range(8)])  11.3 us
    all_to_all x1, starting transfers between devices, shards(): lax.all_to_all(jnp.concatenate([w_gate, w_up, w_down], axis=2), CHIP, 0,...  11.3 us
    pallas_call x1, Pallas kernels, attend(): pl.pallas_call(attend_kernel, out_shape=jax.ShapeDtypeStruct((rows, width...  9.17 us
    ppermute x2, waiting for transfers between devices, across_y(): return lax.ppermute(x, 'yh', SWAP)  7.08 us
  transfers between devices with their start and end apart: 28, of which 11 were waited for; matrix products, arithmetic and copies ran while one was open for 6% of the time, Pallas kernels for 5%

profile of v5, /device:TPU:32, one launch (start us, length us, event | category | flops | bytes accessed | tf_op | source)
XLA Modules:
  0.0 303.6 jit_solution(12688711464272569493)
XLA Ops:
  0.0 3.9 %pad_maximum_fusion = bf16[16,64,2304]{2,1,0:T(8,128)(2,1)} fusion(bf16[16,64,768]{2,1,0:T(8,128)(2,1)} %param.23, bf16[16,64,768]{2,1,0:T(8,128)(2,1)} %param.22, bf16[16,64,768]{2,1,0:T(8,128)(2,1)} %param.21), kind=kLoop, calls=%fused_computation | loop fusion | flops 14155776 | bytes 9437184 | tf_op jit(solution)/shard_map/concatenate | solution.py:240
  3.9 11.3 %all-to-all-start.1 = ((bf16[16,64,2304]{2,1,0:T(8,128)(2,1)}), bf16[16,64,2304]{2,1,0:T(8,128)(2,1)}, u32[]{:S(2)}, u32[]{:S(2)}) async-start(bf16[16,64,2304]{2,1,0:T(8,128)(2,1)} %pad_maximum_fusion), calls=%async_computation.1 | async-start | bytes 9437184 | tf_op jit(solution)/shard_map/all_to_all | solution.py:239
  17.8 4.0 %collective-permute-start.2 = (bf16[768,128]{1,0:T(8,128)(2,1)S(1)}, bf16[768,128]{1,0:T(8,128)(2,1)S(1)}, u32[]{:S(2)}, u32[]{:S(2)}) collective-permute-start(bf16[768,128]{1,0:T(8,128)(2,1)S(1)} %pad_maximum_fusion.2), channel_id=1, source_target_pairs={{32,0},{104,8},{48,16},{120,24},{64,32},{8,40},{80,48},{24,56},{96... | collective-permute-start | bytes 589832 | tf_op jit(solution)/shard_map/ppermute | solution.py:237
  21.8 2.4 collective-permute-start.3
  24.1 2.7 collective-permute-start.4
  26.8 116.9 %collective-permute-done.4.refs_4_ = bf16[384,128]{1,0:T(8,128)(2,1)S(1)} collective-permute-done((bf16[384,128]{1,0:T(8,128)(2,1)S(1)}, bf16[384,128]{1,0:T(8,128)(2,1)S(1)}, u32[]{:S(2)}, u32[]{:S(2)}) %collective-permute-start.4) | collective-permute-done | bytes 98336 | tf_op jit(solution)/shard_map/ppermute | solution.py:238
  145.2 2.2 shard_map.118
  147.4 1.9 collective-permute-start.12
  152.4 1.9 collective-permute-start.9
  154.4 7.1 %collective-permute-done.5.refs_1_ = bf16[1024,128]{1,0:T(8,128)(2,1)S(1)} collective-permute-done((bf16[1024,128]{1,0:T(8,128)(2,1)}, bf16[1024,128]{1,0:T(8,128)(2,1)S(1)}, u32[]{:S(2)}, u32[]{:S(2)}) %collective-permute-start.5) | collective-permute-done | bytes 262176 | tf_op jit(solution)/shard_map/ppermute | solution.py:179
  162.5 4.4 %collective-permute-done.9.refs_5_ = bf16[1024,128]{1,0:T(8,128)(2,1)S(1)} collective-permute-done((bf16[1024,128]{1,0:T(8,128)(2,1)}, bf16[1024,128]{1,0:T(8,128)(2,1)S(1)}, u32[]{:S(2)}, u32[]{:S(2)}) %collective-permute-start.9) | collective-permute-done | bytes 262176 | tf_op jit(solution)/shard_map/ppermute | solution.py:188
  169.5 9.2 %shard_map.119.x_ref = bf16[128,512]{1,0:T(8,128)(2,1)} custom-call(s32[64]{0:T(128)} %span_ref.1, s32[2]{0:T(128)} %pad_add_fusion.where_ref, bf16[128,512]{1,0:T(8,128)(2,1)} %q_ref.1, bf16[1024,128]{1,0:T(8,128)(2,1)} %get-tuple-element.11.refs_0_, bf16[1024,128]{1,0:T(8,128)(2,1)} %copy-done.13, bf16[1024,128]{1,0:T(8,128)(2,1)} %copy-done.14, ...), custom_call_target="tpu_custom_call" | custom-call | flops 1073741824 | bytes 2359296 | tf_op jit(solution)/shard_map/pallas_call | solution.py:94
  180.3 3.3 %shard_map.120 = bf16[128,2048]{1,0:T(8,128)(2,1)} custom-call(s32[1]{0:T(128)} %bitcast.1.ctx_ref, bf16[128,512]{1,0:T(8,128)(2,1)} %shard_map.119.x_ref, bf16[512,512]{1,0:T(8,128)(2,1)} %get-tuple-element.12.refs_0_, bf16[512,512]{1,0:T(8,128)(2,1)} %copy-done, bf16[512,512]{1,0:T(8,128)(2,1)} %copy-done.1, bf16[512,512]{1,0:T(8,128)(2,1)} %copy-done.2), custom_call_target="tpu_custom_call" | custom-call | flops 268435456 | bytes 2752512 | tf_op jit(solution)/shard_map/pallas_call | solution.py:162
  184.7 3.0 collective-permute-start.21
  191.8 2.8 collective-permute-start.17
  197.3 3.1 %collective-permute-done.16 = bf16[16,2048]{1,0:T(8,128)(2,1)S(1)} collective-permute-done((bf16[16,2048]{1,0:T(8,128)(2,1)S(1)}, bf16[16,2048]{1,0:T(8,128)(2,1)S(1)}, u32[]{:S(2)}, u32[]{:S(2)}) %collective-permute-start.16) | collective-permute-done | bytes 65568 | tf_op jit(solution)/shard_map/ppermute | solution.py:260
  203.0 2.1 copy.65
  205.1 14.8 %all-to-all-start = ((bf16[256,2,1024]{2,1,0:T(2,128)(2,1)}), bf16[256,2,1024]{2,1,0:T(2,128)(2,1)S(1)}, u32[]{:S(2)}, u32[]{:S(2)}) async-start(bf16[256,2,1024]{2,1,0:T(2,128)(2,1)} %copy.65), calls=%async_computation | async-start | bytes 2097152 | tf_op jit(solution)/shard_map/all_to_all | solution.py:296
  219.9 3.2 %constant_dynamic-slice_fusion.1 = (bf16[1024,384]{1,0:T(8,128)(2,1)S(1)}, bf16[1024,384]{1,0:T(8,128)(2,1)S(1)}, bf16[1024,384]{1,0:T(8,128)(2,1)S(1)}, bf16[1024,384]{1,0:T(8,128)(2,1)}) fusion(bf16[1024,2304]{1,0:T(8,128)(2,1)} %bitcast.17, s32[]{:T(128)S(6)} %select_n.124, s32[]{:T(128)S(6)} %select_n.125, s32[]{:T(128)S(6)} %select_n.123, s32[]{:T(128)S(6)} %select_n.122), kind=kLoop, calls=%fused_computation.67 | loop fusion | bytes 6291472 | tf_op jit(solution)/shard_map/dynamic_slice | solution.py:301
  223.6 27.0 %all-to-all-done = bf16[256,2,1024]{2,1,0:T(2,128)(2,1)S(1)} async-done(((bf16[256,2,1024]{2,1,0:T(2,128)(2,1)}), bf16[256,2,1024]{2,1,0:T(2,128)(2,1)S(1)}, u32[]{:S(2)}, u32[]{:S(2)}) %all-to-all-start) | async-done | bytes 1048608 | tf_op jit(solution)/shard_map/all_to_all | solution.py:296
  251.9 2.4 fusion
  254.7 2.4 fusion.35
  263.3 6.4 %all-to-all-start.2 = ((bf16[256,2,1024]{2,1,0:T(2,128)(2,1)}), bf16[256,2,1024]{2,1,0:T(2,128)(2,1)S(1)}, u32[]{:S(2)}, u32[]{:S(2)}) async-start(bf16[256,2,1024]{2,1,0:T(2,128)(2,1)} %reshape.138), calls=%async_computation.2 | async-start | bytes 2097152 | tf_op jit(solution)/shard_map/all_to_all | solution.py:321
  269.9 30.6 %all-to-all-done.2 = bf16[256,2,1024]{2,1,0:T(2,128)(2,1)S(1)} async-done(((bf16[256,2,1024]{2,1,0:T(2,128)(2,1)}), bf16[256,2,1024]{2,1,0:T(2,128)(2,1)S(1)}, u32[]{:S(2)}, u32[]{:S(2)}) %all-to-all-start.2) | async-done | bytes 1048608 | tf_op jit(solution)/shard_map/all_to_all | solution.py:321
  (121 shorter events, 34.3 us)
Async XLA Ops:
  3.9 201.1 %all-to-all-start.1 = ((bf16[16,64,2304]{2,1,0:T(8,128)(2,1)}), bf16[16,64,2304]{2,1,0:T(8,128)(2,1)}, u32[]{:S(2)}, u32[]{:S(2)}) async-start(bf16[16,64,2304]{2,1,0:T(8,128)(2,1)} %pad_maximum_fusion), calls=%async_computation.1 | async-start | bytes 9437184 | tf_op jit(solution)/shard_map/all_to_all | solution.py:239
  17.6 126.2 %collective-permute-start.1 = (bf16[768,128]{1,0:T(8,128)(2,1)S(1)}, bf16[768,128]{1,0:T(8,128)(2,1)S(1)}, u32[]{:S(2)}, u32[]{:S(2)}) collective-permute-start(bf16[768,128]{1,0:T(8,128)(2,1)S(1)} %pad_maximum_fusion.2), channel_id=1, source_target_pairs={{16,0},{120,8},{32,16},{8,24},{48,32},{24,40},{64,48},{40,56},{80,... | collective-permute-start | bytes 589832 | tf_op jit(solution)/shard_map/ppermute | solution.py:237
  17.8 125.9 %collective-permute-start.2 = (bf16[768,128]{1,0:T(8,128)(2,1)S(1)}, bf16[768,128]{1,0:T(8,128)(2,1)S(1)}, u32[]{:S(2)}, u32[]{:S(2)}) collective-permute-start(bf16[768,128]{1,0:T(8,128)(2,1)S(1)} %pad_maximum_fusion.2), channel_id=1, source_target_pairs={{32,0},{104,8},{48,16},{120,24},{64,32},{8,40},{80,48},{24,56},{96... | collective-permute-start | bytes 589832 | tf_op jit(solution)/shard_map/ppermute | solution.py:237
  21.8 122.0 %collective-permute-start.3 = (bf16[768,128]{1,0:T(8,128)(2,1)S(1)}, bf16[768,128]{1,0:T(8,128)(2,1)S(1)}, u32[]{:S(2)}, u32[]{:S(2)}) collective-permute-start(bf16[768,128]{1,0:T(8,128)(2,1)S(1)} %pad_maximum_fusion.2), channel_id=1, source_target_pairs={{48,0},{88,8},{64,16},{104,24},{80,32},{120,40},{96,48},{8,56},{11... | collective-permute-start | bytes 589832 | tf_op jit(solution)/shard_map/ppermute | solution.py:237
  24.1 119.6 %collective-permute-start.4 = (bf16[384,128]{1,0:T(8,128)(2,1)S(1)}, bf16[384,128]{1,0:T(8,128)(2,1)S(1)}, u32[]{:S(2)}, u32[]{:S(2)}) collective-permute-start(bf16[384,128]{1,0:T(8,128)(2,1)S(1)} %pad_maximum_fusion.3.refs_0_), channel_id=1, source_target_pairs={{64,0},{80,16},{96,32},{112,48},{0,64},{16,80},{32,96},{48,112},{6... | collective-permute-start | bytes 294920 | tf_op jit(solution)/shard_map/ppermute | solution.py:238
  147.4 14.0 %collective-permute-start.12 = (bf16[512,512]{1,0:T(8,128)(2,1)}, bf16[512,512]{1,0:T(8,128)(2,1)S(1)}, u32[]{:S(2)}, u32[]{:S(2)}) collective-permute-start(bf16[512,512]{1,0:T(8,128)(2,1)} %get-tuple-element.12.refs_0_), channel_id=1, source_target_pairs={{0,128},{128,0},{1,129},{129,1},{2,130},{130,2},{3,131},{131,3},{4... | collective-permute-start | bytes 1572872 | tf_op jit(solution)/shard_map/ppermute | solution.py:179
  149.4 12.1 %collective-permute-start.5 = (bf16[1024,128]{1,0:T(8,128)(2,1)}, bf16[1024,128]{1,0:T(8,128)(2,1)S(1)}, u32[]{:S(2)}, u32[]{:S(2)}) collective-permute-start(bf16[1024,128]{1,0:T(8,128)(2,1)} %get-tuple-element.11.refs_0_), channel_id=1, source_target_pairs={{0,128},{128,0},{1,129},{129,1},{2,130},{130,2},{3,131},{131,3},{4... | collective-permute-start | bytes 786440 | tf_op jit(solution)/shard_map/ppermute | solution.py:179
  150.9 11.0 %collective-permute-start.6 = (bf16[1024,128]{1,0:T(8,128)(2,1)}, bf16[1024,128]{1,0:T(8,128)(2,1)S(1)}, u32[]{:S(2)}, u32[]{:S(2)}) collective-permute-start(bf16[1024,128]{1,0:T(8,128)(2,1)} %get-tuple-element.11.refs_0_), channel_id=1, source_target_pairs={{0,8},{8,0},{1,9},{9,1},{2,10},{10,2},{3,11},{11,3},{4,12},{12,4},... | collective-permute-start | bytes 786440 | tf_op jit(solution)/shard_map/ppermute | solution.py:29
  150.9 11.1 %collective-permute-start.8 = (bf16[1024,128]{1,0:T(8,128)(2,1)}, bf16[1024,128]{1,0:T(8,128)(2,1)S(1)}, u32[]{:S(2)}, u32[]{:S(2)}) collective-permute-start(bf16[1024,128]{1,0:T(8,128)(2,1)} %get-tuple-element.11.refs_0_), channel_id=1, source_target_pairs={{0,1},{1,0},{2,3},{3,2},{4,5},{5,4},{6,7},{7,6},{8,9},{9,8},{10,11... | collective-permute-start | bytes 786440 | tf_op jit(solution)/shard_map/ppermute | solution.py:183
  152.4 14.4 %collective-permute-start.9 = (bf16[1024,128]{1,0:T(8,128)(2,1)}, bf16[1024,128]{1,0:T(8,128)(2,1)S(1)}, u32[]{:S(2)}, u32[]{:S(2)}) collective-permute-start(bf16[1024,128]{1,0:T(8,128)(2,1)} %get-tuple-element.11.refs_0_), channel_id=1, source_target_pairs={{0,129},{1,128},{2,131},{3,130},{4,133},{5,132},{6,135},{7,134},{1... | collective-permute-start | bytes 786440 | tf_op jit(solution)/shard_map/ppermute | solution.py:188
  161.4 17.3 %collective-permute-start.13 = (bf16[512,512]{1,0:T(8,128)(2,1)}, bf16[512,512]{1,0:T(8,128)(2,1)S(1)}, u32[]{:S(2)}, u32[]{:S(2)}) collective-permute-start(bf16[512,512]{1,0:T(8,128)(2,1)} %get-tuple-element.12.refs_0_), channel_id=1, source_target_pairs={{0,8},{8,0},{1,9},{9,1},{2,10},{10,2},{3,11},{11,3},{4,12},{12,4},... | collective-permute-start | bytes 1572872 | tf_op jit(solution)/shard_map/ppermute | solution.py:29
  161.5 17.3 %collective-permute-start.14 = (bf16[512,512]{1,0:T(8,128)(2,1)S(1)}, bf16[512,512]{1,0:T(8,128)(2,1)S(1)}, u32[]{:S(2)}, u32[]{:S(2)}) collective-permute-start(bf16[512,512]{1,0:T(8,128)(2,1)S(1)} %collective-permute-done.12.refs_1_), channel_id=1, source_target_pairs={{0,8},{8,0},{1,9},{9,1},{2,10},{10,2},{3,11},{11,3},{4,12},{12,4},... | collective-permute-start | bytes 1572872 | tf_op jit(solution)/shard_map/ppermute | solution.py:29
  162.0 6.0 %collective-permute-start.7 = (bf16[1024,128]{1,0:T(8,128)(2,1)S(1)}, bf16[1024,128]{1,0:T(8,128)(2,1)S(1)}, u32[]{:S(2)}, u32[]{:S(2)}) collective-permute-start(bf16[1024,128]{1,0:T(8,128)(2,1)S(1)} %collective-permute-done.5.refs_1_), channel_id=1, source_target_pairs={{0,8},{8,0},{1,9},{9,1},{2,10},{10,2},{3,11},{11,3},{4,12},{12,4},... | collective-permute-start | bytes 786440 | tf_op jit(solution)/shard_map/ppermute | solution.py:29
  162.1 5.9 %collective-permute-start.10 = (bf16[1024,128]{1,0:T(8,128)(2,1)S(1)}, bf16[1024,128]{1,0:T(8,128)(2,1)S(1)}, u32[]{:S(2)}, u32[]{:S(2)}) collective-permute-start(bf16[1024,128]{1,0:T(8,128)(2,1)S(1)} %collective-permute-done.8.refs_4_), channel_id=1, source_target_pairs={{0,8},{8,0},{1,9},{9,1},{2,10},{10,2},{3,11},{11,3},{4,12},{12,4},... | collective-permute-start | bytes 786440 | tf_op jit(solution)/shard_map/ppermute | solution.py:29
  184.7 9.9 %collective-permute-start.21 = (bf16[16,2048]{1,0:T(8,128)(2,1)S(1)}, bf16[16,2048]{1,0:T(8,128)(2,1)S(1)}, u32[]{:S(2)}, u32[]{:S(2)}) collective-permute-start(bf16[16,2048]{1,0:T(8,128)(2,1)S(1)} %get-tuple-element.24), channel_id=1, source_target_pairs={{0,7},{1,6},{2,5},{3,4},{4,3},{5,2},{6,1},{7,0},{8,15},{9,14},{10,... | collective-permute-start | bytes 196616 | tf_op jit(solution)/shard_map/ppermute | solution.py:260
  187.6 7.7 %collective-permute-start.20 = (bf16[16,2048]{1,0:T(8,128)(2,1)S(1)}, bf16[16,2048]{1,0:T(8,128)(2,1)S(1)}, u32[]{:S(2)}, u32[]{:S(2)}) collective-permute-start(bf16[16,2048]{1,0:T(8,128)(2,1)S(1)} %get-tuple-element.25), channel_id=1, source_target_pairs={{0,6},{1,7},{2,4},{3,5},{4,2},{5,3},{6,0},{7,1},{8,14},{9,15},{10,... | collective-permute-start | bytes 196616 | tf_op jit(solution)/shard_map/ppermute | solution.py:260
  189.8 6.9 %collective-permute-start.19 = (bf16[16,2048]{1,0:T(8,128)(2,1)S(1)}, bf16[16,2048]{1,0:T(8,128)(2,1)S(1)}, u32[]{:S(2)}, u32[]{:S(2)}) collective-permute-start(bf16[16,2048]{1,0:T(8,128)(2,1)S(1)} %get-tuple-element.26), channel_id=1, source_target_pairs={{0,5},{1,4},{2,7},{3,6},{4,1},{5,0},{6,3},{7,2},{8,13},{9,12},{10,... | collective-permute-start | bytes 196616 | tf_op jit(solution)/shard_map/ppermute | solution.py:260
  190.5 6.5 %collective-permute-start.18 = (bf16[16,2048]{1,0:T(8,128)(2,1)S(1)}, bf16[16,2048]{1,0:T(8,128)(2,1)S(1)}, u32[]{:S(2)}, u32[]{:S(2)}) collective-permute-start(bf16[16,2048]{1,0:T(8,128)(2,1)S(1)} %get-tuple-element.27), channel_id=1, source_target_pairs={{0,4},{1,5},{2,6},{3,7},{4,0},{5,1},{6,2},{7,3},{8,12},{9,13},{10,... | collective-permute-start | bytes 196616 | tf_op jit(solution)/shard_map/ppermute | solution.py:260
  191.8 5.5 %collective-permute-start.17 = (bf16[16,2048]{1,0:T(8,128)(2,1)S(1)}, bf16[16,2048]{1,0:T(8,128)(2,1)S(1)}, u32[]{:S(2)}, u32[]{:S(2)}) collective-permute-start(bf16[16,2048]{1,0:T(8,128)(2,1)S(1)} %get-tuple-element.28), channel_id=1, source_target_pairs={{0,3},{1,2},{2,1},{3,0},{4,7},{5,6},{6,5},{7,4},{8,11},{9,10},{10,... | collective-permute-start | bytes 196616 | tf_op jit(solution)/shard_map/ppermute | solution.py:260
  194.6 5.8 %collective-permute-start.16 = (bf16[16,2048]{1,0:T(8,128)(2,1)S(1)}, bf16[16,2048]{1,0:T(8,128)(2,1)S(1)}, u32[]{:S(2)}, u32[]{:S(2)}) collective-permute-start(bf16[16,2048]{1,0:T(8,128)(2,1)S(1)} %get-tuple-element.29), channel_id=1, source_target_pairs={{0,2},{1,3},{2,0},{3,1},{4,6},{5,7},{6,4},{7,5},{8,10},{9,11},{10,... | collective-permute-start | bytes 196616 | tf_op jit(solution)/shard_map/ppermute | solution.py:260
  195.4 5.0 %collective-permute-start.15 = (bf16[16,2048]{1,0:T(8,128)(2,1)S(1)}, bf16[16,2048]{1,0:T(8,128)(2,1)S(1)}, u32[]{:S(2)}, u32[]{:S(2)}) collective-permute-start(bf16[16,2048]{1,0:T(8,128)(2,1)S(1)} %get-tuple-element.23), channel_id=1, source_target_pairs={{0,1},{1,0},{2,3},{3,2},{4,5},{5,4},{6,7},{7,6},{8,9},{9,8},{10,11... | collective-permute-start | bytes 196616 | tf_op jit(solution)/shard_map/ppermute | solution.py:260
  205.1 45.6 %all-to-all-start = ((bf16[256,2,1024]{2,1,0:T(2,128)(2,1)}), bf16[256,2,1024]{2,1,0:T(2,128)(2,1)S(1)}, u32[]{:S(2)}, u32[]{:S(2)}) async-start(bf16[256,2,1024]{2,1,0:T(2,128)(2,1)} %copy.65), calls=%async_computation | async-start | bytes 2097152 | tf_op jit(solution)/shard_map/all_to_all | solution.py:296
  223.2 31.6 %collective-permute-start.23 = (bf16[1024,768]{1,0:T(8,128)(2,1)S(1)}, bf16[1024,768]{1,0:T(8,128)(2,1)}, u32[]{:S(2)}, u32[]{:S(2)}) collective-permute-start(bf16[1024,768]{1,0:T(8,128)(2,1)S(1)} %pad_maximum_fusion.1), channel_id=1, source_target_pairs={{0,8},{8,0},{1,9},{9,1},{2,10},{10,2},{3,11},{11,3},{4,12},{12,4},... | collective-permute-start | bytes 4718600 | tf_op jit(solution)/shard_map/ppermute | solution.py:29
  263.3 37.2 %all-to-all-start.2 = ((bf16[256,2,1024]{2,1,0:T(2,128)(2,1)}), bf16[256,2,1024]{2,1,0:T(2,128)(2,1)S(1)}, u32[]{:S(2)}, u32[]{:S(2)}) async-start(bf16[256,2,1024]{2,1,0:T(2,128)(2,1)} %reshape.138), calls=%async_computation.2 | async-start | bytes 2097152 | tf_op jit(solution)/shard_map/all_to_all | solution.py:321
  (24 other events, 385.0 us)

commit v6 on v5

--- a/solution.py
+++ b/solution.py
@@ -175,6 +175,44 @@
     )(ctx[None].astype(jnp.int32), x, *weights)
 
 
+def place_kernel(exp_ref, *refs):
+    blocks, (o_ref, row_ref) = refs[:8], refs[8:]
+    for d, block in enumerate(blocks):
+        row_ref[d * 16 : (d + 1) * 16, :] = block[...].astype(jnp.float32)
+    exp = exp_ref[0]
+    codes = jnp.transpose(row_ref[:, D:])
+    slot = lax.broadcasted_iota(jnp.int32, (256, 128), 0)
+    lane = lax.broadcasted_iota(jnp.int32, (256, 128), 1)
+    wanted = ((exp * OWN + slot // 16) * CAP + slot % CAP).astype(jnp.float32)
+    hit = jnp.zeros((256, 128), jnp.float32)
+    for t in range(TOPK):
+        hit = hit + jnp.where(codes[t : t + 1, :] == wanted, 1.0, 0.0)
+    hit = jnp.where((slot % 16) // CAP == jnp.bitwise_xor(lane // 16, exp), hit, 0.0)
+    hit = hit.astype(jnp.bfloat16)
+    for plane in range(2):
+        x = row_ref[:, plane * HALF : (plane + 1) * HALF].astype(jnp.bfloat16)
+        out = jnp.dot(hit, x, preferred_element_type=jnp.float32).astype(o_ref.dtype)
+        for k in range(OWN):
+            o_ref[2 * k + plane, :, :] = out[k * 16 : (k + 1) * 16, :]
+
+
+def placed(exp, blocks):
+    return pl.pallas_call(
+        place_kernel,
+        out_shape=jax.ShapeDtypeStruct((2 * OWN, 16, HALF), jnp.bfloat16),
+        grid_spec=pltpu.PrefetchScalarGridSpec(
+            num_scalar_prefetch=1,
+            grid=(1,),
+            in_specs=[pl.BlockSpec(b.shape, lambda i, *_: (0, 0)) for b in blocks],
+            out_specs=pl.BlockSpec((2 * OWN, 16, HALF), lambda i, *_: (0, 0, 0)),
+            scratch_shapes=[pltpu.VMEM((128, D + 128), jnp.float32)],
+        ),
+        cost_estimate=pl.CostEstimate(
+            flops=2 * 256 * 128 * D, bytes_accessed=1605632, transcendentals=0
+        ),
+    )(exp[None].astype(jnp.int32), *blocks)
+
+
 def across_y(x):
     return lax.ppermute(x, "yh", SWAP)
 
@@ -277,7 +315,8 @@
     rank = jnp.sum(ahead * hits, axis=1).astype(jnp.int32)
     slots = (((flat % OWN) * 8 + flat // OWN) * CAP + rank).reshape(rows, TOPK)
     slot_ids = jnp.arange(EXPERTS * CAP, dtype=jnp.int32)
-    placing = jnp.any(slots[None, :, :] == slot_ids[:, None, None], axis=2).astype(jnp.bfloat16)
+    codes = (flat * CAP + rank).reshape(rows, TOPK).astype(jnp.bfloat16)
+    codes = jnp.pad(codes, ((0, 0), (0, 128 - TOPK)))
     combine = jnp.sum(
         jnp.where(
             slots[:, :, None] == slot_ids[None, None, :],
@@ -287,13 +326,12 @@
         axis=1,
     )
 
-    outgoing = jnp.dot(placing, normed, preferred_element_type=jnp.float32).astype(jnp.bfloat16)
-    outgoing = (
-        outgoing.reshape(OWN, 8, CAP, 2, HALF)
-        .transpose(0, 3, 1, 2, 4)
-        .reshape(256, CAP, HALF)
-    )
-    tokens = lax.all_to_all(outgoing, ALL, 0, 0, tiled=True).reshape(512, HALF)
+    payload = jnp.concatenate([normed, codes], axis=1)
+    blocks = [payload] + [
+        lax.ppermute(payload, "exp", [(e, e ^ d) for e in range(8)]) for d in range(1, 8)
+    ]
+    outgoing = placed(exp, blocks)
+    tokens = lax.all_to_all(outgoing, CTX, 0, 0, tiled=True).reshape(512, HALF)
 
     half = FF // 2
 

time: 305 us -> 316 us (1.036)
  starting transfers between devices: 61.8 us -> 71.6 us
  local copies, waits for them, and re-layouts: 17.6 us -> 13.5 us
    ppermute x0 -> x7, starting transfers between devices: none -> 11.8 us  [shards(): lax.ppermute(payload, 'exp', [(e, e ^ d) for e in range(8)])]
    reshape x4 -> x0, local copies, waits for them, and re-layouts: 4.36 us -> none  [the longest x1 2.06 us: shards(): outgoing = outgoing.reshape(OWN, 8, CAP, 2, HALF).transpose(0, 3, 1, 2, 4...]
    ppermute x0 -> x7, waiting for transfers between devices: none -> 3.8 us  [shards(): lax.ppermute(payload, 'exp', [(e, e ^ d) for e in range(8)])]
  transfers between devices with their start and end apart: 28 -> 35, of which waited for: 11 -> 12; matrix products, arithmetic and copies ran while one was open for 6% -> 4% of each run, Pallas kernels for 5% -> 6%
where the time goes in v6:
time: 316 us; the launch traced here: 315 us
  waiting for transfers between devices  195 us (62%)
  starting transfers between devices  71.6 us (23%)
  Pallas kernels  17.4 us (6%)
  local copies, waits for them, and re-layouts  13.5 us (4%)
  matrix products  8.67 us (3%)
  other arithmetic  7.75 us (2%)
    ppermute x1, waiting for transfers between devices, shards(): lax.ppermute(packed, 'z', [((i + 4) % 8, i) for i in range(8)])  117 us
    all_to_all x1, waiting for transfers between devices, shards(): home = lax.all_to_all(out.reshape(256, CAP, HALF), ALL, 0, 0, tiled=True)  30.6 us
    all_to_all x1, waiting for transfers between devices, shards(): tokens = lax.all_to_all(outgoing, CTX, 0, 0, tiled=True).reshape(512, HALF)  27.1 us
    all_to_all x1, starting transfers between devices, shards(): tokens = lax.all_to_all(outgoing, CTX, 0, 0, tiled=True).reshape(512, HALF)  13.6 us
    ppermute x7, starting transfers between devices, shards(): lax.ppermute(payload, 'exp', [(e, e ^ d) for e in range(8)])  11.8 us
    ppermute x7, starting transfers between devices, shards(): got = lax.ppermute(sent, 'exp', [(e, e ^ d) for e in range(8)])  11.7 us
    all_to_all x1, starting transfers between devices, shards(): lax.all_to_all(jnp.concatenate([w_gate, w_up, w_down], axis=2), CHIP, 0,...  11.3 us
    pallas_call x1, Pallas kernels, attend(): pl.pallas_call(attend_kernel, out_shape=jax.ShapeDtypeStruct((rows, width...  9.17 us
  transfers between devices with their start and end apart: 35, of which 12 were waited for; matrix products, arithmetic and copies ran while one was open for 4% of the time, Pallas kernels for 6%

profile of v6, /device:TPU:32, one launch (start us, length us, event | category | flops | bytes accessed | tf_op | source)
XLA Modules:
  0.0 314.6 jit_solution(12563310003956385355)
XLA Ops:
  0.0 4.0 %pad_maximum_fusion = bf16[16,64,2304]{2,1,0:T(8,128)(2,1)} fusion(bf16[16,64,768]{2,1,0:T(8,128)(2,1)} %param.23, bf16[16,64,768]{2,1,0:T(8,128)(2,1)} %param.22, bf16[16,64,768]{2,1,0:T(8,128)(2,1)} %param.21), kind=kLoop, calls=%fused_computation | loop fusion | flops 14155776 | bytes 9437184 | tf_op jit(solution)/shard_map/concatenate | solution.py:278
  4.0 11.3 %all-to-all-start.1 = ((bf16[16,64,2304]{2,1,0:T(8,128)(2,1)}), bf16[16,64,2304]{2,1,0:T(8,128)(2,1)}, u32[]{:S(2)}, u32[]{:S(2)}) async-start(bf16[16,64,2304]{2,1,0:T(8,128)(2,1)} %pad_maximum_fusion), calls=%async_computation.1 | async-start | bytes 9437184 | tf_op jit(solution)/shard_map/all_to_all | solution.py:277
  17.9 4.0 %collective-permute-start.2 = (bf16[768,128]{1,0:T(8,128)(2,1)S(1)}, bf16[768,128]{1,0:T(8,128)(2,1)S(1)}, u32[]{:S(2)}, u32[]{:S(2)}) collective-permute-start(bf16[768,128]{1,0:T(8,128)(2,1)S(1)} %pad_maximum_fusion.2), channel_id=1, source_target_pairs={{32,0},{104,8},{48,16},{120,24},{64,32},{8,40},{80,48},{24,56},{96... | collective-permute-start | bytes 589832 | tf_op jit(solution)/shard_map/ppermute | solution.py:275
  21.8 2.4 collective-permute-start.3
  24.2 2.7 collective-permute-start.4
  26.9 116.9 %collective-permute-done.4.refs_4_ = bf16[384,128]{1,0:T(8,128)(2,1)S(1)} collective-permute-done((bf16[384,128]{1,0:T(8,128)(2,1)S(1)}, bf16[384,128]{1,0:T(8,128)(2,1)S(1)}, u32[]{:S(2)}, u32[]{:S(2)}) %collective-permute-start.4) | collective-permute-done | bytes 98336 | tf_op jit(solution)/shard_map/ppermute | solution.py:276
  145.2 2.2 shard_map.118
  154.4 7.1 %collective-permute-done.5.refs_1_ = bf16[1024,128]{1,0:T(8,128)(2,1)S(1)} collective-permute-done((bf16[1024,128]{1,0:T(8,128)(2,1)}, bf16[1024,128]{1,0:T(8,128)(2,1)S(1)}, u32[]{:S(2)}, u32[]{:S(2)}) %collective-permute-start.5) | collective-permute-done | bytes 262176 | tf_op jit(solution)/shard_map/ppermute | solution.py:217
  162.5 4.4 %collective-permute-done.9.refs_5_ = bf16[1024,128]{1,0:T(8,128)(2,1)S(1)} collective-permute-done((bf16[1024,128]{1,0:T(8,128)(2,1)}, bf16[1024,128]{1,0:T(8,128)(2,1)S(1)}, u32[]{:S(2)}, u32[]{:S(2)}) %collective-permute-start.9) | collective-permute-done | bytes 262176 | tf_op jit(solution)/shard_map/ppermute | solution.py:226
  169.3 9.2 %shard_map.119.x_ref = bf16[128,512]{1,0:T(8,128)(2,1)} custom-call(s32[64]{0:T(128)} %span_ref.1, s32[2]{0:T(128)} %pad_add_fusion.where_ref, bf16[128,512]{1,0:T(8,128)(2,1)} %q_ref.1, bf16[1024,128]{1,0:T(8,128)(2,1)} %get-tuple-element.11.refs_0_, bf16[1024,128]{1,0:T(8,128)(2,1)} %copy-done.21, bf16[1024,128]{1,0:T(8,128)(2,1)} %copy-done.22, ...), custom_call_target="tpu_custom_call" | custom-call | flops 1073741824 | bytes 2359296 | tf_op jit(solution)/shard_map/pallas_call | solution.py:94
  180.1 3.3 %shard_map.120 = bf16[128,2048]{1,0:T(8,128)(2,1)} custom-call(s32[1]{0:T(128)} %bitcast.1.ctx_ref, bf16[128,512]{1,0:T(8,128)(2,1)} %shard_map.119.x_ref, bf16[512,512]{1,0:T(8,128)(2,1)} %get-tuple-element.12.refs_0_, bf16[512,512]{1,0:T(8,128)(2,1)} %copy-done, bf16[512,512]{1,0:T(8,128)(2,1)} %copy-done.1, bf16[512,512]{1,0:T(8,128)(2,1)} %copy-done.2), custom_call_target="tpu_custom_call" | custom-call | flops 268435456 | bytes 2752512 | tf_op jit(solution)/shard_map/pallas_call | solution.py:162
  184.5 3.0 collective-permute-start.21
  191.4 2.8 collective-permute-start.17
  197.3 2.6 collective-permute-done.16
  207.2 3.1 collective-permute-start.27
  210.3 2.6 collective-permute-start.28
  213.9 2.8 collective-permute-done.28.refs_7_
  217.4 2.6 shard_map.121
  220.0 13.6 %all-to-all-start = ((bf16[32,16,1024]{2,1,0:T(8,128)(2,1)}), bf16[32,16,1024]{2,1,0:T(8,128)(2,1)S(1)}, u32[]{:S(2)}, u32[]{:S(2)}) async-start(bf16[32,16,1024]{2,1,0:T(8,128)(2,1)} %shard_map.121), calls=%async_computation | async-start | bytes 2097152 | tf_op jit(solution)/shard_map/all_to_all | solution.py:334
  233.7 3.1 constant_dynamic-slice_fusion.1
  237.1 27.1 %all-to-all-done = bf16[32,16,1024]{2,1,0:T(8,128)(2,1)S(1)} async-done(((bf16[32,16,1024]{2,1,0:T(8,128)(2,1)}), bf16[32,16,1024]{2,1,0:T(8,128)(2,1)S(1)}, u32[]{:S(2)}, u32[]{:S(2)}) %all-to-all-start) | async-done | bytes 1048608 | tf_op jit(solution)/shard_map/all_to_all | solution.py:334
  266.8 2.4 fusion.34
  275.4 5.3 %all-to-all-start.2 = ((bf16[256,2,1024]{2,1,0:T(2,128)(2,1)}), bf16[256,2,1024]{2,1,0:T(2,128)(2,1)S(1)}, u32[]{:S(2)}, u32[]{:S(2)}) async-start(bf16[256,2,1024]{2,1,0:T(2,128)(2,1)} %reshape.97), calls=%async_computation.2 | async-start | bytes 2097152 | tf_op jit(solution)/shard_map/all_to_all | solution.py:359
  280.9 30.6 %all-to-all-done.2 = bf16[256,2,1024]{2,1,0:T(2,128)(2,1)S(1)} async-done(((bf16[256,2,1024]{2,1,0:T(2,128)(2,1)}), bf16[256,2,1024]{2,1,0:T(2,128)(2,1)S(1)}, u32[]{:S(2)}, u32[]{:S(2)}) %all-to-all-start.2) | async-done | bytes 1048608 | tf_op jit(solution)/shard_map/all_to_all | solution.py:359
  (148 shorter events, 45.1 us)
Async XLA Ops:
  4.0 216.1 %all-to-all-start.1 = ((bf16[16,64,2304]{2,1,0:T(8,128)(2,1)}), bf16[16,64,2304]{2,1,0:T(8,128)(2,1)}, u32[]{:S(2)}, u32[]{:S(2)}) async-start(bf16[16,64,2304]{2,1,0:T(8,128)(2,1)} %pad_maximum_fusion), calls=%async_computation.1 | async-start | bytes 9437184 | tf_op jit(solution)/shard_map/all_to_all | solution.py:277
  17.6 126.2 %collective-permute-start.1 = (bf16[768,128]{1,0:T(8,128)(2,1)S(1)}, bf16[768,128]{1,0:T(8,128)(2,1)S(1)}, u32[]{:S(2)}, u32[]{:S(2)}) collective-permute-start(bf16[768,128]{1,0:T(8,128)(2,1)S(1)} %pad_maximum_fusion.2), channel_id=1, source_target_pairs={{16,0},{120,8},{32,16},{8,24},{48,32},{24,40},{64,48},{40,56},{80,... | collective-permute-start | bytes 589832 | tf_op jit(solution)/shard_map/ppermute | solution.py:275
  17.9 125.9 %collective-permute-start.2 = (bf16[768,128]{1,0:T(8,128)(2,1)S(1)}, bf16[768,128]{1,0:T(8,128)(2,1)S(1)}, u32[]{:S(2)}, u32[]{:S(2)}) collective-permute-start(bf16[768,128]{1,0:T(8,128)(2,1)S(1)} %pad_maximum_fusion.2), channel_id=1, source_target_pairs={{32,0},{104,8},{48,16},{120,24},{64,32},{8,40},{80,48},{24,56},{96... | collective-permute-start | bytes 589832 | tf_op jit(solution)/shard_map/ppermute | solution.py:275
  21.8 122.0 %collective-permute-start.3 = (bf16[768,128]{1,0:T(8,128)(2,1)S(1)}, bf16[768,128]{1,0:T(8,128)(2,1)S(1)}, u32[]{:S(2)}, u32[]{:S(2)}) collective-permute-start(bf16[768,128]{1,0:T(8,128)(2,1)S(1)} %pad_maximum_fusion.2), channel_id=1, source_target_pairs={{48,0},{88,8},{64,16},{104,24},{80,32},{120,40},{96,48},{8,56},{11... | collective-permute-start | bytes 589832 | tf_op jit(solution)/shard_map/ppermute | solution.py:275
  24.2 119.6 %collective-permute-start.4 = (bf16[384,128]{1,0:T(8,128)(2,1)S(1)}, bf16[384,128]{1,0:T(8,128)(2,1)S(1)}, u32[]{:S(2)}, u32[]{:S(2)}) collective-permute-start(bf16[384,128]{1,0:T(8,128)(2,1)S(1)} %pad_maximum_fusion.3.refs_0_), channel_id=1, source_target_pairs={{64,0},{80,16},{96,32},{112,48},{0,64},{16,80},{32,96},{48,112},{6... | collective-permute-start | bytes 294920 | tf_op jit(solution)/shard_map/ppermute | solution.py:276
  147.5 14.0 %collective-permute-start.12 = (bf16[512,512]{1,0:T(8,128)(2,1)}, bf16[512,512]{1,0:T(8,128)(2,1)S(1)}, u32[]{:S(2)}, u32[]{:S(2)}) collective-permute-start(bf16[512,512]{1,0:T(8,128)(2,1)} %get-tuple-element.12.refs_0_), channel_id=1, source_target_pairs={{0,128},{128,0},{1,129},{129,1},{2,130},{130,2},{3,131},{131,3},{4... | collective-permute-start | bytes 1572872 | tf_op jit(solution)/shard_map/ppermute | solution.py:217
  149.4 12.1 %collective-permute-start.5 = (bf16[1024,128]{1,0:T(8,128)(2,1)}, bf16[1024,128]{1,0:T(8,128)(2,1)S(1)}, u32[]{:S(2)}, u32[]{:S(2)}) collective-permute-start(bf16[1024,128]{1,0:T(8,128)(2,1)} %get-tuple-element.11.refs_0_), channel_id=1, source_target_pairs={{0,128},{128,0},{1,129},{129,1},{2,130},{130,2},{3,131},{131,3},{4... | collective-permute-start | bytes 786440 | tf_op jit(solution)/shard_map/ppermute | solution.py:217
  151.0 11.0 %collective-permute-start.6 = (bf16[1024,128]{1,0:T(8,128)(2,1)}, bf16[1024,128]{1,0:T(8,128)(2,1)S(1)}, u32[]{:S(2)}, u32[]{:S(2)}) collective-permute-start(bf16[1024,128]{1,0:T(8,128)(2,1)} %get-tuple-element.11.refs_0_), channel_id=1, source_target_pairs={{0,8},{8,0},{1,9},{9,1},{2,10},{10,2},{3,11},{11,3},{4,12},{12,4},... | collective-permute-start | bytes 786440 | tf_op jit(solution)/shard_map/ppermute | solution.py:29
  151.0 11.1 %collective-permute-start.8 = (bf16[1024,128]{1,0:T(8,128)(2,1)}, bf16[1024,128]{1,0:T(8,128)(2,1)S(1)}, u32[]{:S(2)}, u32[]{:S(2)}) collective-permute-start(bf16[1024,128]{1,0:T(8,128)(2,1)} %get-tuple-element.11.refs_0_), channel_id=1, source_target_pairs={{0,1},{1,0},{2,3},{3,2},{4,5},{5,4},{6,7},{7,6},{8,9},{9,8},{10,11... | collective-permute-start | bytes 786440 | tf_op jit(solution)/shard_map/ppermute | solution.py:221
  152.5 14.4 %collective-permute-start.9 = (bf16[1024,128]{1,0:T(8,128)(2,1)}, bf16[1024,128]{1,0:T(8,128)(2,1)S(1)}, u32[]{:S(2)}, u32[]{:S(2)}) collective-permute-start(bf16[1024,128]{1,0:T(8,128)(2,1)} %get-tuple-element.11.refs_0_), channel_id=1, source_target_pairs={{0,129},{1,128},{2,131},{3,130},{4,133},{5,132},{6,135},{7,134},{1... | collective-permute-start | bytes 786440 | tf_op jit(solution)/shard_map/ppermute | solution.py:226
  161.5 17.0 %collective-permute-start.13 = (bf16[512,512]{1,0:T(8,128)(2,1)}, bf16[512,512]{1,0:T(8,128)(2,1)S(1)}, u32[]{:S(2)}, u32[]{:S(2)}) collective-permute-start(bf16[512,512]{1,0:T(8,128)(2,1)} %get-tuple-element.12.refs_0_), channel_id=1, source_target_pairs={{0,8},{8,0},{1,9},{9,1},{2,10},{10,2},{3,11},{11,3},{4,12},{12,4},... | collective-permute-start | bytes 1572872 | tf_op jit(solution)/shard_map/ppermute | solution.py:29
  161.5 17.0 %collective-permute-start.14 = (bf16[512,512]{1,0:T(8,128)(2,1)S(1)}, bf16[512,512]{1,0:T(8,128)(2,1)S(1)}, u32[]{:S(2)}, u32[]{:S(2)}) collective-permute-start(bf16[512,512]{1,0:T(8,128)(2,1)S(1)} %collective-permute-done.12.refs_1_), channel_id=1, source_target_pairs={{0,8},{8,0},{1,9},{9,1},{2,10},{10,2},{3,11},{11,3},{4,12},{12,4},... | collective-permute-start | bytes 1572872 | tf_op jit(solution)/shard_map/ppermute | solution.py:29
  184.5 9.6 %collective-permute-start.21 = (bf16[16,2048]{1,0:T(8,128)(2,1)S(1)}, bf16[16,2048]{1,0:T(8,128)(2,1)S(1)}, u32[]{:S(2)}, u32[]{:S(2)}) collective-permute-start(bf16[16,2048]{1,0:T(8,128)(2,1)S(1)} %get-tuple-element.24), channel_id=1, source_target_pairs={{0,7},{1,6},{2,5},{3,4},{4,3},{5,2},{6,1},{7,0},{8,15},{9,14},{10,... | collective-permute-start | bytes 196616 | tf_op jit(solution)/shard_map/ppermute | solution.py:298
  187.4 7.7 %collective-permute-start.20 = (bf16[16,2048]{1,0:T(8,128)(2,1)S(1)}, bf16[16,2048]{1,0:T(8,128)(2,1)S(1)}, u32[]{:S(2)}, u32[]{:S(2)}) collective-permute-start(bf16[16,2048]{1,0:T(8,128)(2,1)S(1)} %get-tuple-element.25), channel_id=1, source_target_pairs={{0,6},{1,7},{2,4},{3,5},{4,2},{5,3},{6,0},{7,1},{8,14},{9,15},{10,... | collective-permute-start | bytes 196616 | tf_op jit(solution)/shard_map/ppermute | solution.py:298
  189.3 8.0 %collective-permute-start.19 = (bf16[16,2048]{1,0:T(8,128)(2,1)S(1)}, bf16[16,2048]{1,0:T(8,128)(2,1)S(1)}, u32[]{:S(2)}, u32[]{:S(2)}) collective-permute-start(bf16[16,2048]{1,0:T(8,128)(2,1)S(1)} %get-tuple-element.26), channel_id=1, source_target_pairs={{0,5},{1,4},{2,7},{3,6},{4,1},{5,0},{6,3},{7,2},{8,13},{9,12},{10,... | collective-permute-start | bytes 196616 | tf_op jit(solution)/shard_map/ppermute | solution.py:298
  190.0 7.3 %collective-permute-start.18 = (bf16[16,2048]{1,0:T(8,128)(2,1)S(1)}, bf16[16,2048]{1,0:T(8,128)(2,1)S(1)}, u32[]{:S(2)}, u32[]{:S(2)}) collective-permute-start(bf16[16,2048]{1,0:T(8,128)(2,1)S(1)} %get-tuple-element.27), channel_id=1, source_target_pairs={{0,4},{1,5},{2,6},{3,7},{4,0},{5,1},{6,2},{7,3},{8,12},{9,13},{10,... | collective-permute-start | bytes 196616 | tf_op jit(solution)/shard_map/ppermute | solution.py:298
  202.2 8.1 %collective-permute-start.23 = (bf16[16,2176]{1,0:T(8,128)(2,1)S(1)}, bf16[16,2176]{1,0:T(8,128)(2,1)S(1)}, u32[]{:S(2)}, u32[]{:S(2)}) collective-permute-start(bf16[16,2176]{1,0:T(8,128)(2,1)S(1)} %fusion.19.refs_0_), channel_id=1, source_target_pairs={{0,2},{1,3},{2,0},{3,1},{4,6},{5,7},{6,4},{7,5},{8,10},{9,11},{10,... | collective-permute-start | bytes 208904 | tf_op jit(solution)/shard_map/ppermute | solution.py:331
  204.4 8.6 %collective-permute-start.24 = (bf16[16,2176]{1,0:T(8,128)(2,1)S(1)}, bf16[16,2176]{1,0:T(8,128)(2,1)S(1)}, u32[]{:S(2)}, u32[]{:S(2)}) collective-permute-start(bf16[16,2176]{1,0:T(8,128)(2,1)S(1)} %fusion.19.refs_0_), channel_id=1, source_target_pairs={{0,3},{1,2},{2,1},{3,0},{4,7},{5,6},{6,5},{7,4},{8,11},{9,10},{10,... | collective-permute-start | bytes 208904 | tf_op jit(solution)/shard_map/ppermute | solution.py:331
  205.9 7.1 %collective-permute-start.25 = (bf16[16,2176]{1,0:T(8,128)(2,1)S(1)}, bf16[16,2176]{1,0:T(8,128)(2,1)S(1)}, u32[]{:S(2)}, u32[]{:S(2)}) collective-permute-start(bf16[16,2176]{1,0:T(8,128)(2,1)S(1)} %fusion.19.refs_0_), channel_id=1, source_target_pairs={{0,4},{1,5},{2,6},{3,7},{4,0},{5,1},{6,2},{7,3},{8,12},{9,13},{10,... | collective-permute-start | bytes 208904 | tf_op jit(solution)/shard_map/ppermute | solution.py:331
  207.2 6.7 %collective-permute-start.27 = (bf16[16,2176]{1,0:T(8,128)(2,1)S(1)}, bf16[16,2176]{1,0:T(8,128)(2,1)S(1)}, u32[]{:S(2)}, u32[]{:S(2)}) collective-permute-start(bf16[16,2176]{1,0:T(8,128)(2,1)S(1)} %fusion.19.refs_0_), channel_id=1, source_target_pairs={{0,6},{1,7},{2,4},{3,5},{4,2},{5,3},{6,0},{7,1},{8,14},{9,15},{10,... | collective-permute-start | bytes 208904 | tf_op jit(solution)/shard_map/ppermute | solution.py:331
  210.3 6.4 %collective-permute-start.28 = (bf16[16,2176]{1,0:T(8,128)(2,1)S(1)}, bf16[16,2176]{1,0:T(8,128)(2,1)S(1)}, u32[]{:S(2)}, u32[]{:S(2)}) collective-permute-start(bf16[16,2176]{1,0:T(8,128)(2,1)S(1)} %fusion.19.refs_0_), channel_id=1, source_target_pairs={{0,7},{1,6},{2,5},{3,4},{4,3},{5,2},{6,1},{7,0},{8,15},{9,14},{10,... | collective-permute-start | bytes 208904 | tf_op jit(solution)/shard_map/ppermute | solution.py:331
  220.0 44.1 %all-to-all-start = ((bf16[32,16,1024]{2,1,0:T(8,128)(2,1)}), bf16[32,16,1024]{2,1,0:T(8,128)(2,1)S(1)}, u32[]{:S(2)}, u32[]{:S(2)}) async-start(bf16[32,16,1024]{2,1,0:T(8,128)(2,1)} %shard_map.121), calls=%async_computation | async-start | bytes 2097152 | tf_op jit(solution)/shard_map/all_to_all | solution.py:334
  236.9 29.9 %collective-permute-start.30 = (bf16[1024,768]{1,0:T(8,128)(2,1)S(1)}, bf16[1024,768]{1,0:T(8,128)(2,1)}, u32[]{:S(2)}, u32[]{:S(2)}) collective-permute-start(bf16[1024,768]{1,0:T(8,128)(2,1)S(1)} %pad_maximum_fusion.1), channel_id=1, source_target_pairs={{0,8},{8,0},{1,9},{9,1},{2,10},{10,2},{3,11},{11,3},{4,12},{12,4},... | collective-permute-start | bytes 4718600 | tf_op jit(solution)/shard_map/ppermute | solution.py:29
  275.4 36.1 %all-to-all-start.2 = ((bf16[256,2,1024]{2,1,0:T(2,128)(2,1)}), bf16[256,2,1024]{2,1,0:T(2,128)(2,1)S(1)}, u32[]{:S(2)}, u32[]{:S(2)}) async-start(bf16[256,2,1024]{2,1,0:T(2,128)(2,1)} %reshape.97), calls=%async_computation.2 | async-start | bytes 2097152 | tf_op jit(solution)/shard_map/all_to_all | solution.py:359
  (39 other events, 486.1 us)

commit v7 on v6

--- a/solution.py
+++ b/solution.py
@@ -213,6 +213,76 @@
     )(exp[None].astype(jnp.int32), *blocks)
 
 
+def down_kernel(act_ref, act_other_ref, own_ref, other_ref, o_ref):
+    dims = (((1,), (1,)), ((), ()))
+    out = lax.dot_general(act_ref[...], own_ref[...], dims, preferred_element_type=jnp.float32)
+    out = out + lax.dot_general(
+        act_other_ref[...], other_ref[...], dims, preferred_element_type=jnp.float32
+    )
+    o_ref[...] = out.astype(o_ref.dtype).reshape(o_ref.shape)
+
+
+def project_down(act, act_other, own, other):
+    slots, half = act.shape
+    step = slots // 4
+    rows = pl.BlockSpec((step, half), lambda i: (i, 0))
+    whole = pl.BlockSpec(own.shape, lambda i: (0, 0))
+    return pl.pallas_call(
+        down_kernel,
+        out_shape=jax.ShapeDtypeStruct((slots // CAP, CAP, HALF), jnp.bfloat16),
+        grid=(4,),
+        in_specs=[rows, rows, whole, whole],
+        out_specs=pl.BlockSpec((step // CAP, CAP, HALF), lambda i: (i, 0, 0)),
+        cost_estimate=pl.CostEstimate(
+            flops=4 * slots * half * HALF, bytes_accessed=3407872, transcendentals=0
+        ),
+    )(act, act_other, own, other)
+
+
+def combine_kernel(gates_ref, home_ref, low_ref, high_ref, o_ref):
+    wide = low_ref.shape[1]
+    planes = []
+    for plane, resid_ref in enumerate((low_ref, high_ref)):
+        x = jnp.concatenate(
+            [
+                home_ref[(2 * k + plane) * 8 : (2 * k + plane + 1) * 8, :, :].reshape(16, wide)
+                for k in range(OWN)
+            ],
+            axis=0,
+        )
+        moe = jnp.dot(gates_ref[...], x, preferred_element_type=jnp.float32)
+        planes.append(resid_ref[...] + moe)
+    lane = lax.broadcasted_iota(jnp.int32, (16, 128), 1)
+    for j in range(wide // 128):
+        low = planes[0][:, j * 128 : (j + 1) * 128]
+        high = planes[1][:, j * 128 : (j + 1) * 128]
+        o_ref[:, 2 * j * 128 : (2 * j + 1) * 128] = jnp.where(
+            lane < 64, low, pltpu.roll(high, 64, 1)
+        )
+        o_ref[:, (2 * j + 1) * 128 : (2 * j + 2) * 128] = jnp.where(
+            lane < 64, pltpu.roll(low, 64, 1), high
+        )
+
+
+def combined(gates, home, resid):
+    rows = resid.shape[0]
+    return pl.pallas_call(
+        combine_kernel,
+        out_shape=jax.ShapeDtypeStruct(resid.shape, jnp.float32),
+        grid=(4,),
+        in_specs=[
+            pl.BlockSpec(gates.shape, lambda i: (0, 0)),
+            pl.BlockSpec((256, CAP, HALF // 4), lambda i: (0, 0, i)),
+            pl.BlockSpec((rows, HALF // 4), lambda i: (0, i)),
+            pl.BlockSpec((rows, HALF // 4), lambda i: (0, i + 4)),
+        ],
+        out_specs=pl.BlockSpec((rows, HALF // 2), lambda i: (0, i)),
+        cost_estimate=pl.CostEstimate(
+            flops=2 * 16 * 512 * HALF, bytes_accessed=1318912, transcendentals=0
+        ),
+    )(gates, home, resid, resid)
+
+
 def across_y(x):
     return lax.ppermute(x, "yh", SWAP)
 
@@ -229,11 +299,6 @@
 def by_plane(x):
     rows = x.shape[0]
     return x.reshape(rows, D // 128, 2, 64).transpose(0, 2, 1, 3).reshape(rows, D)
-
-
-def from_planes(x):
-    rows = x.shape[0]
-    return x.reshape(rows, 2, D // 128, 64).transpose(0, 2, 1, 3).reshape(rows, D)
 
 
 def shards(
@@ -350,16 +415,9 @@
     hidden, tokens_other = lax.optimization_barrier((hidden, tokens_other))
     hidden = hidden + jnp.dot(tokens_other, other_w, preferred_element_type=jnp.float32)
     act = (jax.nn.silu(hidden[:, :half]) * hidden[:, half:]).astype(jnp.bfloat16)
-    dims = (((1,), (1,)), ((), ()))
-    act_other = swapped(act)
-    out = lax.dot_general(act, own_down, dims, preferred_element_type=jnp.float32)
-    out, act_other = lax.optimization_barrier((out, act_other))
-    out = out + lax.dot_general(act_other, other_down, dims, preferred_element_type=jnp.float32)
-    out = out.astype(jnp.bfloat16)
-    home = lax.all_to_all(out.reshape(256, CAP, HALF), ALL, 0, 0, tiled=True)
-    home = home.reshape(OWN, 2, 8, CAP, HALF).transpose(0, 2, 3, 1, 4).reshape(EXPERTS * CAP, D)
-    moe = jnp.dot(combine, home, preferred_element_type=jnp.float32)
-    return from_planes(resid + moe)
+    out = project_down(act, swapped(act), own_down, other_down)
+    home = lax.all_to_all(out, ALL, 0, 0, tiled=True)
+    return combined(combine, home, resid)
 
 
 def solution(mesh):

time: 316 us -> 320 us (1.013)
  Pallas kernels: 17.4 us -> 26.3 us
  matrix products: 8.67 us -> 4.67 us
    pallas_call x0 -> x2, Pallas kernels: none -> 8.91 us  [the longest x1 5.17 us: project_down(): pl.pallas_call(down_kernel, out_shape=jax.ShapeDtypeStruct((slots // CAP,...]
    ppermute x1, waiting for transfers between devices: 4.4 us -> 0.01 us  [across_xy(): return lax.ppermute(x, ('yh', 'exp'), pairs)]
    dot_general x3 -> x0, matrix products: 4 us -> none  [the longest x1 1.88 us: shards(): lax.dot_general(act_other, other_down, dims, preferred_element_type=jnp.f...]
    unnamed x59 -> x66, local copies, waits for them, and re-layouts: 4.86 us -> 6.59 us
  transfers between devices with their start and end apart: 35 -> 35, of which waited for: 12 -> 15; matrix products, arithmetic and copies ran while one was open for 4% -> 4% of each run, Pallas kernels for 6% -> 5%
where the time goes in v7:
time: 320 us; the launch traced here: 318 us
  waiting for transfers between devices  194 us (61%)
  starting transfers between devices  72.5 us (23%)
  Pallas kernels  26.3 us (8%)
  local copies, waits for them, and re-layouts  12.3 us (4%)
  other arithmetic  7.89 us (2%)
  matrix products  4.67 us (1%)
    ppermute x1, waiting for transfers between devices, shards(): lax.ppermute(packed, 'z', [((i + 4) % 8, i) for i in range(8)])  117 us
    all_to_all x1, waiting for transfers between devices, shards(): home = lax.all_to_all(out, ALL, 0, 0, tiled=True)  30 us
    all_to_all x1, waiting for transfers between devices, shards(): tokens = lax.all_to_all(outgoing, CTX, 0, 0, tiled=True).reshape(512, HALF)  26.1 us
    all_to_all x1, starting transfers between devices, shards(): tokens = lax.all_to_all(outgoing, CTX, 0, 0, tiled=True).reshape(512, HALF)  13.3 us
    ppermute x7, starting transfers between devices, shards(): got = lax.ppermute(sent, 'exp', [(e, e ^ d) for e in range(8)])  11.9 us
    ppermute x7, starting transfers between devices, shards(): lax.ppermute(payload, 'exp', [(e, e ^ d) for e in range(8)])  11.8 us
    all_to_all x1, starting transfers between devices, shards(): lax.all_to_all(jnp.concatenate([w_gate, w_up, w_down], axis=2), CHIP, 0,...  11.3 us
    pallas_call x1, Pallas kernels, attend(): pl.pallas_call(attend_kernel, out_shape=jax.ShapeDtypeStruct((rows, width...  9.17 us
  transfers between devices with their start and end apart: 35, of which 15 were waited for; matrix products, arithmetic and copies ran while one was open for 4% of the time, Pallas kernels for 5%

profile of v7, /device:TPU:32, one launch (start us, length us, event | category | flops | bytes accessed | tf_op | source)
XLA Modules:
  0.0 318.2 jit_solution(13634094171749215165)
XLA Ops:
  0.0 3.9 %pad_maximum_fusion = bf16[16,64,2304]{2,1,0:T(8,128)(2,1)} fusion(bf16[16,64,768]{2,1,0:T(8,128)(2,1)} %param.23, bf16[16,64,768]{2,1,0:T(8,128)(2,1)} %param.22, bf16[16,64,768]{2,1,0:T(8,128)(2,1)} %param.21), kind=kLoop, calls=%fused_computation | loop fusion | flops 14155776 | bytes 9437184 | tf_op jit(solution)/shard_map/concatenate | solution.py:343
  4.0 11.3 %all-to-all-start.1 = ((bf16[16,64,2304]{2,1,0:T(8,128)(2,1)}), bf16[16,64,2304]{2,1,0:T(8,128)(2,1)}, u32[]{:S(2)}, u32[]{:S(2)}) async-start(bf16[16,64,2304]{2,1,0:T(8,128)(2,1)} %pad_maximum_fusion), calls=%async_computation.1 | async-start | bytes 9437184 | tf_op jit(solution)/shard_map/all_to_all | solution.py:342
  17.9 4.0 %collective-permute-start.2 = (bf16[768,128]{1,0:T(8,128)(2,1)S(1)}, bf16[768,128]{1,0:T(8,128)(2,1)S(1)}, u32[]{:S(2)}, u32[]{:S(2)}) collective-permute-start(bf16[768,128]{1,0:T(8,128)(2,1)S(1)} %pad_maximum_fusion.2), channel_id=1, source_target_pairs={{32,0},{104,8},{48,16},{120,24},{64,32},{8,40},{80,48},{24,56},{96... | collective-permute-start | bytes 589832 | tf_op jit(solution)/shard_map/ppermute | solution.py:340
  24.2 2.7 collective-permute-start.4
  26.9 116.9 %collective-permute-done.4.refs_4_ = bf16[384,128]{1,0:T(8,128)(2,1)S(1)} collective-permute-done((bf16[384,128]{1,0:T(8,128)(2,1)S(1)}, bf16[384,128]{1,0:T(8,128)(2,1)S(1)}, u32[]{:S(2)}, u32[]{:S(2)}) %collective-permute-start.4) | collective-permute-done | bytes 98336 | tf_op jit(solution)/shard_map/ppermute | solution.py:341
  156.0 5.2 %collective-permute-done.12.refs_1_ = bf16[512,512]{1,0:T(8,128)(2,1)S(1)} collective-permute-done((bf16[512,512]{1,0:T(8,128)(2,1)}, bf16[512,512]{1,0:T(8,128)(2,1)S(1)}, u32[]{:S(2)}, u32[]{:S(2)}) %collective-permute-start.12) | collective-permute-done | bytes 524320 | tf_op jit(solution)/shard_map/ppermute | solution.py:287
  166.9 9.2 %shard_map.119.x_ref = bf16[128,512]{1,0:T(8,128)(2,1)} custom-call(s32[64]{0:T(128)} %span_ref.1, s32[2]{0:T(128)} %pad_add_fusion.where_ref, bf16[128,512]{1,0:T(8,128)(2,1)} %q_ref.1, bf16[1024,128]{1,0:T(8,128)(2,1)} %get-tuple-element.9.refs_0_, bf16[1024,128]{1,0:T(8,128)(2,1)} %copy-done.27, bf16[1024,128]{1,0:T(8,128)(2,1)} %copy-done.28, ...), custom_call_target="tpu_custom_call" | custom-call | flops 1073741824 | bytes 2359296 | tf_op jit(solution)/shard_map/pallas_call | solution.py:94
  177.7 3.3 %shard_map.120 = bf16[128,2048]{1,0:T(8,128)(2,1)} custom-call(s32[1]{0:T(128)} %bitcast.2.ctx_ref, bf16[128,512]{1,0:T(8,128)(2,1)} %shard_map.119.x_ref, bf16[512,512]{1,0:T(8,128)(2,1)} %get-tuple-element.10.refs_0_, bf16[512,512]{1,0:T(8,128)(2,1)} %copy-done.3, bf16[512,512]{1,0:T(8,128)(2,1)} %copy-done.4, bf16[512,512]{1,0:T(8,128)(2,1)} %copy-done.5), custom_call_target="tpu_custom_call" | custom-call | flops 268435456 | bytes 2752512 | tf_op jit(solution)/shard_map/pallas_call | solution.py:162
  183.7 2.7 collective-permute-start.16
  189.0 4.0 %collective-permute-start.20 = (bf16[16,2048]{1,0:T(8,128)(2,1)S(1)}, bf16[16,2048]{1,0:T(8,128)(2,1)S(1)}, u32[]{:S(2)}, u32[]{:S(2)}) collective-permute-start(bf16[16,2048]{1,0:T(8,128)(2,1)S(1)} %get-tuple-element.23), channel_id=1, source_target_pairs={{0,6},{1,7},{2,4},{3,5},{4,2},{5,3},{6,0},{7,1},{8,14},{9,15},{10,... | collective-permute-start | bytes 196616 | tf_op jit(solution)/shard_map/ppermute | solution.py:363
  196.0 3.4 %collective-permute-done.21 = bf16[16,2048]{1,0:T(8,128)(2,1)S(1)} collective-permute-done((bf16[16,2048]{1,0:T(8,128)(2,1)S(1)}, bf16[16,2048]{1,0:T(8,128)(2,1)S(1)}, u32[]{:S(2)}, u32[]{:S(2)}) %collective-permute-start.21) | collective-permute-done | bytes 65568 | tf_op jit(solution)/shard_map/ppermute | solution.py:363
  202.6 2.8 collective-permute-start.24
  206.7 2.8 collective-permute-start.27
  209.6 2.9 collective-permute-start.28
  213.5 2.5 collective-permute-done.28.refs_7_
  216.6 2.6 shard_map.121
  219.3 13.3 %all-to-all-start = ((bf16[32,16,1024]{2,1,0:T(8,128)(2,1)}), bf16[32,16,1024]{2,1,0:T(8,128)(2,1)S(1)}, u32[]{:S(2)}, u32[]{:S(2)}) async-start(bf16[32,16,1024]{2,1,0:T(8,128)(2,1)} %shard_map.121), calls=%async_computation | async-start | bytes 2097152 | tf_op jit(solution)/shard_map/all_to_all | solution.py:399
  232.6 4.0 %constant_dynamic-slice_fusion = (bf16[1024,384]{1,0:T(8,128)(2,1)}, bf16[1024,384]{1,0:T(8,128)(2,1)}, bf16[1024,384]{1,0:T(8,128)(2,1)S(1)}, bf16[1024,384]{1,...) fusion(bf16[1024,2304]{1,0:T(8,128)(2,1)} %bitcast.17, s32[]{:T(128)S(6)} %select_n.123, ...), kind=kLoop, calls=%fused_computation.57 | loop fusion | bytes 9437208 | tf_op jit(solution)/shard_map/dynamic_slice | solution.py:404
  236.9 26.1 %all-to-all-done = bf16[32,16,1024]{2,1,0:T(8,128)(2,1)S(1)} async-done(((bf16[32,16,1024]{2,1,0:T(8,128)(2,1)}), bf16[32,16,1024]{2,1,0:T(8,128)(2,1)S(1)}, u32[]{:S(2)}, u32[]{:S(2)}) %all-to-all-start) | async-done | bytes 1048608 | tf_op jit(solution)/shard_map/all_to_all | solution.py:399
  265.7 2.4 fusion.28
  271.1 5.2 %shard_map.122 = bf16[256,2,1024]{2,1,0:T(2,128)(2,1)} custom-call(bf16[512,384]{1,0:T(8,128)(2,1)} %copy-done.2, bf16[512,384]{1,0:T(8,128)(2,1)} %copy-done.7, bf16[1024,384]{1,0:T(8,128)(2,1)} %get-tuple-element.16.own_ref, bf16[1024,384]{1,0:T(8,128)(2,1)} %get-tuple-element.15.other_ref), custom_call_target="tpu_custom_call" | custom-call | flops 805306368 | bytes 3407872 | tf_op jit(solution)/shard_map/pallas_call | solution.py:230
  276.3 6.3 %all-to-all-start.2 = ((bf16[256,2,1024]{2,1,0:T(2,128)(2,1)}), bf16[256,2,1024]{2,1,0:T(2,128)(2,1)S(1)}, u32[]{:S(2)}, u32[]{:S(2)}) async-start(bf16[256,2,1024]{2,1,0:T(2,128)(2,1)} %shard_map.122), calls=%async_computation.2 | async-start | bytes 2097152 | tf_op jit(solution)/shard_map/all_to_all | solution.py:419
  283.5 30.0 %all-to-all-done.2.home_ref = bf16[256,2,1024]{2,1,0:T(2,128)(2,1)S(1)} async-done(((bf16[256,2,1024]{2,1,0:T(2,128)(2,1)}), bf16[256,2,1024]{2,1,0:T(2,128)(2,1)S(1)}, u32[]{:S(2)}, u32[]{:S(2)}) %all-to-all-start.2) | async-done | bytes 1048608 | tf_op jit(solution)/shard_map/all_to_all | solution.py:419
  314.5 3.7 %shard_map.123 = f32[16,2048]{1,0:T(8,128)} custom-call(bf16[16,256]{1,0:T(8,128)(2,1)} %fusion.16.gates_ref, bf16[256,2,1024]{2,1,0:T(2,128)(2,1)} %copy-done, f32[16,2048]{1,0:T(8,128)} %copy-done.1, f32[16,2048]{1,0:T(8,128)} %copy-done.1), custom_call_target="tpu_custom_call" | custom-call | flops 16777216 | bytes 1318912 | tf_op jit(solution)/shard_map/pallas_call | solution.py:269
  (147 shorter events, 46.4 us)
Async XLA Ops:
  4.0 215.3 %all-to-all-start.1 = ((bf16[16,64,2304]{2,1,0:T(8,128)(2,1)}), bf16[16,64,2304]{2,1,0:T(8,128)(2,1)}, u32[]{:S(2)}, u32[]{:S(2)}) async-start(bf16[16,64,2304]{2,1,0:T(8,128)(2,1)} %pad_maximum_fusion), calls=%async_computation.1 | async-start | bytes 9437184 | tf_op jit(solution)/shard_map/all_to_all | solution.py:342
  17.6 126.1 %collective-permute-start.1 = (bf16[768,128]{1,0:T(8,128)(2,1)S(1)}, bf16[768,128]{1,0:T(8,128)(2,1)S(1)}, u32[]{:S(2)}, u32[]{:S(2)}) collective-permute-start(bf16[768,128]{1,0:T(8,128)(2,1)S(1)} %pad_maximum_fusion.2), channel_id=1, source_target_pairs={{16,0},{120,8},{32,16},{8,24},{48,32},{24,40},{64,48},{40,56},{80,... | collective-permute-start | bytes 589832 | tf_op jit(solution)/shard_map/ppermute | solution.py:340
  17.9 125.9 %collective-permute-start.2 = (bf16[768,128]{1,0:T(8,128)(2,1)S(1)}, bf16[768,128]{1,0:T(8,128)(2,1)S(1)}, u32[]{:S(2)}, u32[]{:S(2)}) collective-permute-start(bf16[768,128]{1,0:T(8,128)(2,1)S(1)} %pad_maximum_fusion.2), channel_id=1, source_target_pairs={{32,0},{104,8},{48,16},{120,24},{64,32},{8,40},{80,48},{24,56},{96... | collective-permute-start | bytes 589832 | tf_op jit(solution)/shard_map/ppermute | solution.py:340
  21.8 121.9 %collective-permute-start.3 = (bf16[768,128]{1,0:T(8,128)(2,1)S(1)}, bf16[768,128]{1,0:T(8,128)(2,1)S(1)}, u32[]{:S(2)}, u32[]{:S(2)}) collective-permute-start(bf16[768,128]{1,0:T(8,128)(2,1)S(1)} %pad_maximum_fusion.2), channel_id=1, source_target_pairs={{48,0},{88,8},{64,16},{104,24},{80,32},{120,40},{96,48},{8,56},{11... | collective-permute-start | bytes 589832 | tf_op jit(solution)/shard_map/ppermute | solution.py:340
  24.2 119.5 %collective-permute-start.4 = (bf16[384,128]{1,0:T(8,128)(2,1)S(1)}, bf16[384,128]{1,0:T(8,128)(2,1)S(1)}, u32[]{:S(2)}, u32[]{:S(2)}) collective-permute-start(bf16[384,128]{1,0:T(8,128)(2,1)S(1)} %pad_maximum_fusion.3.refs_0_), channel_id=1, source_target_pairs={{64,0},{80,16},{96,32},{112,48},{0,64},{16,80},{32,96},{48,112},{6... | collective-permute-start | bytes 294920 | tf_op jit(solution)/shard_map/ppermute | solution.py:341
  147.5 13.7 %collective-permute-start.12 = (bf16[512,512]{1,0:T(8,128)(2,1)}, bf16[512,512]{1,0:T(8,128)(2,1)S(1)}, u32[]{:S(2)}, u32[]{:S(2)}) collective-permute-start(bf16[512,512]{1,0:T(8,128)(2,1)} %get-tuple-element.10.refs_0_), channel_id=1, source_target_pairs={{0,128},{128,0},{1,129},{129,1},{2,130},{130,2},{3,131},{131,3},{4... | collective-permute-start | bytes 1572872 | tf_op jit(solution)/shard_map/ppermute | solution.py:287
  150.9 10.3 %collective-permute-start.9 = (bf16[1024,128]{1,0:T(8,128)(2,1)}, bf16[1024,128]{1,0:T(8,128)(2,1)S(1)}, u32[]{:S(2)}, u32[]{:S(2)}) collective-permute-start(bf16[1024,128]{1,0:T(8,128)(2,1)} %get-tuple-element.9.refs_0_), channel_id=1, source_target_pairs={{0,129},{1,128},{2,131},{3,130},{4,133},{5,132},{6,135},{7,134},{1... | collective-permute-start | bytes 786440 | tf_op jit(solution)/shard_map/ppermute | solution.py:296
  152.4 11.5 %collective-permute-start.5 = (bf16[1024,128]{1,0:T(8,128)(2,1)}, bf16[1024,128]{1,0:T(8,128)(2,1)S(1)}, u32[]{:S(2)}, u32[]{:S(2)}) collective-permute-start(bf16[1024,128]{1,0:T(8,128)(2,1)} %get-tuple-element.9.refs_0_), channel_id=1, source_target_pairs={{0,128},{128,0},{1,129},{129,1},{2,130},{130,2},{3,131},{131,3},{4... | collective-permute-start | bytes 786440 | tf_op jit(solution)/shard_map/ppermute | solution.py:287
  154.4 9.6 %collective-permute-start.6 = (bf16[1024,128]{1,0:T(8,128)(2,1)}, bf16[1024,128]{1,0:T(8,128)(2,1)S(1)}, u32[]{:S(2)}, u32[]{:S(2)}) collective-permute-start(bf16[1024,128]{1,0:T(8,128)(2,1)} %get-tuple-element.9.refs_0_), channel_id=1, source_target_pairs={{0,8},{8,0},{1,9},{9,1},{2,10},{10,2},{3,11},{11,3},{4,12},{12,4},... | collective-permute-start | bytes 786440 | tf_op jit(solution)/shard_map/ppermute | solution.py:29
  156.0 20.1 %collective-permute-start.13 = (bf16[512,512]{1,0:T(8,128)(2,1)}, bf16[512,512]{1,0:T(8,128)(2,1)S(1)}, u32[]{:S(2)}, u32[]{:S(2)}) collective-permute-start(bf16[512,512]{1,0:T(8,128)(2,1)} %get-tuple-element.10.refs_0_), channel_id=1, source_target_pairs={{0,8},{8,0},{1,9},{9,1},{2,10},{10,2},{3,11},{11,3},{4,12},{12,4},... | collective-permute-start | bytes 1572872 | tf_op jit(solution)/shard_map/ppermute | solution.py:29
  161.2 15.0 %collective-permute-start.14 = (bf16[512,512]{1,0:T(8,128)(2,1)S(1)}, bf16[512,512]{1,0:T(8,128)(2,1)S(1)}, u32[]{:S(2)}, u32[]{:S(2)}) collective-permute-start(bf16[512,512]{1,0:T(8,128)(2,1)S(1)} %collective-permute-done.12.refs_1_), channel_id=1, source_target_pairs={{0,8},{8,0},{1,9},{9,1},{2,10},{10,2},{3,11},{11,3},{4,12},{12,4},... | collective-permute-start | bytes 1572872 | tf_op jit(solution)/shard_map/ppermute | solution.py:29
  182.1 6.9 %collective-permute-start.15 = (bf16[16,2048]{1,0:T(8,128)(2,1)S(1)}, bf16[16,2048]{1,0:T(8,128)(2,1)S(1)}, u32[]{:S(2)}, u32[]{:S(2)}) collective-permute-start(bf16[16,2048]{1,0:T(8,128)(2,1)S(1)} %get-tuple-element.21), channel_id=1, source_target_pairs={{0,1},{1,0},{2,3},{3,2},{4,5},{5,4},{6,7},{7,6},{8,9},{9,8},{10,11... | collective-permute-start | bytes 196616 | tf_op jit(solution)/shard_map/ppermute | solution.py:363
  183.7 9.3 %collective-permute-start.16 = (bf16[16,2048]{1,0:T(8,128)(2,1)S(1)}, bf16[16,2048]{1,0:T(8,128)(2,1)S(1)}, u32[]{:S(2)}, u32[]{:S(2)}) collective-permute-start(bf16[16,2048]{1,0:T(8,128)(2,1)S(1)} %get-tuple-element.27), channel_id=1, source_target_pairs={{0,2},{1,3},{2,0},{3,1},{4,6},{5,7},{6,4},{7,5},{8,10},{9,11},{10,... | collective-permute-start | bytes 196616 | tf_op jit(solution)/shard_map/ppermute | solution.py:363
  186.7 8.2 %collective-permute-start.17 = (bf16[16,2048]{1,0:T(8,128)(2,1)S(1)}, bf16[16,2048]{1,0:T(8,128)(2,1)S(1)}, u32[]{:S(2)}, u32[]{:S(2)}) collective-permute-start(bf16[16,2048]{1,0:T(8,128)(2,1)S(1)} %get-tuple-element.26), channel_id=1, source_target_pairs={{0,3},{1,2},{2,1},{3,0},{4,7},{5,6},{6,5},{7,4},{8,11},{9,10},{10,... | collective-permute-start | bytes 196616 | tf_op jit(solution)/shard_map/ppermute | solution.py:363
  187.2 7.6 %collective-permute-start.18 = (bf16[16,2048]{1,0:T(8,128)(2,1)S(1)}, bf16[16,2048]{1,0:T(8,128)(2,1)S(1)}, u32[]{:S(2)}, u32[]{:S(2)}) collective-permute-start(bf16[16,2048]{1,0:T(8,128)(2,1)S(1)} %get-tuple-element.25), channel_id=1, source_target_pairs={{0,4},{1,5},{2,6},{3,7},{4,0},{5,1},{6,2},{7,3},{8,12},{9,13},{10,... | collective-permute-start | bytes 196616 | tf_op jit(solution)/shard_map/ppermute | solution.py:363
  187.9 7.0 %collective-permute-start.19 = (bf16[16,2048]{1,0:T(8,128)(2,1)S(1)}, bf16[16,2048]{1,0:T(8,128)(2,1)S(1)}, u32[]{:S(2)}, u32[]{:S(2)}) collective-permute-start(bf16[16,2048]{1,0:T(8,128)(2,1)S(1)} %get-tuple-element.24), channel_id=1, source_target_pairs={{0,5},{1,4},{2,7},{3,6},{4,1},{5,0},{6,3},{7,2},{8,13},{9,12},{10,... | collective-permute-start | bytes 196616 | tf_op jit(solution)/shard_map/ppermute | solution.py:363
  189.0 7.0 %collective-permute-start.20 = (bf16[16,2048]{1,0:T(8,128)(2,1)S(1)}, bf16[16,2048]{1,0:T(8,128)(2,1)S(1)}, u32[]{:S(2)}, u32[]{:S(2)}) collective-permute-start(bf16[16,2048]{1,0:T(8,128)(2,1)S(1)} %get-tuple-element.23), channel_id=1, source_target_pairs={{0,6},{1,7},{2,4},{3,5},{4,2},{5,3},{6,0},{7,1},{8,14},{9,15},{10,... | collective-permute-start | bytes 196616 | tf_op jit(solution)/shard_map/ppermute | solution.py:363
  200.7 8.9 %collective-permute-start.23 = (bf16[16,2176]{1,0:T(8,128)(2,1)S(1)}, bf16[16,2176]{1,0:T(8,128)(2,1)S(1)}, u32[]{:S(2)}, u32[]{:S(2)}) collective-permute-start(bf16[16,2176]{1,0:T(8,128)(2,1)S(1)} %fusion.15.refs_0_), channel_id=1, source_target_pairs={{0,2},{1,3},{2,0},{3,1},{4,6},{5,7},{6,4},{7,5},{8,10},{9,11},{10,... | collective-permute-start | bytes 208904 | tf_op jit(solution)/shard_map/ppermute | solution.py:396
  202.6 9.8 %collective-permute-start.24 = (bf16[16,2176]{1,0:T(8,128)(2,1)S(1)}, bf16[16,2176]{1,0:T(8,128)(2,1)S(1)}, u32[]{:S(2)}, u32[]{:S(2)}) collective-permute-start(bf16[16,2176]{1,0:T(8,128)(2,1)S(1)} %fusion.15.refs_0_), channel_id=1, source_target_pairs={{0,3},{1,2},{2,1},{3,0},{4,7},{5,6},{6,5},{7,4},{8,11},{9,10},{10,... | collective-permute-start | bytes 208904 | tf_op jit(solution)/shard_map/ppermute | solution.py:396
  205.4 7.1 %collective-permute-start.25 = (bf16[16,2176]{1,0:T(8,128)(2,1)S(1)}, bf16[16,2176]{1,0:T(8,128)(2,1)S(1)}, u32[]{:S(2)}, u32[]{:S(2)}) collective-permute-start(bf16[16,2176]{1,0:T(8,128)(2,1)S(1)} %fusion.15.refs_0_), channel_id=1, source_target_pairs={{0,4},{1,5},{2,6},{3,7},{4,0},{5,1},{6,2},{7,3},{8,12},{9,13},{10,... | collective-permute-start | bytes 208904 | tf_op jit(solution)/shard_map/ppermute | solution.py:396
  206.7 6.8 %collective-permute-start.27 = (bf16[16,2176]{1,0:T(8,128)(2,1)S(1)}, bf16[16,2176]{1,0:T(8,128)(2,1)S(1)}, u32[]{:S(2)}, u32[]{:S(2)}) collective-permute-start(bf16[16,2176]{1,0:T(8,128)(2,1)S(1)} %fusion.15.refs_0_), channel_id=1, source_target_pairs={{0,6},{1,7},{2,4},{3,5},{4,2},{5,3},{6,0},{7,1},{8,14},{9,15},{10,... | collective-permute-start | bytes 208904 | tf_op jit(solution)/shard_map/ppermute | solution.py:396
  219.3 43.8 %all-to-all-start = ((bf16[32,16,1024]{2,1,0:T(8,128)(2,1)}), bf16[32,16,1024]{2,1,0:T(8,128)(2,1)S(1)}, u32[]{:S(2)}, u32[]{:S(2)}) async-start(bf16[32,16,1024]{2,1,0:T(8,128)(2,1)} %shard_map.121), calls=%async_computation | async-start | bytes 2097152 | tf_op jit(solution)/shard_map/all_to_all | solution.py:399
  236.7 29.0 %collective-permute-start.30 = (bf16[1024,768]{1,0:T(8,128)(2,1)S(1)}, bf16[1024,768]{1,0:T(8,128)(2,1)}, u32[]{:S(2)}, u32[]{:S(2)}) collective-permute-start(bf16[1024,768]{1,0:T(8,128)(2,1)S(1)} %pad_maximum_fusion.1), channel_id=1, source_target_pairs={{0,8},{8,0},{1,9},{9,1},{2,10},{10,2},{3,11},{11,3},{4,12},{12,4},... | collective-permute-start | bytes 4718600 | tf_op jit(solution)/shard_map/ppermute | solution.py:29
  276.3 37.1 %all-to-all-start.2 = ((bf16[256,2,1024]{2,1,0:T(2,128)(2,1)}), bf16[256,2,1024]{2,1,0:T(2,128)(2,1)S(1)}, u32[]{:S(2)}, u32[]{:S(2)}) async-start(bf16[256,2,1024]{2,1,0:T(2,128)(2,1)} %shard_map.122), calls=%async_computation.2 | async-start | bytes 2097152 | tf_op jit(solution)/shard_map/all_to_all | solution.py:419
  (43 other events, 479.2 us)

commit v8 on v6

--- a/solution.py
+++ b/solution.py
@@ -146,33 +146,38 @@
 
 
 def project_kernel(ctx_ref, x_ref, *refs):
-    weights, (o_ref, w_ref) = refs[:4], refs[4:]
+    weights, outs, (w_ref, out_ref) = refs[:4], refs[4:12], refs[12:]
     for side, w in enumerate(weights):
         for b in range(8):
             plane, half, z = block_of(ctx_ref[0], side, b)
             at = pl.multiple_of(plane * HALF + half * (HALF // 2) + z * 64, 64)
             w_ref[pl.ds(at, 64), :] = w[b * 64 : (b + 1) * 64, :]
-    out = lax.dot_general(
+    out_ref[...] = lax.dot_general(
         x_ref[...], w_ref[...], (((1,), (1,)), ((), ())), preferred_element_type=jnp.float32
     )
-    o_ref[...] = out.astype(o_ref.dtype)
-
-
-def project(ctx, x, weights):
+    for d, o_ref in enumerate(outs):
+        at = pl.multiple_of(jnp.bitwise_xor(ctx_ref[1], d) * 16, 16)
+        o_ref[...] = out_ref[pl.ds(at, 16), :].astype(o_ref.dtype)
+
+
+def project(where, x, weights):
     return pl.pallas_call(
         project_kernel,
-        out_shape=jax.ShapeDtypeStruct((x.shape[0], D), jnp.bfloat16),
+        out_shape=(jax.ShapeDtypeStruct((16, D), jnp.bfloat16),) * 8,
         grid_spec=pltpu.PrefetchScalarGridSpec(
             num_scalar_prefetch=1,
             grid=(1,),
             in_specs=[pl.BlockSpec(a.shape, lambda i, *_: (0, 0)) for a in [x, *weights]],
-            out_specs=pl.BlockSpec((x.shape[0], D), lambda i, *_: (0, 0)),
-            scratch_shapes=[pltpu.VMEM((D, x.shape[1]), jnp.bfloat16)],
+            out_specs=(pl.BlockSpec((16, D), lambda i, *_: (0, 0)),) * 8,
+            scratch_shapes=[
+                pltpu.VMEM((D, x.shape[1]), jnp.bfloat16),
+                pltpu.VMEM((x.shape[0], D), jnp.float32),
+            ],
         ),
         cost_estimate=pl.CostEstimate(
             flops=2 * x.shape[0] * x.shape[1] * D, bytes_accessed=2752512, transcendentals=0
         ),
-    )(ctx[None].astype(jnp.int32), x, *weights)
+    )(where, x, *weights)
 
 
 def place_kernel(exp_ref, *refs):
@@ -291,11 +296,11 @@
         near[0:2] + far[0:2],
         near[2:4] + far[2:4],
     )
-    mixed = project(ctx, attended, wo_near + wo_far).reshape(8, 16, D)
-    summed = lax.dynamic_index_in_dim(mixed, exp, 0, False).astype(jnp.float32)
+    where = jnp.stack([ctx, exp]).astype(jnp.int32)
+    mixed = project(where, attended, wo_near + wo_far)
+    summed = mixed[0].astype(jnp.float32)
     for d in range(1, 8):
-        sent = lax.dynamic_index_in_dim(mixed, exp ^ d, 0, False)
-        got = lax.ppermute(sent, "exp", [(e, e ^ d) for e in range(8)])
+        got = lax.ppermute(mixed[d], "exp", [(e, e ^ d) for e in range(8)])
         summed = summed + got.astype(jnp.float32)
     resid = by_plane(stream_in.astype(jnp.float32)) + summed
     gain = by_plane(norm_gain.astype(jnp.float32)[None])

time: 316 us -> 316 us (level)
  no operation moved by 1% of the time
where the time goes in v8:
time: 316 us; the launch traced here: 314 us
  waiting for transfers between devices  195 us (62%)
  starting transfers between devices  70.8 us (22%)
  Pallas kernels  18.1 us (6%)
  local copies, waits for them, and re-layouts  13 us (4%)
  matrix products  8.67 us (3%)
  other arithmetic  8.31 us (3%)
    ppermute x1, waiting for transfers between devices, shards(): lax.ppermute(packed, 'z', [((i + 4) % 8, i) for i in range(8)])  117 us
    all_to_all x1, waiting for transfers between devices, shards(): home = lax.all_to_all(out.reshape(256, CAP, HALF), ALL, 0, 0, tiled=True)  30.6 us
    all_to_all x1, waiting for transfers between devices, shards(): tokens = lax.all_to_all(outgoing, CTX, 0, 0, tiled=True).reshape(512, HALF)  27.1 us
    all_to_all x1, starting transfers between devices, shards(): tokens = lax.all_to_all(outgoing, CTX, 0, 0, tiled=True).reshape(512, HALF)  12.9 us
    ppermute x7, starting transfers between devices, shards(): lax.ppermute(payload, 'exp', [(e, e ^ d) for e in range(8)])  11.8 us
    ppermute x7, starting transfers between devices, shards(): got = lax.ppermute(mixed[d], 'exp', [(e, e ^ d) for e in range(8)])  11.7 us
    all_to_all x1, starting transfers between devices, shards(): lax.all_to_all(jnp.concatenate([w_gate, w_up, w_down], axis=2), CHIP, 0,...  11.3 us
    pallas_call x1, Pallas kernels, attend(): pl.pallas_call(attend_kernel, out_shape=jax.ShapeDtypeStruct((rows, width...  9.17 us
  transfers between devices with their start and end apart: 35, of which 12 were waited for; matrix products, arithmetic and copies ran while one was open for 4% of the time, Pallas kernels for 6%

profile of v8, /device:TPU:32, one launch (start us, length us, event | category | flops | bytes accessed | tf_op | source)
XLA Modules:
  0.0 314.4 jit_solution(13045765352182583136)
XLA Ops:
  0.0 4.0 %pad_maximum_fusion = bf16[16,64,2304]{2,1,0:T(8,128)(2,1)} fusion(bf16[16,64,768]{2,1,0:T(8,128)(2,1)} %param.23, bf16[16,64,768]{2,1,0:T(8,128)(2,1)} %param.22, bf16[16,64,768]{2,1,0:T(8,128)(2,1)} %param.21), kind=kLoop, calls=%fused_computation | loop fusion | flops 14155776 | bytes 9437184 | tf_op jit(solution)/shard_map/concatenate | solution.py:283
  4.0 11.3 %all-to-all-start.1 = ((bf16[16,64,2304]{2,1,0:T(8,128)(2,1)}), bf16[16,64,2304]{2,1,0:T(8,128)(2,1)}, u32[]{:S(2)}, u32[]{:S(2)}) async-start(bf16[16,64,2304]{2,1,0:T(8,128)(2,1)} %pad_maximum_fusion), calls=%async_computation.1 | async-start | bytes 9437184 | tf_op jit(solution)/shard_map/all_to_all | solution.py:282
  17.9 4.0 %collective-permute-start.2 = (bf16[768,128]{1,0:T(8,128)(2,1)S(1)}, bf16[768,128]{1,0:T(8,128)(2,1)S(1)}, u32[]{:S(2)}, u32[]{:S(2)}) collective-permute-start(bf16[768,128]{1,0:T(8,128)(2,1)S(1)} %pad_maximum_fusion.2), channel_id=1, source_target_pairs={{32,0},{104,8},{48,16},{120,24},{64,32},{8,40},{80,48},{24,56},{96... | collective-permute-start | bytes 589832 | tf_op jit(solution)/shard_map/ppermute | solution.py:280
  21.8 2.4 collective-permute-start.3
  24.2 2.7 collective-permute-start.4
  26.9 116.9 %collective-permute-done.4.refs_4_ = bf16[384,128]{1,0:T(8,128)(2,1)S(1)} collective-permute-done((bf16[384,128]{1,0:T(8,128)(2,1)S(1)}, bf16[384,128]{1,0:T(8,128)(2,1)S(1)}, u32[]{:S(2)}, u32[]{:S(2)}) %collective-permute-start.4) | collective-permute-done | bytes 98336 | tf_op jit(solution)/shard_map/ppermute | solution.py:281
  145.2 2.2 shard_map.118
  154.4 7.1 %collective-permute-done.5.refs_1_ = bf16[1024,128]{1,0:T(8,128)(2,1)S(1)} collective-permute-done((bf16[1024,128]{1,0:T(8,128)(2,1)}, bf16[1024,128]{1,0:T(8,128)(2,1)S(1)}, u32[]{:S(2)}, u32[]{:S(2)}) %collective-permute-start.5) | collective-permute-done | bytes 262176 | tf_op jit(solution)/shard_map/ppermute | solution.py:222
  162.5 4.4 %collective-permute-done.9.refs_5_ = bf16[1024,128]{1,0:T(8,128)(2,1)S(1)} collective-permute-done((bf16[1024,128]{1,0:T(8,128)(2,1)}, bf16[1024,128]{1,0:T(8,128)(2,1)S(1)}, u32[]{:S(2)}, u32[]{:S(2)}) %collective-permute-start.9) | collective-permute-done | bytes 262176 | tf_op jit(solution)/shard_map/ppermute | solution.py:231
  169.8 9.2 %shard_map.119.x_ref = bf16[128,512]{1,0:T(8,128)(2,1)} custom-call(s32[64]{0:T(128)} %span_ref.1, s32[2]{0:T(128)} %pad_add_fusion.1.where_ref, bf16[128,512]{1,0:T(8,128)(2,1)} %q_ref.1, bf16[1024,128]{1,0:T(8,128)(2,1)} %get-tuple-element.19.refs_0_, bf16[1024,128]{1,0:T(8,128)(2,1)} %copy-done.21, bf16[1024,128]{1,0:T(8,128)(2,1)} %copy-done.22, ...), custom_call_target="tpu_custom_call" | custom-call | flops 1073741824 | bytes 2359296 | tf_op jit(solution)/shard_map/pallas_call | solution.py:94
  180.6 4.0 %shard_map.120 = (bf16[16,2048]{1,0:T(8,128)(2,1)}, bf16[16,2048]{1,0:T(8,128)(2,1)}, bf16[16,2048]{1,0:T(8,128)(2,1)}, bf16[16,2048]{1,0:T(8,128)(2,1)}, bf16[1...) custom-call(s32[2]{0:T(128)} %pad_add_fusion.ctx_ref, ...), custom_call_target="tpu_custom_call" | custom-call | flops 268435456 | bytes 2752512 | tf_op jit(solution)/shard_map/pallas_call | solution.py:164
  184.6 2.9 collective-permute-start.21
  191.4 2.8 collective-permute-start.17
  197.6 2.6 collective-permute-done.16
  207.7 3.1 collective-permute-start.27
  210.8 2.4 collective-permute-start.28
  214.4 2.8 collective-permute-done.28.refs_7_
  217.9 2.6 shard_map.121
  220.6 12.9 %all-to-all-start = ((bf16[32,16,1024]{2,1,0:T(8,128)(2,1)}), bf16[32,16,1024]{2,1,0:T(8,128)(2,1)S(1)}, u32[]{:S(2)}, u32[]{:S(2)}) async-start(bf16[32,16,1024]{2,1,0:T(8,128)(2,1)} %shard_map.121), calls=%async_computation | async-start | bytes 2097152 | tf_op jit(solution)/shard_map/all_to_all | solution.py:339
  233.5 3.1 constant_dynamic-slice_fusion.1
  236.9 27.1 %all-to-all-done = bf16[32,16,1024]{2,1,0:T(8,128)(2,1)S(1)} async-done(((bf16[32,16,1024]{2,1,0:T(8,128)(2,1)}), bf16[32,16,1024]{2,1,0:T(8,128)(2,1)S(1)}, u32[]{:S(2)}, u32[]{:S(2)}) %all-to-all-start) | async-done | bytes 1048608 | tf_op jit(solution)/shard_map/all_to_all | solution.py:339
  266.6 2.4 fusion.26
  275.2 5.3 %all-to-all-start.2 = ((bf16[256,2,1024]{2,1,0:T(2,128)(2,1)}), bf16[256,2,1024]{2,1,0:T(2,128)(2,1)S(1)}, u32[]{:S(2)}, u32[]{:S(2)}) async-start(bf16[256,2,1024]{2,1,0:T(2,128)(2,1)} %reshape.91), calls=%async_computation.2 | async-start | bytes 2097152 | tf_op jit(solution)/shard_map/all_to_all | solution.py:364
  280.7 30.6 %all-to-all-done.2 = bf16[256,2,1024]{2,1,0:T(2,128)(2,1)S(1)} async-done(((bf16[256,2,1024]{2,1,0:T(2,128)(2,1)}), bf16[256,2,1024]{2,1,0:T(2,128)(2,1)S(1)}, u32[]{:S(2)}, u32[]{:S(2)}) %all-to-all-start.2) | async-done | bytes 1048608 | tf_op jit(solution)/shard_map/all_to_all | solution.py:364
  (148 shorter events, 45.3 us)
Async XLA Ops:
  4.0 216.6 %all-to-all-start.1 = ((bf16[16,64,2304]{2,1,0:T(8,128)(2,1)}), bf16[16,64,2304]{2,1,0:T(8,128)(2,1)}, u32[]{:S(2)}, u32[]{:S(2)}) async-start(bf16[16,64,2304]{2,1,0:T(8,128)(2,1)} %pad_maximum_fusion), calls=%async_computation.1 | async-start | bytes 9437184 | tf_op jit(solution)/shard_map/all_to_all | solution.py:282
  17.6 126.2 %collective-permute-start.1 = (bf16[768,128]{1,0:T(8,128)(2,1)S(1)}, bf16[768,128]{1,0:T(8,128)(2,1)S(1)}, u32[]{:S(2)}, u32[]{:S(2)}) collective-permute-start(bf16[768,128]{1,0:T(8,128)(2,1)S(1)} %pad_maximum_fusion.2), channel_id=1, source_target_pairs={{16,0},{120,8},{32,16},{8,24},{48,32},{24,40},{64,48},{40,56},{80,... | collective-permute-start | bytes 589832 | tf_op jit(solution)/shard_map/ppermute | solution.py:280
  17.9 125.9 %collective-permute-start.2 = (bf16[768,128]{1,0:T(8,128)(2,1)S(1)}, bf16[768,128]{1,0:T(8,128)(2,1)S(1)}, u32[]{:S(2)}, u32[]{:S(2)}) collective-permute-start(bf16[768,128]{1,0:T(8,128)(2,1)S(1)} %pad_maximum_fusion.2), channel_id=1, source_target_pairs={{32,0},{104,8},{48,16},{120,24},{64,32},{8,40},{80,48},{24,56},{96... | collective-permute-start | bytes 589832 | tf_op jit(solution)/shard_map/ppermute | solution.py:280
  21.8 122.0 %collective-permute-start.3 = (bf16[768,128]{1,0:T(8,128)(2,1)S(1)}, bf16[768,128]{1,0:T(8,128)(2,1)S(1)}, u32[]{:S(2)}, u32[]{:S(2)}) collective-permute-start(bf16[768,128]{1,0:T(8,128)(2,1)S(1)} %pad_maximum_fusion.2), channel_id=1, source_target_pairs={{48,0},{88,8},{64,16},{104,24},{80,32},{120,40},{96,48},{8,56},{11... | collective-permute-start | bytes 589832 | tf_op jit(solution)/shard_map/ppermute | solution.py:280
  24.2 119.6 %collective-permute-start.4 = (bf16[384,128]{1,0:T(8,128)(2,1)S(1)}, bf16[384,128]{1,0:T(8,128)(2,1)S(1)}, u32[]{:S(2)}, u32[]{:S(2)}) collective-permute-start(bf16[384,128]{1,0:T(8,128)(2,1)S(1)} %pad_maximum_fusion.3.refs_0_), channel_id=1, source_target_pairs={{64,0},{80,16},{96,32},{112,48},{0,64},{16,80},{32,96},{48,112},{6... | collective-permute-start | bytes 294920 | tf_op jit(solution)/shard_map/ppermute | solution.py:281
  147.5 14.0 %collective-permute-start.12 = (bf16[512,512]{1,0:T(8,128)(2,1)}, bf16[512,512]{1,0:T(8,128)(2,1)S(1)}, u32[]{:S(2)}, u32[]{:S(2)}) collective-permute-start(bf16[512,512]{1,0:T(8,128)(2,1)} %get-tuple-element.20.refs_0_), channel_id=1, source_target_pairs={{0,128},{128,0},{1,129},{129,1},{2,130},{130,2},{3,131},{131,3},{4... | collective-permute-start | bytes 1572872 | tf_op jit(solution)/shard_map/ppermute | solution.py:222
  149.4 12.1 %collective-permute-start.5 = (bf16[1024,128]{1,0:T(8,128)(2,1)}, bf16[1024,128]{1,0:T(8,128)(2,1)S(1)}, u32[]{:S(2)}, u32[]{:S(2)}) collective-permute-start(bf16[1024,128]{1,0:T(8,128)(2,1)} %get-tuple-element.19.refs_0_), channel_id=1, source_target_pairs={{0,128},{128,0},{1,129},{129,1},{2,130},{130,2},{3,131},{131,3},{4... | collective-permute-start | bytes 786440 | tf_op jit(solution)/shard_map/ppermute | solution.py:222
  151.0 11.0 %collective-permute-start.6 = (bf16[1024,128]{1,0:T(8,128)(2,1)}, bf16[1024,128]{1,0:T(8,128)(2,1)S(1)}, u32[]{:S(2)}, u32[]{:S(2)}) collective-permute-start(bf16[1024,128]{1,0:T(8,128)(2,1)} %get-tuple-element.19.refs_0_), channel_id=1, source_target_pairs={{0,8},{8,0},{1,9},{9,1},{2,10},{10,2},{3,11},{11,3},{4,12},{12,4},... | collective-permute-start | bytes 786440 | tf_op jit(solution)/shard_map/ppermute | solution.py:29
  151.0 11.1 %collective-permute-start.8 = (bf16[1024,128]{1,0:T(8,128)(2,1)}, bf16[1024,128]{1,0:T(8,128)(2,1)S(1)}, u32[]{:S(2)}, u32[]{:S(2)}) collective-permute-start(bf16[1024,128]{1,0:T(8,128)(2,1)} %get-tuple-element.19.refs_0_), channel_id=1, source_target_pairs={{0,1},{1,0},{2,3},{3,2},{4,5},{5,4},{6,7},{7,6},{8,9},{9,8},{10,11... | collective-permute-start | bytes 786440 | tf_op jit(solution)/shard_map/ppermute | solution.py:226
  152.5 14.4 %collective-permute-start.9 = (bf16[1024,128]{1,0:T(8,128)(2,1)}, bf16[1024,128]{1,0:T(8,128)(2,1)S(1)}, u32[]{:S(2)}, u32[]{:S(2)}) collective-permute-start(bf16[1024,128]{1,0:T(8,128)(2,1)} %get-tuple-element.19.refs_0_), channel_id=1, source_target_pairs={{0,129},{1,128},{2,131},{3,130},{4,133},{5,132},{6,135},{7,134},{1... | collective-permute-start | bytes 786440 | tf_op jit(solution)/shard_map/ppermute | solution.py:231
  161.5 17.5 %collective-permute-start.13 = (bf16[512,512]{1,0:T(8,128)(2,1)}, bf16[512,512]{1,0:T(8,128)(2,1)S(1)}, u32[]{:S(2)}, u32[]{:S(2)}) collective-permute-start(bf16[512,512]{1,0:T(8,128)(2,1)} %get-tuple-element.20.refs_0_), channel_id=1, source_target_pairs={{0,8},{8,0},{1,9},{9,1},{2,10},{10,2},{3,11},{11,3},{4,12},{12,4},... | collective-permute-start | bytes 1572872 | tf_op jit(solution)/shard_map/ppermute | solution.py:29
  161.5 17.5 %collective-permute-start.14 = (bf16[512,512]{1,0:T(8,128)(2,1)S(1)}, bf16[512,512]{1,0:T(8,128)(2,1)S(1)}, u32[]{:S(2)}, u32[]{:S(2)}) collective-permute-start(bf16[512,512]{1,0:T(8,128)(2,1)S(1)} %collective-permute-done.12.refs_1_), channel_id=1, source_target_pairs={{0,8},{8,0},{1,9},{9,1},{2,10},{10,2},{3,11},{11,3},{4,12},{12,4},... | collective-permute-start | bytes 1572872 | tf_op jit(solution)/shard_map/ppermute | solution.py:29
  184.6 9.6 %collective-permute-start.21 = (bf16[16,2048]{1,0:T(8,128)(2,1)}, bf16[16,2048]{1,0:T(8,128)(2,1)S(1)}, u32[]{:S(2)}, u32[]{:S(2)}) collective-permute-start(bf16[16,2048]{1,0:T(8,128)(2,1)} %get-tuple-element.28), channel_id=1, source_target_pairs={{0,7},{1,6},{2,5},{3,4},{4,3},{5,2},{6,1},{7,0},{8,15},{9,14},{10,... | collective-permute-start | bytes 196616 | tf_op jit(solution)/shard_map/ppermute | solution.py:303
  187.5 7.9 %collective-permute-start.20 = (bf16[16,2048]{1,0:T(8,128)(2,1)}, bf16[16,2048]{1,0:T(8,128)(2,1)S(1)}, u32[]{:S(2)}, u32[]{:S(2)}) collective-permute-start(bf16[16,2048]{1,0:T(8,128)(2,1)} %get-tuple-element.27), channel_id=1, source_target_pairs={{0,6},{1,7},{2,4},{3,5},{4,2},{5,3},{6,0},{7,1},{8,14},{9,15},{10,... | collective-permute-start | bytes 196616 | tf_op jit(solution)/shard_map/ppermute | solution.py:303
  189.4 8.2 %collective-permute-start.19 = (bf16[16,2048]{1,0:T(8,128)(2,1)}, bf16[16,2048]{1,0:T(8,128)(2,1)S(1)}, u32[]{:S(2)}, u32[]{:S(2)}) collective-permute-start(bf16[16,2048]{1,0:T(8,128)(2,1)} %get-tuple-element.26), channel_id=1, source_target_pairs={{0,5},{1,4},{2,7},{3,6},{4,1},{5,0},{6,3},{7,2},{8,13},{9,12},{10,... | collective-permute-start | bytes 196616 | tf_op jit(solution)/shard_map/ppermute | solution.py:303
  190.1 7.5 %collective-permute-start.18 = (bf16[16,2048]{1,0:T(8,128)(2,1)}, bf16[16,2048]{1,0:T(8,128)(2,1)S(1)}, u32[]{:S(2)}, u32[]{:S(2)}) collective-permute-start(bf16[16,2048]{1,0:T(8,128)(2,1)} %get-tuple-element.25), channel_id=1, source_target_pairs={{0,4},{1,5},{2,6},{3,7},{4,0},{5,1},{6,2},{7,3},{8,12},{9,13},{10,... | collective-permute-start | bytes 196616 | tf_op jit(solution)/shard_map/ppermute | solution.py:303
  202.7 8.1 %collective-permute-start.23 = (bf16[16,2176]{1,0:T(8,128)(2,1)S(1)}, bf16[16,2176]{1,0:T(8,128)(2,1)S(1)}, u32[]{:S(2)}, u32[]{:S(2)}) collective-permute-start(bf16[16,2176]{1,0:T(8,128)(2,1)S(1)} %fusion.12.refs_0_), channel_id=1, source_target_pairs={{0,2},{1,3},{2,0},{3,1},{4,6},{5,7},{6,4},{7,5},{8,10},{9,11},{10,... | collective-permute-start | bytes 208904 | tf_op jit(solution)/shard_map/ppermute | solution.py:336
  204.9 8.4 %collective-permute-start.24 = (bf16[16,2176]{1,0:T(8,128)(2,1)S(1)}, bf16[16,2176]{1,0:T(8,128)(2,1)S(1)}, u32[]{:S(2)}, u32[]{:S(2)}) collective-permute-start(bf16[16,2176]{1,0:T(8,128)(2,1)S(1)} %fusion.12.refs_0_), channel_id=1, source_target_pairs={{0,3},{1,2},{2,1},{3,0},{4,7},{5,6},{6,5},{7,4},{8,11},{9,10},{10,... | collective-permute-start | bytes 208904 | tf_op jit(solution)/shard_map/ppermute | solution.py:336
  206.1 7.1 %collective-permute-start.25 = (bf16[16,2176]{1,0:T(8,128)(2,1)S(1)}, bf16[16,2176]{1,0:T(8,128)(2,1)S(1)}, u32[]{:S(2)}, u32[]{:S(2)}) collective-permute-start(bf16[16,2176]{1,0:T(8,128)(2,1)S(1)} %fusion.12.refs_0_), channel_id=1, source_target_pairs={{0,4},{1,5},{2,6},{3,7},{4,0},{5,1},{6,2},{7,3},{8,12},{9,13},{10,... | collective-permute-start | bytes 208904 | tf_op jit(solution)/shard_map/ppermute | solution.py:336
  207.7 6.7 %collective-permute-start.27 = (bf16[16,2176]{1,0:T(8,128)(2,1)S(1)}, bf16[16,2176]{1,0:T(8,128)(2,1)S(1)}, u32[]{:S(2)}, u32[]{:S(2)}) collective-permute-start(bf16[16,2176]{1,0:T(8,128)(2,1)S(1)} %fusion.12.refs_0_), channel_id=1, source_target_pairs={{0,6},{1,7},{2,4},{3,5},{4,2},{5,3},{6,0},{7,1},{8,14},{9,15},{10,... | collective-permute-start | bytes 208904 | tf_op jit(solution)/shard_map/ppermute | solution.py:336
  210.8 6.4 %collective-permute-start.28 = (bf16[16,2176]{1,0:T(8,128)(2,1)S(1)}, bf16[16,2176]{1,0:T(8,128)(2,1)S(1)}, u32[]{:S(2)}, u32[]{:S(2)}) collective-permute-start(bf16[16,2176]{1,0:T(8,128)(2,1)S(1)} %fusion.12.refs_0_), channel_id=1, source_target_pairs={{0,7},{1,6},{2,5},{3,4},{4,3},{5,2},{6,1},{7,0},{8,15},{9,14},{10,... | collective-permute-start | bytes 208904 | tf_op jit(solution)/shard_map/ppermute | solution.py:336
  220.6 43.4 %all-to-all-start = ((bf16[32,16,1024]{2,1,0:T(8,128)(2,1)}), bf16[32,16,1024]{2,1,0:T(8,128)(2,1)S(1)}, u32[]{:S(2)}, u32[]{:S(2)}) async-start(bf16[32,16,1024]{2,1,0:T(8,128)(2,1)} %shard_map.121), calls=%async_computation | async-start | bytes 2097152 | tf_op jit(solution)/shard_map/all_to_all | solution.py:339
  236.7 29.9 %collective-permute-start.30 = (bf16[1024,768]{1,0:T(8,128)(2,1)S(1)}, bf16[1024,768]{1,0:T(8,128)(2,1)}, u32[]{:S(2)}, u32[]{:S(2)}) collective-permute-start(bf16[1024,768]{1,0:T(8,128)(2,1)S(1)} %pad_maximum_fusion.1), channel_id=1, source_target_pairs={{0,8},{8,0},{1,9},{9,1},{2,10},{10,2},{3,11},{11,3},{4,12},{12,4},... | collective-permute-start | bytes 4718600 | tf_op jit(solution)/shard_map/ppermute | solution.py:29
  275.2 36.1 %all-to-all-start.2 = ((bf16[256,2,1024]{2,1,0:T(2,128)(2,1)}), bf16[256,2,1024]{2,1,0:T(2,128)(2,1)S(1)}, u32[]{:S(2)}, u32[]{:S(2)}) async-start(bf16[256,2,1024]{2,1,0:T(2,128)(2,1)} %reshape.91), calls=%async_computation.2 | async-start | bytes 2097152 | tf_op jit(solution)/shard_map/all_to_all | solution.py:364
  (39 other events, 488.4 us)

commit v9 on v8

--- a/solution.py
+++ b/solution.py
@@ -183,9 +183,9 @@
 def place_kernel(exp_ref, *refs):
     blocks, (o_ref, row_ref) = refs[:8], refs[8:]
     for d, block in enumerate(blocks):
-        row_ref[d * 16 : (d + 1) * 16, :] = block[...].astype(jnp.float32)
+        row_ref[d * 16 : (d + 1) * 16, :] = block[...]
     exp = exp_ref[0]
-    codes = jnp.transpose(row_ref[:, D:])
+    codes = jnp.transpose(row_ref[:, D:].astype(jnp.float32))
     slot = lax.broadcasted_iota(jnp.int32, (256, 128), 0)
     lane = lax.broadcasted_iota(jnp.int32, (256, 128), 1)
     wanted = ((exp * OWN + slot // 16) * CAP + slot % CAP).astype(jnp.float32)
@@ -195,7 +195,7 @@
     hit = jnp.where((slot % 16) // CAP == jnp.bitwise_xor(lane // 16, exp), hit, 0.0)
     hit = hit.astype(jnp.bfloat16)
     for plane in range(2):
-        x = row_ref[:, plane * HALF : (plane + 1) * HALF].astype(jnp.bfloat16)
+        x = row_ref[:, plane * HALF : (plane + 1) * HALF]
         out = jnp.dot(hit, x, preferred_element_type=jnp.float32).astype(o_ref.dtype)
         for k in range(OWN):
             o_ref[2 * k + plane, :, :] = out[k * 16 : (k + 1) * 16, :]
@@ -210,7 +210,7 @@
             grid=(1,),
             in_specs=[pl.BlockSpec(b.shape, lambda i, *_: (0, 0)) for b in blocks],
             out_specs=pl.BlockSpec((2 * OWN, 16, HALF), lambda i, *_: (0, 0, 0)),
-            scratch_shapes=[pltpu.VMEM((128, D + 128), jnp.float32)],
+            scratch_shapes=[pltpu.VMEM((128, D + 128), jnp.bfloat16)],
         ),
         cost_estimate=pl.CostEstimate(
             flops=2 * 256 * 128 * D, bytes_accessed=1605632, transcendentals=0
@@ -287,7 +287,8 @@
     near = [piece, across_y(piece), across_x(piece), across_xy(piece)]
     wo_near = [wo_near, across_y(wo_near)]
     far = [swapped(p) for p in near]
-    wo_far = [swapped(w) for w in wo_near]
+    wo_far = [swapped(wo_near[0])]
+    wo_far.append(swapped(wo_near[1]))
 
     attended = attend(
         span_order,

time: 316 us -> 316 us (level)
  no operation moved by 1% of the time
where the time goes in v9:
time: 316 us; the launch traced here: 314 us
  waiting for transfers between devices  195 us (62%)
  starting transfers between devices  70.8 us (22%)
  Pallas kernels  18.1 us (6%)
  local copies, waits for them, and re-layouts  13 us (4%)
  matrix products  8.67 us (3%)
  other arithmetic  8.31 us (3%)
    ppermute x1, waiting for transfers between devices, shards(): lax.ppermute(packed, 'z', [((i + 4) % 8, i) for i in range(8)])  117 us
    all_to_all x1, waiting for transfers between devices, shards(): home = lax.all_to_all(out.reshape(256, CAP, HALF), ALL, 0, 0, tiled=True)  30.6 us
    all_to_all x1, waiting for transfers between devices, shards(): tokens = lax.all_to_all(outgoing, CTX, 0, 0, tiled=True).reshape(512, HALF)  27.1 us
    all_to_all x1, starting transfers between devices, shards(): tokens = lax.all_to_all(outgoing, CTX, 0, 0, tiled=True).reshape(512, HALF)  12.9 us
    ppermute x7, starting transfers between devices, shards(): lax.ppermute(payload, 'exp', [(e, e ^ d) for e in range(8)])  11.8 us
    ppermute x7, starting transfers between devices, shards(): got = lax.ppermute(mixed[d], 'exp', [(e, e ^ d) for e in range(8)])  11.7 us
    all_to_all x1, starting transfers between devices, shards(): lax.all_to_all(jnp.concatenate([w_gate, w_up, w_down], axis=2), CHIP, 0,...  11.3 us
    pallas_call x1, Pallas kernels, attend(): pl.pallas_call(attend_kernel, out_shape=jax.ShapeDtypeStruct((rows, width...  9.17 us
  transfers between devices with their start and end apart: 35, of which 12 were waited for; matrix products, arithmetic and copies ran while one was open for 4% of the time, Pallas kernels for 6%

profile of v9, /device:TPU:32, one launch (start us, length us, event | category | flops | bytes accessed | tf_op | source)
XLA Modules:
  0.0 314.4 jit_solution(3907378980457928560)
XLA Ops:
  0.0 4.0 %pad_maximum_fusion = bf16[16,64,2304]{2,1,0:T(8,128)(2,1)} fusion(bf16[16,64,768]{2,1,0:T(8,128)(2,1)} %param.23, bf16[16,64,768]{2,1,0:T(8,128)(2,1)} %param.22, bf16[16,64,768]{2,1,0:T(8,128)(2,1)} %param.21), kind=kLoop, calls=%fused_computation | loop fusion | flops 14155776 | bytes 9437184 | tf_op jit(solution)/shard_map/concatenate | solution.py:283
  4.0 11.3 %all-to-all-start.1 = ((bf16[16,64,2304]{2,1,0:T(8,128)(2,1)}), bf16[16,64,2304]{2,1,0:T(8,128)(2,1)}, u32[]{:S(2)}, u32[]{:S(2)}) async-start(bf16[16,64,2304]{2,1,0:T(8,128)(2,1)} %pad_maximum_fusion), calls=%async_computation.1 | async-start | bytes 9437184 | tf_op jit(solution)/shard_map/all_to_all | solution.py:282
  17.9 4.0 %collective-permute-start.2 = (bf16[768,128]{1,0:T(8,128)(2,1)S(1)}, bf16[768,128]{1,0:T(8,128)(2,1)S(1)}, u32[]{:S(2)}, u32[]{:S(2)}) collective-permute-start(bf16[768,128]{1,0:T(8,128)(2,1)S(1)} %pad_maximum_fusion.2), channel_id=1, source_target_pairs={{32,0},{104,8},{48,16},{120,24},{64,32},{8,40},{80,48},{24,56},{96... | collective-permute-start | bytes 589832 | tf_op jit(solution)/shard_map/ppermute | solution.py:280
  21.8 2.4 collective-permute-start.3
  24.2 2.7 collective-permute-start.4
  26.9 116.9 %collective-permute-done.4.refs_4_ = bf16[384,128]{1,0:T(8,128)(2,1)S(1)} collective-permute-done((bf16[384,128]{1,0:T(8,128)(2,1)S(1)}, bf16[384,128]{1,0:T(8,128)(2,1)S(1)}, u32[]{:S(2)}, u32[]{:S(2)}) %collective-permute-start.4) | collective-permute-done | bytes 98336 | tf_op jit(solution)/shard_map/ppermute | solution.py:281
  145.2 2.2 shard_map.118
  154.4 7.1 %collective-permute-done.5.refs_1_ = bf16[1024,128]{1,0:T(8,128)(2,1)S(1)} collective-permute-done((bf16[1024,128]{1,0:T(8,128)(2,1)}, bf16[1024,128]{1,0:T(8,128)(2,1)S(1)}, u32[]{:S(2)}, u32[]{:S(2)}) %collective-permute-start.5) | collective-permute-done | bytes 262176 | tf_op jit(solution)/shard_map/ppermute | solution.py:222
  162.5 4.4 %collective-permute-done.9.refs_5_ = bf16[1024,128]{1,0:T(8,128)(2,1)S(1)} collective-permute-done((bf16[1024,128]{1,0:T(8,128)(2,1)}, bf16[1024,128]{1,0:T(8,128)(2,1)S(1)}, u32[]{:S(2)}, u32[]{:S(2)}) %collective-permute-start.9) | collective-permute-done | bytes 262176 | tf_op jit(solution)/shard_map/ppermute | solution.py:231
  169.8 9.2 %shard_map.119.x_ref = bf16[128,512]{1,0:T(8,128)(2,1)} custom-call(s32[64]{0:T(128)} %span_ref.1, s32[2]{0:T(128)} %pad_add_fusion.1.where_ref, bf16[128,512]{1,0:T(8,128)(2,1)} %q_ref.1, bf16[1024,128]{1,0:T(8,128)(2,1)} %get-tuple-element.19.refs_0_, bf16[1024,128]{1,0:T(8,128)(2,1)} %copy-done.21, bf16[1024,128]{1,0:T(8,128)(2,1)} %copy-done.22, ...), custom_call_target="tpu_custom_call" | custom-call | flops 1073741824 | bytes 2359296 | tf_op jit(solution)/shard_map/pallas_call | solution.py:94
  180.6 4.0 %shard_map.120 = (bf16[16,2048]{1,0:T(8,128)(2,1)}, bf16[16,2048]{1,0:T(8,128)(2,1)}, bf16[16,2048]{1,0:T(8,128)(2,1)}, bf16[16,2048]{1,0:T(8,128)(2,1)}, bf16[1...) custom-call(s32[2]{0:T(128)} %pad_add_fusion.ctx_ref, ...), custom_call_target="tpu_custom_call" | custom-call | flops 268435456 | bytes 2752512 | tf_op jit(solution)/shard_map/pallas_call | solution.py:164
  184.6 2.9 collective-permute-start.21
  191.4 2.8 collective-permute-start.17
  197.6 2.6 collective-permute-done.16
  207.7 3.1 collective-permute-start.27
  210.8 2.4 collective-permute-start.28
  214.4 2.8 collective-permute-done.28.refs_7_
  217.9 2.7 shard_map.121
  220.6 12.9 %all-to-all-start = ((bf16[32,16,1024]{2,1,0:T(8,128)(2,1)}), bf16[32,16,1024]{2,1,0:T(8,128)(2,1)S(1)}, u32[]{:S(2)}, u32[]{:S(2)}) async-start(bf16[32,16,1024]{2,1,0:T(8,128)(2,1)} %shard_map.121), calls=%async_computation | async-start | bytes 2097152 | tf_op jit(solution)/shard_map/all_to_all | solution.py:340
  233.5 3.1 constant_dynamic-slice_fusion.1
  236.9 27.1 %all-to-all-done = bf16[32,16,1024]{2,1,0:T(8,128)(2,1)S(1)} async-done(((bf16[32,16,1024]{2,1,0:T(8,128)(2,1)}), bf16[32,16,1024]{2,1,0:T(8,128)(2,1)S(1)}, u32[]{:S(2)}, u32[]{:S(2)}) %all-to-all-start) | async-done | bytes 1048608 | tf_op jit(solution)/shard_map/all_to_all | solution.py:340
  266.6 2.4 fusion.26
  275.2 5.3 %all-to-all-start.2 = ((bf16[256,2,1024]{2,1,0:T(2,128)(2,1)}), bf16[256,2,1024]{2,1,0:T(2,128)(2,1)S(1)}, u32[]{:S(2)}, u32[]{:S(2)}) async-start(bf16[256,2,1024]{2,1,0:T(2,128)(2,1)} %reshape.91), calls=%async_computation.2 | async-start | bytes 2097152 | tf_op jit(solution)/shard_map/all_to_all | solution.py:365
  280.8 30.6 %all-to-all-done.2 = bf16[256,2,1024]{2,1,0:T(2,128)(2,1)S(1)} async-done(((bf16[256,2,1024]{2,1,0:T(2,128)(2,1)}), bf16[256,2,1024]{2,1,0:T(2,128)(2,1)S(1)}, u32[]{:S(2)}, u32[]{:S(2)}) %all-to-all-start.2) | async-done | bytes 1048608 | tf_op jit(solution)/shard_map/all_to_all | solution.py:365
  (148 shorter events, 45.3 us)
Async XLA Ops:
  4.0 216.6 %all-to-all-start.1 = ((bf16[16,64,2304]{2,1,0:T(8,128)(2,1)}), bf16[16,64,2304]{2,1,0:T(8,128)(2,1)}, u32[]{:S(2)}, u32[]{:S(2)}) async-start(bf16[16,64,2304]{2,1,0:T(8,128)(2,1)} %pad_maximum_fusion), calls=%async_computation.1 | async-start | bytes 9437184 | tf_op jit(solution)/shard_map/all_to_all | solution.py:282
  17.6 126.2 %collective-permute-start.1 = (bf16[768,128]{1,0:T(8,128)(2,1)S(1)}, bf16[768,128]{1,0:T(8,128)(2,1)S(1)}, u32[]{:S(2)}, u32[]{:S(2)}) collective-permute-start(bf16[768,128]{1,0:T(8,128)(2,1)S(1)} %pad_maximum_fusion.2), channel_id=1, source_target_pairs={{16,0},{120,8},{32,16},{8,24},{48,32},{24,40},{64,48},{40,56},{80,... | collective-permute-start | bytes 589832 | tf_op jit(solution)/shard_map/ppermute | solution.py:280
  17.9 125.9 %collective-permute-start.2 = (bf16[768,128]{1,0:T(8,128)(2,1)S(1)}, bf16[768,128]{1,0:T(8,128)(2,1)S(1)}, u32[]{:S(2)}, u32[]{:S(2)}) collective-permute-start(bf16[768,128]{1,0:T(8,128)(2,1)S(1)} %pad_maximum_fusion.2), channel_id=1, source_target_pairs={{32,0},{104,8},{48,16},{120,24},{64,32},{8,40},{80,48},{24,56},{96... | collective-permute-start | bytes 589832 | tf_op jit(solution)/shard_map/ppermute | solution.py:280
  21.8 122.0 %collective-permute-start.3 = (bf16[768,128]{1,0:T(8,128)(2,1)S(1)}, bf16[768,128]{1,0:T(8,128)(2,1)S(1)}, u32[]{:S(2)}, u32[]{:S(2)}) collective-permute-start(bf16[768,128]{1,0:T(8,128)(2,1)S(1)} %pad_maximum_fusion.2), channel_id=1, source_target_pairs={{48,0},{88,8},{64,16},{104,24},{80,32},{120,40},{96,48},{8,56},{11... | collective-permute-start | bytes 589832 | tf_op jit(solution)/shard_map/ppermute | solution.py:280
  24.2 119.6 %collective-permute-start.4 = (bf16[384,128]{1,0:T(8,128)(2,1)S(1)}, bf16[384,128]{1,0:T(8,128)(2,1)S(1)}, u32[]{:S(2)}, u32[]{:S(2)}) collective-permute-start(bf16[384,128]{1,0:T(8,128)(2,1)S(1)} %pad_maximum_fusion.3.refs_0_), channel_id=1, source_target_pairs={{64,0},{80,16},{96,32},{112,48},{0,64},{16,80},{32,96},{48,112},{6... | collective-permute-start | bytes 294920 | tf_op jit(solution)/shard_map/ppermute | solution.py:281
  147.5 14.0 %collective-permute-start.12 = (bf16[512,512]{1,0:T(8,128)(2,1)}, bf16[512,512]{1,0:T(8,128)(2,1)S(1)}, u32[]{:S(2)}, u32[]{:S(2)}) collective-permute-start(bf16[512,512]{1,0:T(8,128)(2,1)} %get-tuple-element.20.refs_0_), channel_id=1, source_target_pairs={{0,128},{128,0},{1,129},{129,1},{2,130},{130,2},{3,131},{131,3},{4... | collective-permute-start | bytes 1572872 | tf_op jit(solution)/shard_map/ppermute | solution.py:222
  149.4 12.1 %collective-permute-start.5 = (bf16[1024,128]{1,0:T(8,128)(2,1)}, bf16[1024,128]{1,0:T(8,128)(2,1)S(1)}, u32[]{:S(2)}, u32[]{:S(2)}) collective-permute-start(bf16[1024,128]{1,0:T(8,128)(2,1)} %get-tuple-element.19.refs_0_), channel_id=1, source_target_pairs={{0,128},{128,0},{1,129},{129,1},{2,130},{130,2},{3,131},{131,3},{4... | collective-permute-start | bytes 786440 | tf_op jit(solution)/shard_map/ppermute | solution.py:222
  151.0 11.0 %collective-permute-start.6 = (bf16[1024,128]{1,0:T(8,128)(2,1)}, bf16[1024,128]{1,0:T(8,128)(2,1)S(1)}, u32[]{:S(2)}, u32[]{:S(2)}) collective-permute-start(bf16[1024,128]{1,0:T(8,128)(2,1)} %get-tuple-element.19.refs_0_), channel_id=1, source_target_pairs={{0,8},{8,0},{1,9},{9,1},{2,10},{10,2},{3,11},{11,3},{4,12},{12,4},... | collective-permute-start | bytes 786440 | tf_op jit(solution)/shard_map/ppermute | solution.py:29
  151.0 11.1 %collective-permute-start.8 = (bf16[1024,128]{1,0:T(8,128)(2,1)}, bf16[1024,128]{1,0:T(8,128)(2,1)S(1)}, u32[]{:S(2)}, u32[]{:S(2)}) collective-permute-start(bf16[1024,128]{1,0:T(8,128)(2,1)} %get-tuple-element.19.refs_0_), channel_id=1, source_target_pairs={{0,1},{1,0},{2,3},{3,2},{4,5},{5,4},{6,7},{7,6},{8,9},{9,8},{10,11... | collective-permute-start | bytes 786440 | tf_op jit(solution)/shard_map/ppermute | solution.py:226
  152.5 14.4 %collective-permute-start.9 = (bf16[1024,128]{1,0:T(8,128)(2,1)}, bf16[1024,128]{1,0:T(8,128)(2,1)S(1)}, u32[]{:S(2)}, u32[]{:S(2)}) collective-permute-start(bf16[1024,128]{1,0:T(8,128)(2,1)} %get-tuple-element.19.refs_0_), channel_id=1, source_target_pairs={{0,129},{1,128},{2,131},{3,130},{4,133},{5,132},{6,135},{7,134},{1... | collective-permute-start | bytes 786440 | tf_op jit(solution)/shard_map/ppermute | solution.py:231
  161.5 17.5 %collective-permute-start.13 = (bf16[512,512]{1,0:T(8,128)(2,1)}, bf16[512,512]{1,0:T(8,128)(2,1)S(1)}, u32[]{:S(2)}, u32[]{:S(2)}) collective-permute-start(bf16[512,512]{1,0:T(8,128)(2,1)} %get-tuple-element.20.refs_0_), channel_id=1, source_target_pairs={{0,8},{8,0},{1,9},{9,1},{2,10},{10,2},{3,11},{11,3},{4,12},{12,4},... | collective-permute-start | bytes 1572872 | tf_op jit(solution)/shard_map/ppermute | solution.py:29
  161.5 17.5 %collective-permute-start.14 = (bf16[512,512]{1,0:T(8,128)(2,1)S(1)}, bf16[512,512]{1,0:T(8,128)(2,1)S(1)}, u32[]{:S(2)}, u32[]{:S(2)}) collective-permute-start(bf16[512,512]{1,0:T(8,128)(2,1)S(1)} %collective-permute-done.12.refs_1_), channel_id=1, source_target_pairs={{0,8},{8,0},{1,9},{9,1},{2,10},{10,2},{3,11},{11,3},{4,12},{12,4},... | collective-permute-start | bytes 1572872 | tf_op jit(solution)/shard_map/ppermute | solution.py:29
  184.6 9.6 %collective-permute-start.21 = (bf16[16,2048]{1,0:T(8,128)(2,1)}, bf16[16,2048]{1,0:T(8,128)(2,1)S(1)}, u32[]{:S(2)}, u32[]{:S(2)}) collective-permute-start(bf16[16,2048]{1,0:T(8,128)(2,1)} %get-tuple-element.28), channel_id=1, source_target_pairs={{0,7},{1,6},{2,5},{3,4},{4,3},{5,2},{6,1},{7,0},{8,15},{9,14},{10,... | collective-permute-start | bytes 196616 | tf_op jit(solution)/shard_map/ppermute | solution.py:304
  187.5 7.9 %collective-permute-start.20 = (bf16[16,2048]{1,0:T(8,128)(2,1)}, bf16[16,2048]{1,0:T(8,128)(2,1)S(1)}, u32[]{:S(2)}, u32[]{:S(2)}) collective-permute-start(bf16[16,2048]{1,0:T(8,128)(2,1)} %get-tuple-element.27), channel_id=1, source_target_pairs={{0,6},{1,7},{2,4},{3,5},{4,2},{5,3},{6,0},{7,1},{8,14},{9,15},{10,... | collective-permute-start | bytes 196616 | tf_op jit(solution)/shard_map/ppermute | solution.py:304
  189.4 8.2 %collective-permute-start.19 = (bf16[16,2048]{1,0:T(8,128)(2,1)}, bf16[16,2048]{1,0:T(8,128)(2,1)S(1)}, u32[]{:S(2)}, u32[]{:S(2)}) collective-permute-start(bf16[16,2048]{1,0:T(8,128)(2,1)} %get-tuple-element.26), channel_id=1, source_target_pairs={{0,5},{1,4},{2,7},{3,6},{4,1},{5,0},{6,3},{7,2},{8,13},{9,12},{10,... | collective-permute-start | bytes 196616 | tf_op jit(solution)/shard_map/ppermute | solution.py:304
  190.1 7.5 %collective-permute-start.18 = (bf16[16,2048]{1,0:T(8,128)(2,1)}, bf16[16,2048]{1,0:T(8,128)(2,1)S(1)}, u32[]{:S(2)}, u32[]{:S(2)}) collective-permute-start(bf16[16,2048]{1,0:T(8,128)(2,1)} %get-tuple-element.25), channel_id=1, source_target_pairs={{0,4},{1,5},{2,6},{3,7},{4,0},{5,1},{6,2},{7,3},{8,12},{9,13},{10,... | collective-permute-start | bytes 196616 | tf_op jit(solution)/shard_map/ppermute | solution.py:304
  202.7 8.1 %collective-permute-start.23 = (bf16[16,2176]{1,0:T(8,128)(2,1)S(1)}, bf16[16,2176]{1,0:T(8,128)(2,1)S(1)}, u32[]{:S(2)}, u32[]{:S(2)}) collective-permute-start(bf16[16,2176]{1,0:T(8,128)(2,1)S(1)} %fusion.12.refs_0_), channel_id=1, source_target_pairs={{0,2},{1,3},{2,0},{3,1},{4,6},{5,7},{6,4},{7,5},{8,10},{9,11},{10,... | collective-permute-start | bytes 208904 | tf_op jit(solution)/shard_map/ppermute | solution.py:337
  204.9 8.4 %collective-permute-start.24 = (bf16[16,2176]{1,0:T(8,128)(2,1)S(1)}, bf16[16,2176]{1,0:T(8,128)(2,1)S(1)}, u32[]{:S(2)}, u32[]{:S(2)}) collective-permute-start(bf16[16,2176]{1,0:T(8,128)(2,1)S(1)} %fusion.12.refs_0_), channel_id=1, source_target_pairs={{0,3},{1,2},{2,1},{3,0},{4,7},{5,6},{6,5},{7,4},{8,11},{9,10},{10,... | collective-permute-start | bytes 208904 | tf_op jit(solution)/shard_map/ppermute | solution.py:337
  206.1 7.1 %collective-permute-start.25 = (bf16[16,2176]{1,0:T(8,128)(2,1)S(1)}, bf16[16,2176]{1,0:T(8,128)(2,1)S(1)}, u32[]{:S(2)}, u32[]{:S(2)}) collective-permute-start(bf16[16,2176]{1,0:T(8,128)(2,1)S(1)} %fusion.12.refs_0_), channel_id=1, source_target_pairs={{0,4},{1,5},{2,6},{3,7},{4,0},{5,1},{6,2},{7,3},{8,12},{9,13},{10,... | collective-permute-start | bytes 208904 | tf_op jit(solution)/shard_map/ppermute | solution.py:337
  207.7 6.7 %collective-permute-start.27 = (bf16[16,2176]{1,0:T(8,128)(2,1)S(1)}, bf16[16,2176]{1,0:T(8,128)(2,1)S(1)}, u32[]{:S(2)}, u32[]{:S(2)}) collective-permute-start(bf16[16,2176]{1,0:T(8,128)(2,1)S(1)} %fusion.12.refs_0_), channel_id=1, source_target_pairs={{0,6},{1,7},{2,4},{3,5},{4,2},{5,3},{6,0},{7,1},{8,14},{9,15},{10,... | collective-permute-start | bytes 208904 | tf_op jit(solution)/shard_map/ppermute | solution.py:337
  210.8 6.4 %collective-permute-start.28 = (bf16[16,2176]{1,0:T(8,128)(2,1)S(1)}, bf16[16,2176]{1,0:T(8,128)(2,1)S(1)}, u32[]{:S(2)}, u32[]{:S(2)}) collective-permute-start(bf16[16,2176]{1,0:T(8,128)(2,1)S(1)} %fusion.12.refs_0_), channel_id=1, source_target_pairs={{0,7},{1,6},{2,5},{3,4},{4,3},{5,2},{6,1},{7,0},{8,15},{9,14},{10,... | collective-permute-start | bytes 208904 | tf_op jit(solution)/shard_map/ppermute | solution.py:337
  220.6 43.4 %all-to-all-start = ((bf16[32,16,1024]{2,1,0:T(8,128)(2,1)}), bf16[32,16,1024]{2,1,0:T(8,128)(2,1)S(1)}, u32[]{:S(2)}, u32[]{:S(2)}) async-start(bf16[32,16,1024]{2,1,0:T(8,128)(2,1)} %shard_map.121), calls=%async_computation | async-start | bytes 2097152 | tf_op jit(solution)/shard_map/all_to_all | solution.py:340
  236.7 29.9 %collective-permute-start.30 = (bf16[1024,768]{1,0:T(8,128)(2,1)S(1)}, bf16[1024,768]{1,0:T(8,128)(2,1)}, u32[]{:S(2)}, u32[]{:S(2)}) collective-permute-start(bf16[1024,768]{1,0:T(8,128)(2,1)S(1)} %pad_maximum_fusion.1), channel_id=1, source_target_pairs={{0,8},{8,0},{1,9},{9,1},{2,10},{10,2},{3,11},{11,3},{4,12},{12,4},... | collective-permute-start | bytes 4718600 | tf_op jit(solution)/shard_map/ppermute | solution.py:29
  275.2 36.1 %all-to-all-start.2 = ((bf16[256,2,1024]{2,1,0:T(2,128)(2,1)}), bf16[256,2,1024]{2,1,0:T(2,128)(2,1)S(1)}, u32[]{:S(2)}, u32[]{:S(2)}) async-start(bf16[256,2,1024]{2,1,0:T(2,128)(2,1)} %reshape.91), calls=%async_computation.2 | async-start | bytes 2097152 | tf_op jit(solution)/shard_map/all_to_all | solution.py:365
  (39 other events, 488.4 us)
